TPU v7x, 32 devices: a whole 2x2x4 slice. The times are simulated.
32 devices in a mesh: wide: 8 (over y, x, core), by: 4 (over z).
Axes of the slice: x: 2, y: 2, z: 4, core: 2. Of those that a mesh axis runs over, the one named last changes fastest.
Arguments:
- tiles: float32 [704, 512, 512], P(('wide', 'by')), may hold values from -6 to 6
- tile_rows: int32 [704], P(('wide', 'by')), may hold values from 0 to 7
- tile_cols: int32 [704], P(('wide', 'by')), may hold values from 0 to 63, as said below
- start_panel: float32 [32768, 64], P('wide'), may hold values from -6 to 6
Outputs:
- panel: float32 [32768, 64], P('wide')
- factor: float32 [64, 64], replicated
Inputs may be any that keep to these rules, and one draw needn't show every extreme that they name: `tile_cols`: within one device's 22 tiles, at most 3 have block columns in the block rows of one index of wide, and one index of wide takes exactly 3 of them.
All inputs are finite; a program needn't handle non-finite values.
Results may differ from a plain program's by a relative error of at most 0.0001.
Values sent between devices are 32-bit elements; how exact they have to be, the bound alone decides.
No kernel may reach another device: no remote copies, remote signals or barrier semaphores. Data moves between devices by JAX's collectives and lax.ppermute only.
A program may use at most 192 MiB of HBM per device.

v0:
```python
import jax
import jax.numpy as jnp
from jax import lax
from jax.sharding import PartitionSpec as P

ITERS = 2


def local(tiles, tile_rows, tile_cols, start_panel):
    wide_count = lax.axis_size("wide")
    my_wide = lax.axis_index("wide")
    tile_count = tiles.shape[0]
    block_size = tiles.shape[1]
    width = start_panel.shape[1]
    block_rows = start_panel.shape[0] // block_size
    capacity = max(2, tile_count // wide_count + 1)
    slot_count = wide_count * capacity
    highest = lax.Precision.HIGHEST
    peer_index = tile_cols // block_rows
    positions = jnp.arange(tile_count, dtype=jnp.int32)
    earlier = positions[:, None] > positions[None, :]
    same_peer = peer_index[:, None] == peer_index[None, :]
    rank_within = jnp.sum((earlier & same_peer).astype(jnp.int32), axis=1)
    slot_of = peer_index * capacity + rank_within
    slot_match = slot_of[:, None] == jnp.arange(slot_count, dtype=jnp.int32)[None, :]
    slot_table = slot_match.astype(jnp.float32)
    request = jnp.sum(jnp.where(slot_match, tile_cols[:, None] + 1, 0), axis=0) - 1
    incoming = lax.all_to_all(
        request.reshape(wide_count, capacity), "wide", split_axis=0, concat_axis=0, tiled=True
    ).reshape(slot_count)
    local_in = incoming - my_wide * block_rows
    block_iota = jnp.arange(block_rows, dtype=jnp.int32)
    serve_table = (local_in[:, None] == block_iota[None, :]).astype(jnp.float32)
    row_table = (tile_rows[:, None] == block_iota[None, :]).astype(jnp.float32)
    panel = start_panel
    factor = jnp.zeros((width, width), jnp.float32)
    for step in range(ITERS):
        flat_panel = panel.reshape(block_rows, block_size * width)
        outgoing = jnp.dot(serve_table, flat_panel, precision=highest)
        received = lax.all_to_all(outgoing, "wide", split_axis=0, concat_axis=0, tiled=True)
        col_panels = jnp.dot(slot_table, received, precision=highest).reshape(
            tile_count, block_size, width
        )
        row_panels = jnp.dot(row_table, flat_panel, precision=highest).reshape(
            tile_count, block_size, width
        )
        direct = jnp.einsum("tab,tbk->tak", tiles, col_panels, precision=highest)
        mirror = jnp.einsum("tba,tbk->tak", tiles, row_panels, precision=highest)
        partial_rows = jnp.dot(
            row_table.T, direct.reshape(tile_count, block_size * width), precision=highest
        )
        mirror_flat = mirror.reshape(tile_count, block_size * width)
        placed = jnp.dot(slot_table.T, mirror_flat, precision=highest)
        returned = lax.all_to_all(placed, "wide", split_axis=0, concat_axis=0, tiled=True)
        partial_rows = partial_rows + jnp.dot(serve_table.T, returned, precision=highest)
        partial_rows = partial_rows.reshape(block_rows * block_size, width)
        image = lax.psum(partial_rows, "by")
        gram = lax.psum(jnp.dot(image.T, image, precision=highest), "wide")
        factor = jnp.linalg.cholesky(gram)
        panel = jax.scipy.linalg.solve_triangular(factor, image.T, lower=True).T
    return (panel, factor)


def solution(mesh):
    placed = (P(("wide", "by"), None, None), P(("wide", "by")), P(("wide", "by")), P("wide", None))
    return jax.shard_map(
        local, mesh=mesh, in_specs=placed, out_specs=(P("wide", None), P()), check_vma=False
    )
```

profile of v0, /device:TPU:0, one launch (start us, length us, event | category | flops | bytes accessed | tf_op | source)
XLA Modules:
  0.0 638.6 jit_solution(3037137050593948503)
XLA Ops:
  8.8 5.2 all-to-all-start
  22.6 21.3 %fusion.13 = f32[22,512,64]{1,2,0:T(8,128)} fusion(f32[22,512,512]{2,1,0:T(8,128)} %param.7, f32[22,512,64]{1,0,2:T(8,128)S(1)} %fusion.60), kind=kOutput, calls=%fused_computation.15 | convolution fusion | flops 4429185024 | bytes 28835840 | tf_op jit(solution)/shard_map/tba,tbk->tak/dot_general | solution.py:48
  43.9 5.3 copy.59
  49.2 6.3 reshape.153
  75.3 41.6 %all-to-all-done.2 = f32[8,3,32768]{2,1,0:T(4,128)} async-done(((f32[8,3,32768]{2,1,0:T(4,128)}), f32[8,3,32768]{2,1,0:T(4,128)}, u32[]{:S(2)}, u32[]{:S(2)}) %all-to-all-start.2) | async-done | bytes 3145760 | tf_op jit(solution)/shard_map/all_to_all | solution.py:54
  125.3 45.2 %all-to-all-done.1 = f32[8,3,32768]{2,1,0:T(4,128)} async-done(((f32[8,3,32768]{2,1,0:T(4,128)}), f32[8,3,32768]{2,1,0:T(4,128)}, u32[]{:S(2)}, u32[]{:S(2)}) %all-to-all-start.1) | async-done | bytes 3145760 | tf_op jit(solution)/shard_map/all_to_all | solution.py:40
  170.5 5.5 all_to_all.30
  176.0 6.4 %dot_general.80 = f32[512,64,24]{1,0,2:T(8,128)} reshape(f32[32768,24]{0,1:T(8,128)} %bitcast.82) | data formatting | bytes 6291456 | tf_op jit(solution)/shard_map/dot_general | solution.py:41
  182.4 6.6 %copy.54 = f32[512,64,24]{0,2,1:T(8,128)} copy(f32[512,64,24]{1,0,2:T(8,128)} %dot_general.80) | data formatting | bytes 6291456 | tf_op jit(solution)/shard_map/dot_general | solution.py:41
  192.6 27.3 %fusion.10 = f32[22,512,64]{1,2,0:T(8,128)} fusion(f32[22,512,512]{2,1,0:T(8,128)} %param.7, f32[22,512,64]{1,0,2:T(8,128)S(1)} %fusion.37), kind=kOutput, calls=%fused_computation.14 | convolution fusion | flops 4429185024 | bytes 28835840 | tf_op jit(solution)/shard_map/tab,tbk->tak/dot_general | solution.py:47
  219.9 5.3 copy.56
  225.3 6.5 %reshape.143 = f32[22,32768]{1,0:T(8,128)} reshape(f32[22,512,64]{2,1,0:T(8,128)} %copy.56) | data formatting | bytes 5767168 | tf_op jit(solution)/shard_map/reshape | solution.py:50
  240.5 86.1 %all-reduce.3.cloned.1.call-done = f32[4096,64]{1,0:T(8,128)} async-done(((f32[4096,64]{1,0:T(8,128)}), f32[4096,64]{1,0:T(8,128)}) %all-reduce.3.cloned.1.call-update) | async-done | bytes 1048592 | tf_op jit(solution)/shard_map/psum | solution.py:57
  326.6 5.9 fusion.68
  332.5 24.3 %psum.29 = f32[64,64]{0,1:T(8,128)S(1)} all-reduce(f32[64,64]{0,1:T(8,128)S(1)} %fusion.68), channel_id=1, replica_groups=mesh['wide'=8,'by'=4] {'wide'}, use_global_device_ids=true, to_apply=%region_3.4 | all-reduce | flops 4096 | bytes 32768 | tf_op jit(solution)/shard_map/psum | solution.py:58
  356.9 5.8 cholesky.44
  386.9 19.4 %fusion.19 = f32[22,512,64]{1,2,0:T(8,128)S(1)} fusion(f32[22,512,512]{2,1,0:T(8,128)} %param.7, f32[22,512,64]{1,0,2:T(8,128)S(1)} %fusion.58), kind=kOutput, calls=%fused_computation.17 | convolution fusion | flops 4429185024 | bytes 28835840 | tf_op jit(solution)/shard_map/tba,tbk->tak/dot_general | solution.py:48
  420.5 11.6 %all-to-all-done.3 = f32[8,3,32768]{2,1,0:T(4,128)} async-done(((f32[8,3,32768]{2,1,0:T(4,128)}), f32[8,3,32768]{2,1,0:T(4,128)}, u32[]{:S(2)}, u32[]{:S(2)}) %all-to-all-start.3) | async-done | bytes 3145760 | tf_op jit(solution)/shard_map/all_to_all | solution.py:40
  445.4 5.0 copy.65
  452.1 25.6 %fusion.16 = f32[22,512,64]{1,2,0:T(8,128)S(1)} fusion(f32[22,512,512]{2,1,0:T(8,128)} %param.7, f32[22,512,64]{1,0,2:T(8,128)S(1)} %fusion.35), kind=kOutput, calls=%fused_computation.16 | convolution fusion | flops 4429185024 | bytes 28835840 | tf_op jit(solution)/shard_map/tab,tbk->tak/dot_general | solution.py:47
  498.9 86.2 %all-reduce.5.cloned.1.call-done = f32[4096,64]{1,0:T(8,128)} async-done(((f32[4096,64]{1,0:T(8,128)}), f32[4096,64]{1,0:T(8,128)}) %all-reduce.5.cloned.1.call-update) | async-done | bytes 1048592 | tf_op jit(solution)/shard_map/psum | solution.py:57
  585.1 5.9 fusion.69
  591.0 24.4 %psum.31 = f32[64,64]{0,1:T(8,128)S(1)} all-reduce(f32[64,64]{0,1:T(8,128)S(1)} %fusion.69), channel_id=1, replica_groups=mesh['wide'=8,'by'=4] {'wide'}, use_global_device_ids=true, to_apply=%region_7.10 | all-reduce | flops 4096 | bytes 32768 | tf_op jit(solution)/shard_map/psum | solution.py:58
  615.5 5.8 cholesky.55
  (77 shorter events, 135.4 us)
Async XLA Ops:
  8.8 54.4 %all-to-all-start = ((s32[8,1,3]{2,1,0:T(1,128)}), s32[8,1,3]{2,1,0:T(1,128)S(1)}, u32[]{:S(2)}, u32[]{:S(2)}) async-start(s32[8,1,3]{2,1,0:T(1,128)} %bitcast.1), calls=%async_computation | async-start | bytes 8192 | tf_op jit(solution)/shard_map/all_to_all | solution.py:28
  16.5 4.7 copy-start.2
  63.2 53.7 %all-to-all-start.2 = ((f32[8,3,32768]{2,1,0:T(4,128)}), f32[8,3,32768]{2,1,0:T(4,128)}, u32[]{:S(2)}, u32[]{:S(2)}) async-start(f32[8,3,32768]{2,1,0:T(4,128)} %copy.60), calls=%async_computation.2 | async-start | bytes 8388608 | tf_op jit(solution)/shard_map/all_to_all | solution.py:54
  116.9 53.7 %all-to-all-start.1 = ((f32[8,3,32768]{2,1,0:T(4,128)}), f32[8,3,32768]{2,1,0:T(4,128)}, u32[]{:S(2)}, u32[]{:S(2)}) async-start(f32[8,3,32768]{2,1,0:T(4,128)} %copy.53), calls=%async_computation.1 | async-start | bytes 8388608 | tf_op jit(solution)/shard_map/all_to_all | solution.py:40
  121.4 205.1 %all-reduce.3.cloned.1.call-start = ((), (), s32[]{:S(2)}) async-start(), calls=%async_computation.5 | async-start | bytes 4194304 | tf_op jit(solution)/shard_map/psum | solution.py:57
  326.6 42.5 %copy-start.1 = (f32[4096,64]{1,0:T(8,128)S(1)}, f32[4096,64]{1,0:T(8,128)}, u32[]{:S(2)}) copy-start(f32[4096,64]{1,0:T(8,128)} %all-reduce.3.cloned.1.call-done) | copy-start | bytes 3145732
  378.2 54.0 %all-to-all-start.3 = ((f32[8,3,32768]{2,1,0:T(4,128)}), f32[8,3,32768]{2,1,0:T(4,128)}, u32[]{:S(2)}, u32[]{:S(2)}) async-start(f32[8,3,32768]{2,1,0:T(4,128)} %copy.64), calls=%async_computation.3 | async-start | bytes 8388608 | tf_op jit(solution)/shard_map/all_to_all | solution.py:40
  432.2 56.1 %all-to-all-start.4 = ((f32[8,3,32768]{2,1,0:T(4,128)}), f32[8,3,32768]{2,1,0:T(4,128)}, u32[]{:S(2)}, u32[]{:S(2)}) async-start(f32[8,3,32768]{2,1,0:T(4,128)} %copy.71), calls=%async_computation.4 | async-start | bytes 8388608 | tf_op jit(solution)/shard_map/all_to_all | solution.py:54
  436.7 148.4 %all-reduce.5.cloned.1.call-start = ((), (), s32[]{:S(2)}) async-start(), calls=%async_computation.6 | async-start | bytes 4194304 | tf_op jit(solution)/shard_map/psum | solution.py:57
  585.1 43.1 %copy-start = (f32[4096,64]{1,0:T(8,128)S(1)}, f32[4096,64]{1,0:T(8,128)}, u32[]{:S(2)}) copy-start(f32[4096,64]{1,0:T(8,128)} %all-reduce.5.cloned.1.call-done) | copy-start | bytes 3145732
Sparse Core Ops, SparseCore 0:
  240.6 85.9 all-reduce.2
  499.0 86.0 all-reduce.4
where the time goes:
time: 648 us; the launch traced here: 639 us
  waiting for transfers between devices  271 us (42%)
  matrix products  138 us (21%)
  local copies, waits for them, and re-layouts  116 us (18%)
  blocking collectives  48.7 us (8%)
  other arithmetic  26.4 us (4%)
  starting transfers between devices  23.7 us (4%)
  between operations  14.6 us (2%)
    psum x2, waiting for transfers between devices, local(): image = lax.psum(partial_rows, 'by')  172 us
    all_to_all x2, waiting for transfers between devices, local(): lax.all_to_all(outgoing, 'wide', split_axis=0, concat_axis=0, tiled=True)  56.9 us
    dot_general x2, matrix products, local(): direct = jnp.einsum('tab,tbk->tak', tiles, col_panels, precision=highest)  52.9 us
    psum x2, blocking collectives, local(): gram = lax.psum(jnp.dot(image.T, image, precision=highest), 'wide')  48.7 us
    all_to_all x2, waiting for transfers between devices, local(): lax.all_to_all(placed, 'wide', split_axis=0, concat_axis=0, tiled=True)  41.6 us
    dot_general x2, matrix products, local(): mirror = jnp.einsum('tba,tbk->tak', tiles, row_panels, precision=highest)  40.7 us
    dot_general x4, local copies, waits for them, and re-layouts, local(): jnp.dot(slot_table, received, precision=highest)  22.9 us
    another operation x6, other arithmetic, local(): factor = jnp.linalg.cholesky(gram)  13 us
  transfers between devices with their start and end apart: 7, of which 5 were waited for; matrix products, arithmetic and copies ran while one was open for 22% of the time, Pallas kernels for 0%

commit v1 on v0

v1 whole, which is shorter than its diff:
```python
import functools

import jax
import jax.numpy as jnp
from jax import lax
from jax.experimental import pallas as pl
from jax.experimental.pallas import tpu as pltpu
from jax.sharding import PartitionSpec as P

ITERS = 2
HIGHEST = lax.Precision.HIGHEST


def split_pair(x):
    high = x.astype(jnp.bfloat16)
    low = (x - high.astype(jnp.float32)).astype(jnp.bfloat16)
    return high, low


def serve_kernel(wide, cap, bs, place_ref, wanted_ref, *refs):
    n_by = len(refs) - wide - 4
    quarters = refs[:n_by]
    panel_out = refs[n_by]
    outs = refs[n_by + 1 : n_by + 1 + wide]
    whole, in_sem, out_sem = refs[n_by + 1 + wide :]
    me, me_by = place_ref[0], place_ref[1]
    quarter = quarters[0].shape[1]
    loads = []
    for j in range(n_by):
        at = pl.multiple_of((me_by ^ j) * quarter, quarter)
        loads.append(
            pltpu.make_async_copy(quarters[j], whole.at[:, pl.ds(at, quarter)], in_sem.at[j])
        )
    for load in loads:
        load.start()
    for load in loads:
        load.wait()
    stores = [pltpu.make_async_copy(whole, panel_out, out_sem.at[wide * cap])]
    for k in range(wide):
        for c in range(cap):
            block = wanted_ref[(me ^ k) * cap + c]
            at = pl.multiple_of(block * bs, bs)
            stores.append(
                pltpu.make_async_copy(
                    whole.at[:, pl.ds(at, bs)],
                    outs[k].at[:, pl.ds(c * bs, bs)],
                    out_sem.at[k * cap + c],
                )
            )
    for store in stores:
        store.start()
    for store in stores:
        store.wait()


def serve(place, wanted, quarters, wide, cap, bs):
    n_by = len(quarters)
    width, quarter = quarters[0].shape
    rows = quarter * n_by
    shape = functools.partial(jax.ShapeDtypeStruct, dtype=jnp.float32)
    any_spec = pl.BlockSpec(memory_space=pl.ANY)
    outs = pl.pallas_call(
        functools.partial(serve_kernel, wide, cap, bs),
        grid_spec=pltpu.PrefetchScalarGridSpec(
            num_scalar_prefetch=2,
            grid=(),
            in_specs=[any_spec] * n_by,
            out_specs=[any_spec] * (wide + 1),
            scratch_shapes=[
                pltpu.VMEM((width, rows), jnp.float32),
                pltpu.SemaphoreType.DMA((n_by,)),
                pltpu.SemaphoreType.DMA((wide * cap + 1,)),
            ],
        ),
        out_shape=[shape((width, rows))] + [shape((width, cap * bs))] * wide,
        name="serve",
    )(place, wanted, *quarters)
    return outs[0], outs[1:]


def tile_products(stacked, tile, transposed):
    width = stacked.shape[0] // 2
    high, low = split_pair(tile)
    dims = (((1,), (1 if transposed else 0,)), ((), ()))
    both = lax.dot_general(stacked, high, dims, preferred_element_type=jnp.float32)
    rest = lax.dot_general(stacked[:width], low, dims, preferred_element_type=jnp.float32)
    return both[:width] + (both[width:] + rest)


def mirror_kernel(wide, cap, place_ref, tile_ref, row_ref, valid_ref, tile, panel, *refs):
    outs = refs[:wide]
    stacked, = refs[wide:]
    bs = tile.shape[1]
    width = panel.shape[0]
    step = pl.program_id(0)
    slot = (place_ref[0] ^ (step // cap)) * cap + step % cap

    @pl.when(step == 0)
    def _():
        for b in range(stacked.shape[0]):
            high, low = split_pair(panel[:, b * bs : (b + 1) * bs])
            stacked[b, :width] = high
            stacked[b, width:] = low

    def put(value):
        for k in range(wide):
            @pl.when(step // cap == k)
            def _():
                at = pl.multiple_of((step % cap) * bs, bs)
                outs[k][:, pl.ds(at, bs)] = value()

    @pl.when(valid_ref[slot] == 1)
    def _():
        result = tile_products(stacked[row_ref[slot]], tile[0], False)
        put(lambda: result)

    @pl.when(valid_ref[slot] == 0)
    def _():
        put(lambda: jnp.zeros((width, bs), jnp.float32))


def mirror(place, slot_tile, slot_row, slot_valid, tiles, panel, wide, cap):
    width, rows = panel.shape
    bs = tiles.shape[1]
    steps = wide * cap

    def tile_map(step, place, slot_tile, slot_row, slot_valid):
        return (slot_tile[(place[0] ^ (step // cap)) * cap + step % cap], 0, 0)

    whole = lambda step, *_: (0, 0)
    return pl.pallas_call(
        functools.partial(mirror_kernel, wide, cap),
        grid_spec=pltpu.PrefetchScalarGridSpec(
            num_scalar_prefetch=4,
            grid=(steps,),
            in_specs=[pl.BlockSpec((1, bs, bs), tile_map), pl.BlockSpec((width, rows), whole)],
            out_specs=[pl.BlockSpec((width, cap * bs), whole)] * wide,
            scratch_shapes=[pltpu.VMEM((rows // bs, 2 * width, bs), jnp.bfloat16)],
        ),
        out_shape=[jax.ShapeDtypeStruct((width, cap * bs), jnp.float32)] * wide,
        compiler_params=pltpu.CompilerParams(vmem_limit_bytes=48 << 20),
        name="mirror",
    )(place, slot_tile, slot_row, slot_valid, tiles, panel)


def direct_kernel(wide, cap, place_ref, tile_ref, row_ref, valid_ref, tile, *refs):
    received = refs[:wide]
    total, stacked = refs[wide:]
    bs = tile.shape[1]
    width = total.shape[0]
    step = pl.program_id(0)
    slot = (place_ref[0] ^ (step // cap)) * cap + step % cap

    @pl.when(step == 0)
    def _():
        total[...] = jnp.zeros_like(total)

    @pl.when(valid_ref[slot] == 1)
    def _():
        for k in range(wide):
            @pl.when(step // cap == k)
            def _():
                high, low = split_pair(received[k][...])
                stacked[:width] = high
                stacked[width:] = low

        at = pl.multiple_of(row_ref[slot] * bs, bs)
        total[:, pl.ds(at, bs)] += tile_products(stacked[...], tile[0], True)


def direct(place, slot_tile, slot_row, slot_valid, tiles, received, rows, wide, cap):
    bs = tiles.shape[1]
    width = received[0].shape[0]
    steps = wide * cap

    def tile_map(step, place, slot_tile, slot_row, slot_valid):
        return (slot_tile[(place[0] ^ (step // cap)) * cap + step % cap], 0, 0)

    def block_map(k, step, *_):
        return (0, jnp.clip(step - k * cap, 0, cap - 1))

    return pl.pallas_call(
        functools.partial(direct_kernel, wide, cap),
        grid_spec=pltpu.PrefetchScalarGridSpec(
            num_scalar_prefetch=4,
            grid=(steps,),
            in_specs=[pl.BlockSpec((1, bs, bs), tile_map)]
            + [pl.BlockSpec((width, bs), functools.partial(block_map, k)) for k in range(wide)],
            out_specs=pl.BlockSpec((width, rows), lambda step, *_: (0, 0)),
            scratch_shapes=[pltpu.VMEM((2 * width, bs), jnp.bfloat16)],
        ),
        out_shape=jax.ShapeDtypeStruct((width, rows), jnp.float32),
        compiler_params=pltpu.CompilerParams(vmem_limit_bytes=48 << 20),
        name="direct",
    )(place, slot_tile, slot_row, slot_valid, tiles, *received)


def gather_kernel(wide, cap, n_by, bs, place_ref, wanted_ref, flag_ref, start, *refs):
    returned = refs[:wide]
    outs = refs[wide : wide + n_by]
    total, = refs[wide + n_by :]
    step = pl.program_id(0)
    slot = (place_ref[0] ^ (step // cap)) * cap + step % cap

    @pl.when(step == 0)
    def _():
        total[...] = start[...]

    @pl.when(flag_ref[slot] == 1)
    def _():
        at = pl.multiple_of(wanted_ref[slot] * bs, bs)
        for k in range(wide):
            @pl.when(step // cap == k)
            def _():
                total[:, pl.ds(at, bs)] += returned[k][...]

    @pl.when(step == wide * cap - 1)
    def _():
        quarter = outs[0].shape[1]
        for j in range(n_by):
            at = pl.multiple_of((place_ref[1] ^ j) * quarter, quarter)
            outs[j][...] = total[:, pl.ds(at, quarter)]


def gather(place, wanted, flag, start, returned, wide, cap, n_by, bs):
    width, rows = start.shape
    quarter = rows // n_by

    def block_map(k, step, *_):
        return (0, jnp.clip(step - k * cap, 0, cap - 1))

    whole = lambda step, *_: (0, 0)
    return pl.pallas_call(
        functools.partial(gather_kernel, wide, cap, n_by, bs),
        grid_spec=pltpu.PrefetchScalarGridSpec(
            num_scalar_prefetch=3,
            grid=(wide * cap,),
            in_specs=[pl.BlockSpec((width, rows), whole)]
            + [pl.BlockSpec((width, bs), functools.partial(block_map, k)) for k in range(wide)],
            out_specs=[pl.BlockSpec((width, quarter), whole)] * n_by,
            scratch_shapes=[pltpu.VMEM((width, rows), jnp.float32)],
        ),
        out_shape=[jax.ShapeDtypeStruct((width, quarter), jnp.float32)] * n_by,
        compiler_params=pltpu.CompilerParams(vmem_limit_bytes=48 << 20),
        name="gather",
    )(place, wanted, flag, start, *returned)


def cholesky_kernel(gram, factor_t, inverse):
    n = gram.shape[0]
    row = lax.broadcasted_iota(jnp.int32, (n, 2 * n), 0)
    lane = lax.broadcasted_iota(jnp.int32, (n, 2 * n), 1)
    eye = (row[:, :n] == lane[:, :n]).astype(jnp.float32)
    work = jnp.concatenate([gram[...], eye], axis=1)
    for j in range(n):
        scale = 1.0 / jnp.sqrt(work[j : j + 1, j : j + 1])
        pivot_row = work[j : j + 1, :] * scale
        column = work[:, j : j + 1] * scale
        work = jnp.where(row == j, pivot_row, jnp.where(row > j, work - column * pivot_row, work))
    upper = row[:, :n] <= lane[:, :n]
    factor_t[...] = jnp.where(upper, work[:, :n], 0.0)
    inverse[...] = jnp.where(row[:, :n] >= lane[:, :n], work[:, n:], 0.0)


def cholesky(gram):
    n = gram.shape[0]
    shape = jax.ShapeDtypeStruct((n, n), jnp.float32)
    factor_t, inverse = pl.pallas_call(cholesky_kernel, out_shape=[shape, shape], name="cholesky")(gram)
    return factor_t.T, inverse


def final_kernel(place_ref, inverse, *refs):
    quarters, out = refs[:-1], refs[-1]
    quarter = quarters[0].shape[1]
    for j in range(len(quarters)):
        at = pl.multiple_of((place_ref[0] ^ j) * quarter, quarter)
        out[:, pl.ds(at, quarter)] = jnp.dot(
            inverse[...], quarters[j][...], precision=HIGHEST, preferred_element_type=jnp.float32
        )


def final(me_by, inverse, quarters):
    width, quarter = quarters[0].shape
    rows = quarter * len(quarters)
    vmem = pl.BlockSpec(memory_space=pltpu.VMEM)
    return pl.pallas_call(
        final_kernel,
        in_specs=[pl.BlockSpec(memory_space=pltpu.SMEM)] + [vmem] * (1 + len(quarters)),
        out_specs=vmem,
        out_shape=jax.ShapeDtypeStruct((width, rows), jnp.float32),
        compiler_params=pltpu.CompilerParams(vmem_limit_bytes=32 << 20),
        name="final",
    )(me_by, inverse, *quarters)


def local(tiles, tile_rows, tile_cols, start_panel):
    wide = lax.axis_size("wide")
    n_by = lax.axis_size("by")
    me = lax.axis_index("wide")
    me_by = lax.axis_index("by")
    tile_count, bs, _ = tiles.shape
    rows, width = start_panel.shape
    block_rows = rows // bs
    cap = max(2, tile_count // wide + 1)
    slots = wide * cap
    i32 = jnp.int32

    def swap(x, axis, size, k):
        return lax.ppermute(x, axis, [(i, i ^ k) for i in range(size)])

    def swap_wide(parts):
        return [parts[0]] + [swap(parts[k], "wide", wide, k) for k in range(1, wide)]

    peer = tile_cols // block_rows
    order = jnp.arange(tile_count, dtype=i32)
    earlier = (order[:, None] > order[None, :]) & (peer[:, None] == peer[None, :])
    rank = jnp.sum(earlier.astype(i32), axis=1)
    match = (peer * cap + rank)[:, None] == jnp.arange(slots, dtype=i32)[None, :]
    pick = lambda v: jnp.sum(jnp.where(match, v[:, None], 0), axis=0)
    slot_tile = pick(order)
    slot_row = pick(tile_rows)
    slot_valid = pick(jnp.ones_like(order))
    request = pick(tile_cols - peer * block_rows + 1)
    incoming = lax.all_to_all(
        request.reshape(wide, cap), "wide", split_axis=0, concat_axis=0, tiled=True
    ).reshape(slots)
    flag = (incoming > 0).astype(i32)
    wanted = jnp.maximum(incoming - 1, 0)
    place = jnp.stack([me, me_by]).astype(i32)

    def product(panel, served):
        received = swap_wide(served)
        mirrored = mirror(place, slot_tile, slot_row, slot_valid, tiles, panel, wide, cap)
        total = direct(place, slot_tile, slot_row, slot_valid, tiles, received, rows, wide, cap)
        returned = swap_wide(mirrored)
        chunks = gather(place, wanted, flag, total, returned, wide, cap, n_by, bs)
        quarter = chunks[0]
        for j in range(1, n_by):
            quarter = quarter + swap(chunks[j], "by", n_by, j)
        return quarter

    def spread(quarter):
        return [quarter] + [swap(quarter, "by", n_by, j) for j in range(1, n_by)]

    def gram_of(quarter):
        gram = jnp.dot(quarter, quarter.T, precision=HIGHEST)
        for axis, size in (("wide", wide), ("by", n_by)):
            k = 1
            while k < size:
                gram = gram + swap(gram, axis, size, k)
                k *= 2
        return gram

    panel_t = start_panel.T
    parts = [
        lax.dynamic_slice_in_dim(panel_t, (me_by ^ j) * (rows // n_by), rows // n_by, axis=1)
        for j in range(n_by)
    ]
    inverse = None
    for step in range(ITERS):
        panel, served = serve(place, wanted, parts, wide, cap, bs)
        quarter = product(panel, served)
        if inverse is not None:
            quarter = jnp.dot(inverse, quarter, precision=HIGHEST)
        parts = spread(quarter)
        factor, inverse = cholesky(gram_of(quarter))
    out = final(place[1:], inverse, parts)
    return (out.T, factor)


def solution(mesh):
    placed = (P(("wide", "by"), None, None), P(("wide", "by")), P(("wide", "by")), P("wide", None))
    return jax.shard_map(
        local, mesh=mesh, in_specs=placed, out_specs=(P("wide", None), P()), check_vma=False
    )
```

time: 648 us -> 338 us (0.52); the launches traced: 639 us -> 336 us
  waiting for transfers between devices: 271 us -> 113 us
  matrix products: 138 us -> 1.84 us
  Pallas kernels: 0 us -> 125 us
  local copies, waits for them, and re-layouts: 116 us -> 25.7 us
  blocking collectives: 48.7 us -> 0 us
  starting transfers between devices: 23.7 us -> 64.4 us
  other arithmetic: 26.4 us -> 4.21 us
  between operations: 14.6 us -> 0.97 us
    psum x2 -> x0, waiting for transfers between devices: 172 us -> none  [local(): image = lax.psum(partial_rows, 'by')]
    dot_general x18 -> x3, matrix products: 133 us -> 1.84 us  [the longest x1 1.12 us: local(): quarter = jnp.dot(inverse, quarter, precision=HIGHEST)]
    pallas_call x0 -> x11, Pallas kernels: none -> 125 us  [the longest x2 45.9 us: direct(): pl.pallas_call(functools.partial(direct_kernel, wide, cap), grid_spec=plt...]
    ppermute x0 -> x50, waiting for transfers between devices: none -> 112 us  [swap(): return lax.ppermute(x, axis, [(i, i ^ k) for i in range(size)])]
    all_to_all x5 -> x1, waiting for transfers between devices: 98.5 us -> 1.71 us  [local(): lax.all_to_all(request.reshape(wide, cap), 'wide', split_axis=0, concat_a...]
    dot_general x16 -> x0, local copies, waits for them, and re-layouts: 64.3 us -> none  [the longest x4 22.9 us: local(): jnp.dot(slot_table, received, precision=highest)]
    ppermute x0 -> x50, starting transfers between devices: none -> 59.2 us  [swap(): return lax.ppermute(x, axis, [(i, i ^ k) for i in range(size)])]
    psum x2 -> x0, blocking collectives: 48.7 us -> none  [local(): gram = lax.psum(jnp.dot(image.T, image, precision=highest), 'wide')]
  transfers between devices with their start and end apart: 7 -> 51, of which waited for: 5 -> 21; matrix products, arithmetic and copies ran while one was open for 22% -> 2% of each run, Pallas kernels for 0% -> 31%
where the time goes in v1:
time: 338 us; the launch traced here: 336 us
  Pallas kernels  125 us (37%)
  waiting for transfers between devices  113 us (33%)
  starting transfers between devices  64.4 us (19%)
  local copies, waits for them, and re-layouts  25.7 us (8%)
  other arithmetic  4.21 us (1%)
    ppermute x50, waiting for transfers between devices, swap(): return lax.ppermute(x, axis, [(i, i ^ k) for i in range(size)])  112 us
    ppermute x50, starting transfers between devices, swap(): return lax.ppermute(x, axis, [(i, i ^ k) for i in range(size)])  59.2 us
    pallas_call x2, Pallas kernels, direct(): pl.pallas_call(functools.partial(direct_kernel, wide, cap), grid_spec=plt...  45.9 us
    pallas_call x2, Pallas kernels, mirror(): pl.pallas_call(functools.partial(mirror_kernel, wide, cap), grid_spec=plt...  43.1 us
    unnamed x77, local copies, waits for them, and re-layouts  20.9 us
    pallas_call x2, Pallas kernels, cholesky(): pl.pallas_call(cholesky_kernel, out_shape=[shape, shape], name='cholesky')  15.4 us
    pallas_call x2, Pallas kernels, gather(): pl.pallas_call(functools.partial(gather_kernel, wide, cap, n_by, bs), gri...  10.8 us
    pallas_call x2, Pallas kernels, serve(): pl.pallas_call(functools.partial(serve_kernel, wide, cap, bs), grid_spec=...  8.2 us
  transfers between devices with their start and end apart: 51, of which 21 were waited for; matrix products, arithmetic and copies ran while one was open for 2% of the time, Pallas kernels for 31%

profile of v1, /device:TPU:0, one launch (start us, length us, event | category | flops | bytes accessed | tf_op | source)
XLA Modules:
  0.0 335.7 jit_solution(3902147492399747745)
XLA Ops:
  2.9 5.2 %all-to-all-start = ((s32[8,1,3]{2,1,0:T(1,128)}), s32[8,1,3]{2,1,0:T(1,128)S(1)}, u32[]{:S(2)}, u32[]{:S(2)}) async-start(s32[8,1,3]{2,1,0:T(1,128)} %bitcast.2), calls=%async_computation | async-start | bytes 8192 | tf_op jit(solution)/shard_map/all_to_all | solution.py:324
  13.9 4.1 %serve.2 = (f32[64,4096]{1,0:T(8,128)}, f32[64,1536]{1,0:T(8,128)}, f32[64,1536]{1,0:T(8,128)}, f32[64,1536]{1,0:T(8,128)}, f32[64,1536]{1,0:T(8,128)}, /*index=...) custom-call(s32[2]{0:T(128)} %pad_add_fusion.place_ref, s32[24]{0:T(128)} %max.6.wanted_ref, ...), custom_call_target="tpu_custom_call" | custom-call | tf_op jit(solution)/shard_map/serve/pallas_call | solution.py:62
  23.5 22.3 %mirror.2 = (f32[64,1536]{1,0:T(8,128)S(1)}, f32[64,1536]{1,0:T(8,128)S(1)}, f32[64,1536]{1,0:T(8,128)S(1)}, f32[64,1536]{1,0:T(8,128)}, f32[64,1536]{1,0:T(8,12...) custom-call(s32[2]{0:T(128)S(1)} %copy-done.18, s32[24]{0:T(128)S(1)} %get-tuple-element.104.tile_ref, ...), custom_call_target="tpu_custom_call" | custom-call | tf_op jit(solution)/shard_map/mirror/pallas_call | solution.py:131
  54.2 5.2 %collective-permute-done.5.refs_6_ = f32[64,1536]{1,0:T(8,128)S(1)} collective-permute-done((f32[64,1536]{1,0:T(8,128)S(1)}, f32[64,1536]{1,0:T(8,128)S(1)}, u32[]{:S(2)}, u32[]{:S(2)}) %collective-permute-start.5) | collective-permute-done | bytes 393248 | tf_op jit(solution)/shard_map/ppermute | solution.py:309
  60.8 6.2 %collective-permute-done.6.refs_7_ = f32[64,1536]{1,0:T(8,128)S(1)} collective-permute-done((f32[64,1536]{1,0:T(8,128)S(1)}, f32[64,1536]{1,0:T(8,128)S(1)}, u32[]{:S(2)}, u32[]{:S(2)}) %collective-permute-start.6) | collective-permute-done | bytes 393248 | tf_op jit(solution)/shard_map/ppermute | solution.py:309
  69.7 5.8 %collective-permute-done.8.refs_2_ = f32[64,1536]{1,0:T(8,128)S(1)} collective-permute-done((f32[64,1536]{1,0:T(8,128)S(1)}, f32[64,1536]{1,0:T(8,128)S(1)}, u32[]{:S(2)}, u32[]{:S(2)}) %collective-permute-start.8) | collective-permute-done | bytes 393248 | tf_op jit(solution)/shard_map/ppermute | solution.py:309
  85.0 22.9 %direct.2.start = f32[64,4096]{1,0:T(8,128)S(1)} custom-call(s32[2]{0:T(128)S(1)} %copy-done.19, s32[24]{0:T(128)S(1)} %copy-done.23, s32[24]{0:T(128)S(1)} %get-tuple-element.103.row_ref, s32[24]{0:T(128)S(1)} %get-tuple-element.102.valid_ref, f32[22,512,512]{2,1,0:T(8,128)} %tile.7, f32[64,1536]{1,0:T(8,128)S(1)} %copy-done.2, f32[64,1536]{1,0:T(8,128)S(1)} %copy-done.5, ...), custom_call_target="tpu_custom_call" | custom-call | tf_op jit(solution)/shard_map/direct/pallas_call | solution.py:182
  108.6 5.3 %gather.2 = (f32[64,1024]{1,0:T(8,128)S(1)}, f32[64,1024]{1,0:T(8,128)S(1)}, f32[64,1024]{1,0:T(8,128)S(1)}, f32[64,1024]{1,0:T(8,128)S(1)}) custom-call(s32[2]{0:T(128)S(1)} %copy-done.19, s32[24]{0:T(128)S(1)} %copy-done.25, s32[24]{0:T(128)S(1)} %copy-done.27, f32[64,4096]{1,0:T(8,128)S(1)} %direct.2.start, f32[64,1536]{1,0:T(8,128)S(1)} %get-tuple-element.56.refs_0_, ...), custom_call_target="tpu_custom_call" | custom-call | tf_op jit(solution)/shard_map/gather/pallas_call | solution.py:233
  118.3 10.1 %collective-permute-done.14 = f32[64,1024]{1,0:T(8,128)S(1)} collective-permute-done((f32[64,1024]{1,0:T(8,128)S(1)}, f32[64,1024]{1,0:T(8,128)S(1)}, u32[]{:S(2)}, u32[]{:S(2)}) %collective-permute-start.14) | collective-permute-done | bytes 262176 | tf_op jit(solution)/shard_map/ppermute | solution.py:309
  128.4 7.8 %collective-permute-done.16 = f32[64,1024]{1,0:T(8,128)S(1)} collective-permute-done((f32[64,1024]{1,0:T(8,128)S(1)}, f32[64,1024]{1,0:T(8,128)S(1)}, u32[]{:S(2)}, u32[]{:S(2)}) %collective-permute-start.16) | collective-permute-done | bytes 262176 | tf_op jit(solution)/shard_map/ppermute | solution.py:309
  139.5 10.5 %collective-permute-start.23 = (f32[64,1024]{1,0:T(8,128)S(1)}, f32[64,1024]{1,0:T(8,128)S(1)}, u32[]{:S(2)}, u32[]{:S(2)}) collective-permute-start(f32[64,1024]{1,0:T(8,128)S(1)} %add_add_fusion.refs_0_), channel_id=1, source_target_pairs={{0,2},{1,3},{2,0},{3,1},{4,6},{5,7},{6,4},{7,5},{8,10},{9,11},{10,... | collective-permute-start | bytes 786440 | tf_op jit(solution)/shard_map/ppermute | solution.py:309
  150.4 17.2 %collective-permute-done.23.refs_2_ = f32[64,1024]{1,0:T(8,128)S(1)} collective-permute-done((f32[64,1024]{1,0:T(8,128)S(1)}, f32[64,1024]{1,0:T(8,128)S(1)}, u32[]{:S(2)}, u32[]{:S(2)}) %collective-permute-start.23) | collective-permute-done | bytes 262176 | tf_op jit(solution)/shard_map/ppermute | solution.py:309
  169.0 4.1 %serve.3 = (f32[64,4096]{1,0:T(8,128)}, f32[64,1536]{1,0:T(8,128)}, f32[64,1536]{1,0:T(8,128)}, f32[64,1536]{1,0:T(8,128)}, f32[64,1536]{1,0:T(8,128)}, /*index=...) custom-call(s32[2]{0:T(128)} %pad_add_fusion.place_ref, s32[24]{0:T(128)} %max.6.wanted_ref, ...), custom_call_target="tpu_custom_call" | custom-call | tf_op jit(solution)/shard_map/serve/pallas_call | solution.py:62
  178.7 20.9 %mirror.3 = (f32[64,1536]{1,0:T(8,128)S(1)}, f32[64,1536]{1,0:T(8,128)S(1)}, f32[64,1536]{1,0:T(8,128)S(1)}, f32[64,1536]{1,0:T(8,128)S(1)}, f32[64,1536]{1,0:T(...) custom-call(s32[2]{0:T(128)S(1)} %copy-done.20, s32[24]{0:T(128)S(1)} %copy-done.24, ...), custom_call_target="tpu_custom_call" | custom-call | tf_op jit(solution)/shard_map/mirror/pallas_call | solution.py:131
  204.4 8.1 %collective-permute-done.30.refs_6_ = f32[64,1536]{1,0:T(8,128)S(1)} collective-permute-done((f32[64,1536]{1,0:T(8,128)S(1)}, f32[64,1536]{1,0:T(8,128)S(1)}, u32[]{:S(2)}, u32[]{:S(2)}) %collective-permute-start.30) | collective-permute-done | bytes 393248 | tf_op jit(solution)/shard_map/ppermute | solution.py:309
  213.6 6.7 %collective-permute-done.31.refs_7_ = f32[64,1536]{1,0:T(8,128)S(1)} collective-permute-done((f32[64,1536]{1,0:T(8,128)S(1)}, f32[64,1536]{1,0:T(8,128)S(1)}, u32[]{:S(2)}, u32[]{:S(2)}) %collective-permute-start.31) | collective-permute-done | bytes 393248 | tf_op jit(solution)/shard_map/ppermute | solution.py:309
  223.3 5.8 %collective-permute-done.33.refs_2_ = f32[64,1536]{1,0:T(8,128)S(1)} collective-permute-done((f32[64,1536]{1,0:T(8,128)S(1)}, f32[64,1536]{1,0:T(8,128)S(1)}, u32[]{:S(2)}, u32[]{:S(2)}) %collective-permute-start.33) | collective-permute-done | bytes 393248 | tf_op jit(solution)/shard_map/ppermute | solution.py:309
  230.5 22.9 %direct.3.start = f32[64,4096]{1,0:T(8,128)S(1)} custom-call(s32[2]{0:T(128)S(1)} %copy-done.20, s32[24]{0:T(128)S(1)} %copy-done.24, s32[24]{0:T(128)S(1)} %get-tuple-element.103.row_ref, s32[24]{0:T(128)S(1)} %get-tuple-element.102.valid_ref, f32[22,512,512]{2,1,0:T(8,128)} %tile.7, f32[64,1536]{1,0:T(8,128)S(1)} %copy-done.3, ...), custom_call_target="tpu_custom_call" | custom-call | tf_op jit(solution)/shard_map/direct/pallas_call | solution.py:182
  254.0 5.5 %gather.3 = (f32[64,1024]{1,0:T(8,128)S(1)}, f32[64,1024]{1,0:T(8,128)S(1)}, f32[64,1024]{1,0:T(8,128)S(1)}, f32[64,1024]{1,0:T(8,128)S(1)}) custom-call(s32[2]{0:T(128)S(1)} %copy-done.20, s32[24]{0:T(128)S(1)} %copy-done.26, s32[24]{0:T(128)S(1)} %copy-done.28, f32[64,4096]{1,0:T(8,128)S(1)} %direct.3.start, f32[64,1536]{1,0:T(8,128)S(1)} %get-tuple-element.78.refs_0_, ...), custom_call_target="tpu_custom_call" | custom-call | tf_op jit(solution)/shard_map/gather/pallas_call | solution.py:233
  273.4 8.2 %collective-permute-done.20 = f32[64,64]{1,0:T(8,128)S(1)} collective-permute-done((f32[64,64]{1,0:T(8,128)S(1)}, f32[64,64]{1,0:T(8,128)S(1)}, u32[]{:S(2)}, u32[]{:S(2)}) %collective-permute-start.20) | collective-permute-done | bytes 16416 | tf_op jit(solution)/shard_map/ppermute | solution.py:309
  282.6 5.8 %collective-permute-done.21 = f32[64,64]{1,0:T(8,128)S(1)} collective-permute-done((f32[64,64]{1,0:T(8,128)S(1)}, f32[64,64]{1,0:T(8,128)S(1)}, u32[]{:S(2)}, u32[]{:S(2)}) %collective-permute-start.21) | collective-permute-done | bytes 16416 | tf_op jit(solution)/shard_map/ppermute | solution.py:309
  289.0 7.7 %cholesky.2 = (f32[64,64]{1,0:T(8,128)}, f32[64,64]{1,0:T(8,128)}) custom-call(f32[64,64]{1,0:T(8,128)} %add.82.gram), custom_call_target="tpu_custom_call" | custom-call | tf_op jit(solution)/shard_map/cholesky/pallas_call | solution.py:268
  311.9 6.2 %collective-permute-done.45 = f32[64,64]{1,0:T(8,128)S(1)} collective-permute-done((f32[64,64]{1,0:T(8,128)S(1)}, f32[64,64]{1,0:T(8,128)S(1)}, u32[]{:S(2)}, u32[]{:S(2)}) %collective-permute-start.45) | collective-permute-done | bytes 16416 | tf_op jit(solution)/shard_map/ppermute | solution.py:309
  323.9 7.7 %cholesky.3 = (f32[64,64]{1,0:T(8,128)}, f32[64,64]{1,0:T(8,128)}) custom-call(f32[64,64]{1,0:T(8,128)} %add.90.gram), custom_call_target="tpu_custom_call" | custom-call | tf_op jit(solution)/shard_map/cholesky/pallas_call | solution.py:268
  (190 shorter events, 102.5 us)
Async XLA Ops:
  18.0 27.8 %collective-permute-start = (f32[64,1536]{1,0:T(8,128)}, f32[64,1536]{1,0:T(8,128)S(1)}, u32[]{:S(2)}, u32[]{:S(2)}) collective-permute-start(f32[64,1536]{1,0:T(8,128)} %get-tuple-element.48), channel_id=1, source_target_pairs={{0,4},{4,0},{8,12},{12,8},{16,20},{20,16},{24,28},{28,24},{1,5},{5... | collective-permute-start | bytes 1179656 | tf_op jit(solution)/shard_map/ppermute | solution.py:309
  18.1 30.1 %collective-permute-start.1 = (f32[64,1536]{1,0:T(8,128)}, f32[64,1536]{1,0:T(8,128)S(1)}, u32[]{:S(2)}, u32[]{:S(2)}) collective-permute-start(f32[64,1536]{1,0:T(8,128)} %get-tuple-element.49), channel_id=1, source_target_pairs={{0,8},{4,12},{8,0},{12,4},{16,24},{20,28},{24,16},{28,20},{1,9},{5... | collective-permute-start | bytes 1179656 | tf_op jit(solution)/shard_map/ppermute | solution.py:309
  18.7 31.3 %collective-permute-start.2 = (f32[64,1536]{1,0:T(8,128)}, f32[64,1536]{1,0:T(8,128)S(1)}, u32[]{:S(2)}, u32[]{:S(2)}) collective-permute-start(f32[64,1536]{1,0:T(8,128)} %get-tuple-element.50), channel_id=1, source_target_pairs={{0,12},{4,8},{8,4},{12,0},{16,28},{20,24},{24,20},{28,16},{1,13},{... | collective-permute-start | bytes 1179656 | tf_op jit(solution)/shard_map/ppermute | solution.py:309
  19.9 31.2 %collective-permute-start.3 = (f32[64,1536]{1,0:T(8,128)}, f32[64,1536]{1,0:T(8,128)S(1)}, u32[]{:S(2)}, u32[]{:S(2)}) collective-permute-start(f32[64,1536]{1,0:T(8,128)} %get-tuple-element.51), channel_id=1, source_target_pairs={{0,16},{4,20},{8,24},{12,28},{16,0},{20,4},{24,8},{28,12},{1,17},{... | collective-permute-start | bytes 1179656 | tf_op jit(solution)/shard_map/ppermute | solution.py:309
  20.5 31.6 %collective-permute-start.4 = (f32[64,1536]{1,0:T(8,128)}, f32[64,1536]{1,0:T(8,128)S(1)}, u32[]{:S(2)}, u32[]{:S(2)}) collective-permute-start(f32[64,1536]{1,0:T(8,128)} %get-tuple-element.52), channel_id=1, source_target_pairs={{0,20},{4,16},{8,28},{12,24},{16,4},{20,0},{24,12},{28,8},{1,21},{... | collective-permute-start | bytes 1179656 | tf_op jit(solution)/shard_map/ppermute | solution.py:309
  52.8 55.1 %collective-permute-start.9 = (f32[64,1536]{1,0:T(8,128)}, f32[64,1536]{1,0:T(8,128)S(1)}, u32[]{:S(2)}, u32[]{:S(2)}) collective-permute-start(f32[64,1536]{1,0:T(8,128)} %get-tuple-element.59), channel_id=1, source_target_pairs={{0,12},{4,8},{8,4},{12,0},{16,28},{20,24},{24,20},{28,16},{1,13},{... | collective-permute-start | bytes 1179656 | tf_op jit(solution)/shard_map/ppermute | solution.py:309
  60.2 47.8 %collective-permute-start.10 = (f32[64,1536]{1,0:T(8,128)}, f32[64,1536]{1,0:T(8,128)S(1)}, u32[]{:S(2)}, u32[]{:S(2)}) collective-permute-start(f32[64,1536]{1,0:T(8,128)} %get-tuple-element.60), channel_id=1, source_target_pairs={{0,16},{4,20},{8,24},{12,28},{16,0},{20,4},{24,8},{28,12},{1,17},{... | collective-permute-start | bytes 1179656 | tf_op jit(solution)/shard_map/ppermute | solution.py:309
  67.8 40.2 %collective-permute-start.11 = (f32[64,1536]{1,0:T(8,128)}, f32[64,1536]{1,0:T(8,128)S(1)}, u32[]{:S(2)}, u32[]{:S(2)}) collective-permute-start(f32[64,1536]{1,0:T(8,128)} %get-tuple-element.61), channel_id=1, source_target_pairs={{0,20},{4,16},{8,28},{12,24},{16,4},{20,0},{24,12},{28,8},{1,21},{... | collective-permute-start | bytes 1179656 | tf_op jit(solution)/shard_map/ppermute | solution.py:309
  68.7 39.3 %collective-permute-start.12 = (f32[64,1536]{1,0:T(8,128)}, f32[64,1536]{1,0:T(8,128)S(1)}, u32[]{:S(2)}, u32[]{:S(2)}) collective-permute-start(f32[64,1536]{1,0:T(8,128)} %get-tuple-element.62), channel_id=1, source_target_pairs={{0,24},{4,28},{8,16},{12,20},{16,8},{20,12},{24,0},{28,4},{1,25},{... | collective-permute-start | bytes 1179656 | tf_op jit(solution)/shard_map/ppermute | solution.py:309
  75.5 32.5 %collective-permute-start.13 = (f32[64,1536]{1,0:T(8,128)}, f32[64,1536]{1,0:T(8,128)S(1)}, u32[]{:S(2)}, u32[]{:S(2)}) collective-permute-start(f32[64,1536]{1,0:T(8,128)} %get-tuple-element.63), channel_id=1, source_target_pairs={{0,28},{4,24},{8,20},{12,16},{16,12},{20,8},{24,4},{28,0},{1,29},{... | collective-permute-start | bytes 1179656 | tf_op jit(solution)/shard_map/ppermute | solution.py:309
  139.5 28.2 %collective-permute-start.23 = (f32[64,1024]{1,0:T(8,128)S(1)}, f32[64,1024]{1,0:T(8,128)S(1)}, u32[]{:S(2)}, u32[]{:S(2)}) collective-permute-start(f32[64,1024]{1,0:T(8,128)S(1)} %add_add_fusion.refs_0_), channel_id=1, source_target_pairs={{0,2},{1,3},{2,0},{3,1},{4,6},{5,7},{6,4},{7,5},{8,10},{9,11},{10,... | collective-permute-start | bytes 786440 | tf_op jit(solution)/shard_map/ppermute | solution.py:309
  173.2 28.3 %collective-permute-start.26 = (f32[64,1536]{1,0:T(8,128)}, f32[64,1536]{1,0:T(8,128)S(1)}, u32[]{:S(2)}, u32[]{:S(2)}) collective-permute-start(f32[64,1536]{1,0:T(8,128)} %get-tuple-element.71), channel_id=1, source_target_pairs={{0,8},{4,12},{8,0},{12,4},{16,24},{20,28},{24,16},{28,20},{1,9},{5... | collective-permute-start | bytes 1179656 | tf_op jit(solution)/shard_map/ppermute | solution.py:309
  175.2 27.6 %collective-permute-start.28 = (f32[64,1536]{1,0:T(8,128)}, f32[64,1536]{1,0:T(8,128)S(1)}, u32[]{:S(2)}, u32[]{:S(2)}) collective-permute-start(f32[64,1536]{1,0:T(8,128)} %get-tuple-element.73), channel_id=1, source_target_pairs={{0,16},{4,20},{8,24},{12,28},{16,0},{20,4},{24,8},{28,12},{1,17},{... | collective-permute-start | bytes 1179656 | tf_op jit(solution)/shard_map/ppermute | solution.py:309
  176.1 28.1 %collective-permute-start.29 = (f32[64,1536]{1,0:T(8,128)}, f32[64,1536]{1,0:T(8,128)S(1)}, u32[]{:S(2)}, u32[]{:S(2)}) collective-permute-start(f32[64,1536]{1,0:T(8,128)} %get-tuple-element.74), channel_id=1, source_target_pairs={{0,20},{4,16},{8,28},{12,24},{16,4},{20,0},{24,12},{28,8},{1,21},{... | collective-permute-start | bytes 1179656 | tf_op jit(solution)/shard_map/ppermute | solution.py:309
  204.3 49.1 %collective-permute-start.34 = (f32[64,1536]{1,0:T(8,128)S(1)}, f32[64,1536]{1,0:T(8,128)S(1)}, u32[]{:S(2)}, u32[]{:S(2)}) collective-permute-start(f32[64,1536]{1,0:T(8,128)S(1)} %get-tuple-element.81), channel_id=1, source_target_pairs={{0,12},{4,8},{8,4},{12,0},{16,28},{20,24},{24,20},{28,16},{1,13},{... | collective-permute-start | bytes 1179656 | tf_op jit(solution)/shard_map/ppermute | solution.py:309
  212.5 40.9 %collective-permute-start.35 = (f32[64,1536]{1,0:T(8,128)S(1)}, f32[64,1536]{1,0:T(8,128)S(1)}, u32[]{:S(2)}, u32[]{:S(2)}) collective-permute-start(f32[64,1536]{1,0:T(8,128)S(1)} %get-tuple-element.82), channel_id=1, source_target_pairs={{0,16},{4,20},{8,24},{12,28},{16,0},{20,4},{24,8},{28,12},{1,17},{... | collective-permute-start | bytes 1179656 | tf_op jit(solution)/shard_map/ppermute | solution.py:309
  220.3 33.1 %collective-permute-start.36 = (f32[64,1536]{1,0:T(8,128)S(1)}, f32[64,1536]{1,0:T(8,128)S(1)}, u32[]{:S(2)}, u32[]{:S(2)}) collective-permute-start(f32[64,1536]{1,0:T(8,128)S(1)} %get-tuple-element.83), channel_id=1, source_target_pairs={{0,20},{4,16},{8,28},{12,24},{16,4},{20,0},{24,12},{28,8},{1,21},{... | collective-permute-start | bytes 1179656 | tf_op jit(solution)/shard_map/ppermute | solution.py:309
  221.5 31.9 %collective-permute-start.37 = (f32[64,1536]{1,0:T(8,128)S(1)}, f32[64,1536]{1,0:T(8,128)S(1)}, u32[]{:S(2)}, u32[]{:S(2)}) collective-permute-start(f32[64,1536]{1,0:T(8,128)S(1)} %get-tuple-element.84), channel_id=1, source_target_pairs={{0,24},{4,28},{8,16},{12,20},{16,8},{20,12},{24,0},{28,4},{1,25},{... | collective-permute-start | bytes 1179656 | tf_op jit(solution)/shard_map/ppermute | solution.py:309
  259.4 37.3 %collective-permute-start.39 = (f32[64,1024]{1,0:T(8,128)S(1)}, f32[64,1024]{1,0:T(8,128)S(1)}, u32[]{:S(2)}, u32[]{:S(2)}) collective-permute-start(f32[64,1024]{1,0:T(8,128)S(1)} %get-tuple-element.87), channel_id=1, source_target_pairs={{0,1},{1,0},{2,3},{3,2},{4,5},{5,4},{6,7},{7,6},{8,9},{9,8},{10,11... | collective-permute-start | bytes 786440 | tf_op jit(solution)/shard_map/ppermute | solution.py:309
  259.5 37.2 %collective-permute-start.40 = (f32[64,1024]{1,0:T(8,128)S(1)}, f32[64,1024]{1,0:T(8,128)S(1)}, u32[]{:S(2)}, u32[]{:S(2)}) collective-permute-start(f32[64,1024]{1,0:T(8,128)S(1)} %get-tuple-element.88), channel_id=1, source_target_pairs={{0,2},{1,3},{2,0},{3,1},{4,6},{5,7},{6,4},{7,5},{8,10},{9,11},{10,... | collective-permute-start | bytes 786440 | tf_op jit(solution)/shard_map/ppermute | solution.py:309
  263.0 33.7 %collective-permute-start.41 = (f32[64,1024]{1,0:T(8,128)S(1)}, f32[64,1024]{1,0:T(8,128)S(1)}, u32[]{:S(2)}, u32[]{:S(2)}) collective-permute-start(f32[64,1024]{1,0:T(8,128)S(1)} %get-tuple-element.89), channel_id=1, source_target_pairs={{0,3},{1,2},{2,1},{3,0},{4,7},{5,6},{6,5},{7,4},{8,11},{9,10},{10,... | collective-permute-start | bytes 786440 | tf_op jit(solution)/shard_map/ppermute | solution.py:309
  297.8 35.2 %collective-permute-start.49 = (f32[64,1024]{1,0:T(8,128)S(1)}, f32[64,1024]{1,0:T(8,128)S(1)}, u32[]{:S(2)}, u32[]{:S(2)}) collective-permute-start(f32[64,1024]{1,0:T(8,128)S(1)} %fusion.refs_0_), channel_id=1, source_target_pairs={{0,3},{1,2},{2,1},{3,0},{4,7},{5,6},{6,5},{7,4},{8,11},{9,10},{10,... | collective-permute-start | bytes 786440 | tf_op jit(solution)/shard_map/ppermute | solution.py:309
  300.3 32.7 %collective-permute-start.48 = (f32[64,1024]{1,0:T(8,128)S(1)}, f32[64,1024]{1,0:T(8,128)S(1)}, u32[]{:S(2)}, u32[]{:S(2)}) collective-permute-start(f32[64,1024]{1,0:T(8,128)S(1)} %fusion.refs_0_), channel_id=1, source_target_pairs={{0,2},{1,3},{2,0},{3,1},{4,6},{5,7},{6,4},{7,5},{8,10},{9,11},{10,... | collective-permute-start | bytes 786440 | tf_op jit(solution)/shard_map/ppermute | solution.py:309
  300.3 32.7 %collective-permute-start.47 = (f32[64,1024]{1,0:T(8,128)S(1)}, f32[64,1024]{1,0:T(8,128)S(1)}, u32[]{:S(2)}, u32[]{:S(2)}) collective-permute-start(f32[64,1024]{1,0:T(8,128)S(1)} %fusion.refs_0_), channel_id=1, source_target_pairs={{0,1},{1,0},{2,3},{3,2},{4,5},{5,4},{6,7},{7,6},{8,9},{9,8},{10,11... | collective-permute-start | bytes 786440 | tf_op jit(solution)/shard_map/ppermute | solution.py:309
  (65 other events, 1156.2 us)

commit v2 on v0

v2 whole, which is shorter than its diff:
```python
import functools

import jax
import jax.numpy as jnp
from jax import lax
from jax.experimental import pallas as pl
from jax.experimental.pallas import tpu as pltpu
from jax.sharding import PartitionSpec as P

ITERS = 2
HALVES = 2
RING = 6
HIGHEST = lax.Precision.HIGHEST
F32 = jnp.float32
SMEM = pl.BlockSpec(memory_space=pltpu.SMEM)
VMEM = pl.BlockSpec(memory_space=pltpu.VMEM)
ANY = pl.BlockSpec(memory_space=pl.ANY)
HBM = pl.BlockSpec(memory_space=pltpu.HBM)


def shape(*dims):
    return jax.ShapeDtypeStruct(dims, F32)


def params(mib):
    return pltpu.CompilerParams(vmem_limit_bytes=mib << 20)


def block(index, size):
    return pl.ds(pl.multiple_of(index * size, size), size)


def split_pair(x):
    high = x.astype(jnp.bfloat16)
    low = (x - high.astype(F32)).astype(jnp.bfloat16)
    return high, low


def load_kernel(tiles, *refs):
    high, low, ring, sems = refs[-4:]
    count, depth = tiles.shape[0], ring.shape[0]

    def copy(t):
        at = lax.rem(t, depth)
        return pltpu.make_async_copy(tiles.at[t], ring.at[at], sems.at[at])

    for t in range(min(depth, count)):
        copy(t).start()

    def step(t, carry):
        copy(t).wait()
        high[t], low[t] = split_pair(ring[lax.rem(t, depth)])

        @pl.when(t + depth < count)
        def _():
            copy(t + depth).start()

        return carry

    lax.fori_loop(0, count, step, 0)


def load(tiles, after=()):
    split = jax.ShapeDtypeStruct(tiles.shape, jnp.bfloat16)
    return pl.pallas_call(
        load_kernel,
        in_specs=[ANY] * (1 + len(after)),
        out_specs=[VMEM] * 2,
        out_shape=[split] * 2,
        scratch_shapes=[
            pltpu.VMEM((RING,) + tiles.shape[1:], F32),
            pltpu.SemaphoreType.DMA((RING,)),
        ],
        compiler_params=params(8),
        name="load",
    )(tiles, *after)


def tile_products(panel, tile, transposed):
    width = panel.shape[0]
    panel_high, panel_low = split_pair(panel)
    stacked = jnp.concatenate([panel_high, panel_low], axis=0)
    dims = (((1,), (1 if transposed else 0,)), ((), ()))
    both = lax.dot_general(stacked, tile[0][...], dims, preferred_element_type=F32)
    rest = lax.dot_general(panel_high, tile[1][...], dims, preferred_element_type=F32)
    return both[:width] + (both[width:] + rest)


def serve_kernel(chips, group, bs, place, wanted, own, sibling, *refs):
    pair, outs = refs[-chips], refs[1 - chips :]
    core = place[1]
    rows = own.shape[1]
    pair[:, block(core, rows)] = own[...]
    pair[:, block(1 - core, rows)] = sibling[...]
    for k in range(1, chips):
        for i in range(group):
            slot = (place[0] ^ k) * group + i
            outs[k - 1][:, i * bs : (i + 1) * bs] = pair[:, block(wanted[slot], bs)]


def serve(place, wanted, own, sibling, chips, group, bs, after=()):
    width, rows = own.shape
    outs = pl.pallas_call(
        functools.partial(serve_kernel, chips, group, bs),
        in_specs=[SMEM, SMEM, VMEM, VMEM] + [ANY] * len(after),
        out_specs=[VMEM] * chips,
        out_shape=[shape(width, 2 * rows)] + [shape(width, group * bs)] * (chips - 1),
        compiler_params=params(6),
        name="serve",
    )(place, wanted, own, sibling, *after)
    return outs[0], outs[1:]


def panel_block(pieces, at):
    return jnp.concatenate([piece[:, at] for piece in pieces], axis=0)


def visit_tiles(ks, group, place, tile_ref, valid_ref, tiles, body):
    def step(s, carry):
        slot = (place[0] ^ (ks[0] + s // group)) * group + s % group

        @pl.when(valid_ref[slot] == 1)
        def _():
            body(slot, [part.at[tile_ref[slot]] for part in tiles])

        return carry

    lax.fori_loop(0, len(ks) * group, step, 0)


def mirror_kernel(chips, group, parts, place, tile_ref, valid_ref, row_ref, high, low, *refs):
    pairs = refs[:parts]
    outs = refs[1 - chips :]
    bs = high.shape[1]
    base = place[1] * (pairs[0].shape[1] // (2 * bs))

    def body(slot, tile):
        panel = panel_block(pairs, block(base + row_ref[slot], bs))
        value = tile_products(panel, tile, False)
        for k in range(1, chips):
            @pl.when(slot // group == place[0] ^ k)
            def _():
                outs[k - 1][:, block(slot % group, bs)] = value

    visit_tiles(range(1, chips), group, place, tile_ref, valid_ref, [high, low], body)


def mirror(place, tables, tiles, pairs, chips, group, after=()):
    half = pairs[0].shape[0]
    bs = tiles[0].shape[1]
    parts = len(pairs)
    return pl.pallas_call(
        functools.partial(mirror_kernel, chips, group, parts),
        in_specs=[SMEM] * 4 + [VMEM] * 2 + [VMEM] * parts + [ANY] * len(after),
        out_specs=[VMEM] * (chips - 1),
        out_shape=[shape(half * parts, group * bs)] * (chips - 1),
        compiler_params=params(6),
        name="mirror",
    )(place, *tables[:3], *tiles, *pairs, *after)


def own_kernel(group, parts, place, tile_ref, valid_ref, row_ref, col_ref, high, low, *refs):
    pairs, total = refs[:parts], refs[-1]
    bs = high.shape[1]
    base = place[1] * (total.shape[1] // (2 * bs))
    total[...] = jnp.zeros_like(total)

    def body(slot, tile):
        row = block(base + row_ref[slot], bs)
        col = block(col_ref[slot], bs)
        total[:, col] += tile_products(panel_block(pairs, row), tile, False)
        total[:, row] += tile_products(panel_block(pairs, col), tile, True)

    visit_tiles(range(1), group, place, tile_ref, valid_ref, [high, low], body)


def own(place, tables, tiles, pairs, group, after=()):
    parts = len(pairs)
    half, rows = pairs[0].shape
    return pl.pallas_call(
        functools.partial(own_kernel, group, parts),
        in_specs=[SMEM] * 5 + [VMEM] * (2 + parts) + [ANY] * len(after),
        out_specs=VMEM,
        out_shape=shape(half * parts, rows),
        compiler_params=params(6),
        name="own",
    )(place, *tables, *tiles, *pairs, *after)


def direct_kernel(chips, group, parts, place, tile_ref, valid_ref, row_ref, high, low, *refs):
    received = refs[: parts * (chips - 1)]
    start = refs[parts * (chips - 1)]
    total, panel = refs[-2:]
    bs = high.shape[1]
    base = place[1] * (total.shape[1] // (2 * bs))
    total[...] = start[...]

    def body(slot, tile):
        for k in range(1, chips):
            @pl.when(slot // group == place[0] ^ k)
            def _():
                source = [received[h * (chips - 1) + k - 1] for h in range(parts)]
                panel[...] = panel_block(source, block(slot % group, bs))

        row = block(base + row_ref[slot], bs)
        total[:, row] += tile_products(panel[...], tile, True)

    visit_tiles(range(1, chips), group, place, tile_ref, valid_ref, [high, low], body)


def direct(place, tables, tiles, start, received, chips, group, after=()):
    parts = len(received)
    arrived = [x for xs in received for x in xs]
    return pl.pallas_call(
        functools.partial(direct_kernel, chips, group, parts),
        in_specs=[SMEM] * 4 + [VMEM] * (3 + len(arrived)) + [ANY] * len(after),
        out_specs=VMEM,
        out_shape=shape(*start.shape),
        scratch_shapes=[pltpu.VMEM((start.shape[0], tiles[0].shape[1]), F32)],
        compiler_params=params(6),
        name="direct",
    )(place, *tables[:3], *tiles, *arrived, start, *after)


def gather_kernel(chips, group, bs, place, wanted, flag, start, *refs):
    returned = refs[: chips - 1]
    own, sibling, total = refs[-3:]
    total[...] = start[...]
    for k in range(1, chips):
        first = (place[0] ^ k) * group

        def step(i, carry):
            @pl.when(flag[first + i] == 1)
            def _():
                total[:, block(wanted[first + i], bs)] += returned[k - 1][:, block(i, bs)]

            return carry

        lax.fori_loop(0, group, step, 0)
    rows = own.shape[1]
    own[...] = total[:, block(place[1], rows)]
    sibling[...] = total[:, block(1 - place[1], rows)]


def gather(place, wanted, flag, start, returned, chips, group, bs, after=()):
    width, rows = start.shape
    return pl.pallas_call(
        functools.partial(gather_kernel, chips, group, bs),
        in_specs=[SMEM] * 3 + [VMEM] * chips + [ANY] * len(after),
        out_specs=[VMEM] * 2,
        out_shape=[shape(width, rows // 2)] * 2,
        scratch_shapes=[pltpu.VMEM((width, rows), F32)],
        compiler_params=params(6),
        name="gather",
    )(place, wanted, flag, start, *returned, *after)


def deal_kernel(place, own, other, *outs):
    half, quarter = outs[0].shape[0], outs[0].shape[1] // 2
    for n, out in enumerate(outs):
        rows = slice(n // 2 * half, (n // 2 + 1) * half)
        for at, j in enumerate(((0, 3), (1, 2))[n % 2]):
            source = block(place[2] ^ j, quarter)
            out[:, at * quarter : (at + 1) * quarter] = own[rows, source] + other[rows, source]


def deal(place, own, other, n_by, parts):
    width, rows = own.shape
    outs = pl.pallas_call(
        deal_kernel,
        in_specs=[SMEM, VMEM, VMEM],
        out_specs=[VMEM] * (parts * 2),
        out_shape=[shape(width // parts, rows // 2)] * (parts * 2),
        compiler_params=params(6),
        name="deal",
    )(place, own, other)
    return [outs[h * 2 : (h + 1) * 2] for h in range(parts)]


def add_kernel(kept, arrived, mine, other):
    quarter = mine.shape[1]
    mine[...] = kept[:, :quarter] + arrived[:, :quarter]
    other[...] = kept[:, quarter:] + arrived[:, quarter:]


def add_pair(kept, arrived):
    half, both = kept.shape
    return pl.pallas_call(
        add_kernel,
        in_specs=[VMEM] * 2,
        out_specs=[VMEM] * 2,
        out_shape=[shape(half, both // 2)] * 2,
        compiler_params=params(6),
        name="add",
    )(kept, arrived)


def total_kernel(mine, arrived, *refs):
    refs[-1][...] = mine[...] + arrived[...]


def total(mine, arrived, after=()):
    return pl.pallas_call(
        total_kernel,
        in_specs=[VMEM] * 2 + [ANY] * len(after),
        out_specs=VMEM,
        out_shape=shape(*mine.shape),
        compiler_params=params(6),
        name="total",
    )(mine, arrived, *after)


def join_kernel(place, mine, across, nearby, *refs):
    out = refs[-1]
    quarter = mine.shape[1]
    out[:, block(place[2], quarter)] = mine[...]
    out[:, block(place[2] ^ 3, quarter)] = across[...]
    out[:, block(place[2] ^ 1, quarter)] = nearby[:, :quarter]
    out[:, block(place[2] ^ 2, quarter)] = nearby[:, quarter:]


def join(place, mine, across, nearby, after=()):
    half, quarter = mine.shape
    return pl.pallas_call(
        join_kernel,
        in_specs=[SMEM] + [VMEM] * 3 + [ANY] * len(after),
        out_specs=VMEM,
        out_shape=shape(half, quarter * 4),
        compiler_params=params(6),
        name="join",
    )(place, mine, across, nearby, *after)


def cholesky_kernel(gram, factor_t, inverse):
    n = gram.shape[0]
    row = lax.broadcasted_iota(jnp.int32, (n, 2 * n), 0)
    lane = lax.broadcasted_iota(jnp.int32, (n, 2 * n), 1)
    eye = (row[:, :n] == lane[:, :n]).astype(F32)
    work = jnp.concatenate([gram[...], eye], axis=1)
    for j in range(n):
        scale = 1.0 / jnp.sqrt(work[j : j + 1, j : j + 1])
        pivot_row = work[j : j + 1, :] * scale
        column = work[:, j : j + 1] * scale
        work = jnp.where(row == j, pivot_row, jnp.where(row > j, work - column * pivot_row, work))
    upper = row[:, :n] <= lane[:, :n]
    factor_t[...] = jnp.where(upper, work[:, :n], 0.0)
    inverse[...] = jnp.where(row[:, :n] >= lane[:, :n], work[:, n:], 0.0)


def cholesky(gram):
    n = gram.shape[0]
    factor_t, inverse = pl.pallas_call(
        cholesky_kernel, out_shape=[shape(n, n)] * 2, compiler_params=params(8), name="cholesky"
    )(gram)
    return factor_t.T, inverse


def final_kernel(inverse, panel, out):
    out[...] = jnp.dot(inverse[...], panel[...], precision=HIGHEST, preferred_element_type=F32)


def final(inverse, panel):
    return pl.pallas_call(
        final_kernel,
        in_specs=[VMEM] * 2,
        out_specs=VMEM,
        out_shape=shape(*panel.shape),
        compiler_params=params(16),
        name="final",
    )(inverse, panel)


def local(tiles, tile_rows, tile_cols, start_panel):
    wide = lax.axis_size("wide")
    n_by = lax.axis_size("by")
    me = lax.axis_index("wide")
    tile_count, bs, _ = tiles.shape
    rows, width = start_panel.shape
    block_rows = rows // bs
    cap = max(2, tile_count // wide + 1)
    chips, group = wide // 2, 2 * cap
    slots = wide * cap
    i32 = jnp.int32

    def swap(x, axis, k):
        size = wide if axis == "wide" else n_by
        return lax.ppermute(x, axis, [(i, i ^ k) for i in range(size)])

    def swap_core(x):
        return swap(x, "wide", 1)

    def swap_chips(parts):
        return [swap(part, "wide", 2 * (k + 1)) for k, part in enumerate(parts)]

    peer = tile_cols // block_rows
    order = jnp.arange(tile_count, dtype=i32)
    earlier = (order[:, None] > order[None, :]) & (peer[:, None] == peer[None, :])
    rank = jnp.sum(earlier.astype(i32), axis=1)
    match = (peer * cap + rank)[:, None] == jnp.arange(slots, dtype=i32)[None, :]
    pick = lambda v: jnp.sum(jnp.where(match, v[:, None], 0), axis=0)
    request = pick(tile_cols % (2 * block_rows) + 1)
    tables = (pick(order), (request > 0).astype(i32), pick(tile_rows), jnp.maximum(request - 1, 0))
    place = jnp.stack([me // 2, me % 2, lax.axis_index("by")]).astype(i32)

    by_chip = request.reshape(chips, group)
    mine = place[0] ^ jnp.arange(chips, dtype=i32)
    xored = by_chip[mine]
    asked = jnp.stack([jnp.zeros((group,), i32)] + swap_chips([xored[k] for k in range(1, chips)]))
    incoming = asked[mine].reshape(slots)
    flag = (incoming > 0).astype(i32)
    wanted = jnp.maximum(incoming - 1, 0)

    halves = range(HALVES)

    def gate(x, *deps):
        return lax.optimization_barrier((x, *deps))[0] if deps else x

    def all_sum(x, axis, masks, *deps):
        level = [x] + [gate(swap(x, axis, mask), *deps) for mask in masks[1:]]
        while len(level) > 1:
            level = [level[i] + level[i + 1] for i in range(0, len(level), 2)]
        return level[0]

    def gram_of(quarters):
        panel = jnp.concatenate(quarters, axis=0)
        return jnp.dot(panel, panel.T, precision=HIGHEST)

    def gram_chips(gram):
        done = 1
        while done < chips:
            step = min(4, chips // done)
            gram = all_sum(gram, "wide", [2 * done * m for m in range(step)])
            done *= step
        return gram

    def serve_half(own, sibling, after=()):
        return serve(place, wanted, own, sibling, chips, group, bs, after)

    def reduce_halves(start, returned, after=()):
        own, other = gather(place, wanted, flag, start, returned, chips, group, bs)
        dealt = deal(place, own, swap_core(other), n_by, HALVES)
        crossing = [add_pair(kept, swap(sent, "by", 1)) for kept, sent in dealt]
        quarters = []
        for mine, other in crossing:
            quarters.append(total(mine, swap(other, "by", 3), after))
            after = [quarters[-1]]
        return quarters

    def spread(quarter):
        across = swap(quarter, "by", 3)
        nearby = swap(jnp.concatenate([quarter, across], axis=1), "by", 1)
        return quarter, across, nearby

    by_all, core_pair = list(range(n_by)), [0, 1]
    panel_t = start_panel.T
    pair, served = serve_half(panel_t, swap_core(panel_t))
    received = [swap_chips(served)]
    tiles = load(tiles, [pair])
    mirrored = mirror(place, tables, tiles, [pair], chips, group)
    start = own(place, tables, tiles, [pair], group, [mirrored[0]])
    start = direct(place, tables, tiles, start, received, chips, group)
    quarters = reduce_halves(start, swap_chips(mirrored))
    spreads = [spread(quarter) for quarter in quarters]
    gram = all_sum(gram_of(quarters), "wide", core_pair)
    pairs, served, last = [], [], [quarters[-1]]
    for h in halves:
        piece = join(place, *spreads[h], last)
        pair, out = serve_half(piece, swap_core(piece), [gram])
        pairs.append(pair)
        served.append(out)
        if h == 0:
            gram = gram_chips(gram)
            last = [out[0], gram]
    received = [swap_chips(out) for out in served]
    mirrored = mirror(place, tables, tiles, pairs, chips, group)
    returned = swap_chips([gate(x, *received[0]) for x in mirrored])
    gram = all_sum(gram, "by", by_all)
    start = own(place, tables, tiles, pairs, group, [mirrored[0], gram])
    factor, inverse = cholesky(gate(gram, start))
    start = direct(place, tables, tiles, start, received, chips, group, [inverse])
    quarters = reduce_halves(start, returned)
    quarter = jnp.dot(inverse, jnp.concatenate(quarters, axis=0), precision=HIGHEST)
    gram = all_sum(gram_of([quarter]), "by", by_all)
    normal = join(place, *spread(gate(quarter, gram)))
    gram = gram_chips(all_sum(gram, "wide", core_pair))
    factor, inverse = cholesky(gram)
    out = final(inverse, normal)
    return (out.T, factor)


def solution(mesh):
    placed = (P(("wide", "by"), None, None), P(("wide", "by")), P(("wide", "by")), P("wide", None))
    return jax.shard_map(
        local, mesh=mesh, in_specs=placed, out_specs=(P("wide", None), P()), check_vma=False
    )
```

time: 648 us -> 290 us (0.45); the launches traced: 639 us -> 290 us
  waiting for transfers between devices: 271 us -> 133 us
  matrix products: 138 us -> 1.06 us
  local copies, waits for them, and re-layouts: 116 us -> 13 us
  Pallas kernels: 0 us -> 75.3 us
  blocking collectives: 48.7 us -> 0 us
  starting transfers between devices: 23.7 us -> 64.4 us
  other arithmetic: 26.4 us -> 1.9 us
  between operations: 14.6 us -> 0.99 us
    psum x2 -> x0, waiting for transfers between devices: 172 us -> none  [local(): image = lax.psum(partial_rows, 'by')]
    ppermute x0 -> x51, waiting for transfers between devices: none -> 133 us  [swap(): return lax.ppermute(x, axis, [(i, i ^ k) for i in range(size)])]
    dot_general x18 -> x3, matrix products: 133 us -> 1.06 us  [the longest x2 0.71 us: gram_of(): return jnp.dot(panel, panel.T, precision=HIGHEST)]
    all_to_all x5 -> x0, waiting for transfers between devices: 98.5 us -> none  [the longest x2 56.9 us: local(): lax.all_to_all(outgoing, 'wide', split_axis=0, concat_axis=0, tiled=True)]
    pallas_call x0 -> x28, Pallas kernels: none -> 75.3 us  [the longest x2 18.6 us: direct(): pl.pallas_call(functools.partial(direct_kernel, chips, group, parts), in_...]
    ppermute x0 -> x51, starting transfers between devices: none -> 64.4 us  [swap(): return lax.ppermute(x, axis, [(i, i ^ k) for i in range(size)])]
    dot_general x16 -> x0, local copies, waits for them, and re-layouts: 64.3 us -> none  [the longest x4 22.9 us: local(): jnp.dot(slot_table, received, precision=highest)]
    psum x2 -> x0, blocking collectives: 48.7 us -> none  [local(): gram = lax.psum(jnp.dot(image.T, image, precision=highest), 'wide')]
  transfers between devices with their start and end apart: 7 -> 51, of which waited for: 5 -> 34; matrix products, arithmetic and copies ran while one was open for 22% -> 1% of each run, Pallas kernels for 0% -> 22%
where the time goes in v2:
time: 290 us
  waiting for transfers between devices  133 us (46%)
  Pallas kernels  75.3 us (26%)
  starting transfers between devices  64.4 us (22%)
  local copies, waits for them, and re-layouts  13 us (4%)
    ppermute x51, waiting for transfers between devices, swap(): return lax.ppermute(x, axis, [(i, i ^ k) for i in range(size)])  133 us
    ppermute x51, starting transfers between devices, swap(): return lax.ppermute(x, axis, [(i, i ^ k) for i in range(size)])  64.4 us
    pallas_call x2, Pallas kernels, direct(): pl.pallas_call(functools.partial(direct_kernel, chips, group, parts), in_...  18.6 us
    pallas_call x2, Pallas kernels, mirror(): pl.pallas_call(functools.partial(mirror_kernel, chips, group, parts), in_...  13.9 us
    pallas_call x2, Pallas kernels, cholesky(): pl.pallas_call(cholesky_kernel, out_shape=[shape(n, n)] * 2, compiler_par...  13.2 us
    unnamed x19, local copies, waits for them, and re-layouts  11.6 us
    pallas_call x2, Pallas kernels, own(): pl.pallas_call(functools.partial(own_kernel, group, parts), in_specs=[SME...  9.1 us
    pallas_call x1, Pallas kernels, load(): pl.pallas_call(load_kernel, in_specs=[ANY] * (1 + len(after)), out_specs=...  8.07 us
  transfers between devices with their start and end apart: 51, of which 34 were waited for; matrix products, arithmetic and copies ran while one was open for 1% of the time, Pallas kernels for 22%

profile of v2, /device:TPU:0, one launch (start us, length us, event | category | flops | bytes accessed | tf_op | source)
XLA Modules:
  0.0 289.7 jit_solution(3484004329376153485)
XLA Ops:
  19.4 8.1 %load.1 = (bf16[22,512,512]{2,1,0:T(8,128)(2,1)S(1)}, bf16[22,512,512]{2,1,0:T(8,128)(2,1)S(1)}) custom-call(f32[22,512,512]{2,1,0:T(8,128)} %tiles.1, f32[64,8192]{1,0:T(8,128)S(1)} %get-tuple-element.50.refs_0_), custom_call_target="tpu_custom_call" | custom-call | tf_op jit(solution)/shard_map/load/pallas_call | solution.py:65
  27.5 8.0 %mirror.2 = (f32[64,3072]{1,0:T(8,128)S(1)}, f32[64,3072]{1,0:T(8,128)}, f32[64,3072]{1,0:T(8,128)}) custom-call(s32[3]{0:T(128)S(1)} %pad_add_fusion.1.place, s32[24]{0:T(128)S(1)} %get-tuple-element.103.tile_ref, s32[24]{0:T(128)S(1)} %compare_convert_fusion.valid_ref, s32[24]{0:T(128)S(1)} %get-tuple-element.102.row_ref, ...), custom_call_target="tpu_custom_call" | custom-call | tf_op jit(solution)/shard_map/mirror/pallas_call | solution.py:152
  40.2 4.3 %copy-done.1 = bf16[22,512,512]{2,1,0:T(8,128)(2,1)S(1)} copy-done((bf16[22,512,512]{2,1,0:T(8,128)(2,1)S(1)}, bf16[22,512,512]{2,1,0:T(8,128)(2,1)}, u32[]{:S(2)}) %copy-start.1) | copy-done | bytes 11534360
  44.5 4.3 %copy-done.4 = bf16[22,512,512]{2,1,0:T(8,128)(2,1)S(1)} copy-done((bf16[22,512,512]{2,1,0:T(8,128)(2,1)S(1)}, bf16[22,512,512]{2,1,0:T(8,128)(2,1)}, u32[]{:S(2)}) %copy-start.4) | copy-done | bytes 11534360
  48.8 4.6 %own.2.refs_3_ = f32[64,8192]{1,0:T(8,128)S(1)} custom-call(s32[3]{0:T(128)S(1)} %pad_add_fusion.1.place, s32[24]{0:T(128)S(1)} %get-tuple-element.103.tile_ref, s32[24]{0:T(128)S(1)} %compare_convert_fusion.valid_ref, s32[24]{0:T(128)S(1)} %get-tuple-element.102.row_ref, s32[24]{0:T(128)S(1)} %add_maximum_fusion.1.col_ref, ...), custom_call_target="tpu_custom_call" | custom-call | tf_op jit(solution)/shard_map/own/pallas_call | solution.py:180
  53.4 14.0 %collective-permute-done.5.refs_1_ = f32[64,3072]{1,0:T(8,128)} collective-permute-done((f32[64,3072]{1,0:T(8,128)}, f32[64,3072]{1,0:T(8,128)}, u32[]{:S(2)}, u32[]{:S(2)}) %collective-permute-start.5) | collective-permute-done | bytes 786464 | tf_op jit(solution)/shard_map/ppermute | solution.py:387
  67.4 9.7 %direct.2.start = f32[64,8192]{1,0:T(8,128)S(1)} custom-call(s32[3]{0:T(128)S(1)} %pad_add_fusion.1.place, s32[24]{0:T(128)S(1)} %get-tuple-element.103.tile_ref, s32[24]{0:T(128)S(1)} %compare_convert_fusion.valid_ref, s32[24]{0:T(128)S(1)} %get-tuple-element.102.row_ref, bf16[22,512,512]{2,1,0:T(8,128)(2,1)S(1)} %copy-done.2, ...), custom_call_target="tpu_custom_call" | custom-call | tf_op jit(solution)/shard_map/direct/pallas_call | solution.py:214
  77.1 8.2 %collective-permute-done.8.refs_1_ = f32[64,3072]{1,0:T(8,128)} collective-permute-done((f32[64,3072]{1,0:T(8,128)}, f32[64,3072]{1,0:T(8,128)}, u32[]{:S(2)}, u32[]{:S(2)}) %collective-permute-start.8) | collective-permute-done | bytes 786464 | tf_op jit(solution)/shard_map/ppermute | solution.py:387
  93.1 7.1 %collective-permute-done.11.arrived = f32[32,2048]{1,0:T(8,128)S(1)} collective-permute-done((f32[32,2048]{1,0:T(8,128)S(1)}, f32[32,2048]{1,0:T(8,128)S(1)}, u32[]{:S(2)}, u32[]{:S(2)}) %collective-permute-start.11) | collective-permute-done | bytes 262176 | tf_op jit(solution)/shard_map/ppermute | solution.py:387
  104.0 6.1 %collective-permute-done.12.arrived = f32[32,1024]{1,0:T(8,128)S(1)} collective-permute-done((f32[32,1024]{1,0:T(8,128)S(1)}, f32[32,1024]{1,0:T(8,128)S(1)}, u32[]{:S(2)}, u32[]{:S(2)}) %collective-permute-start.12) | collective-permute-done | bytes 131104 | tf_op jit(solution)/shard_map/ppermute | solution.py:387
  114.1 4.3 %collective-permute-done.22.across = f32[32,1024]{1,0:T(8,128)S(1)} collective-permute-done((f32[32,1024]{1,0:T(8,128)S(1)}, f32[32,1024]{1,0:T(8,128)S(1)}, u32[]{:S(2)}, u32[]{:S(2)}) %collective-permute-start.22) | collective-permute-done | bytes 131104 | tf_op jit(solution)/shard_map/ppermute | solution.py:387
  144.8 5.8 %mirror.3 = (f32[64,3072]{1,0:T(8,128)S(1)}, f32[64,3072]{1,0:T(8,128)S(1)}, f32[64,3072]{1,0:T(8,128)S(1)}) custom-call(s32[3]{0:T(128)S(1)} %pad_add_fusion.1.place, s32[24]{0:T(128)S(1)} %get-tuple-element.103.tile_ref, s32[24]{0:T(128)S(1)} %compare_convert_fusion.valid_ref, s32[24]{0:T(128)S(1)} %get-tuple-element.102.row_ref, ...), custom_call_target="tpu_custom_call" | custom-call | tf_op jit(solution)/shard_map/mirror/pallas_call | solution.py:152
  150.6 9.2 %collective-permute-done.29.refs_1_ = f32[32,3072]{1,0:T(8,128)S(1)} collective-permute-done((f32[32,3072]{1,0:T(8,128)S(1)}, f32[32,3072]{1,0:T(8,128)S(1)}, u32[]{:S(2)}, u32[]{:S(2)}) %collective-permute-start.29) | collective-permute-done | bytes 393248 | tf_op jit(solution)/shard_map/ppermute | solution.py:387
  167.7 3.7 %collective-permute-done.21 = f32[64,64]{1,0:T(8,128)S(1)} collective-permute-done((f32[64,64]{1,0:T(8,128)S(1)}, f32[64,64]{1,0:T(8,128)S(1)}, u32[]{:S(2)}, u32[]{:S(2)}) %collective-permute-start.21) | collective-permute-done | bytes 16416 | tf_op jit(solution)/shard_map/ppermute | solution.py:387
  171.4 4.8 %collective-permute-done.20 = f32[64,64]{1,0:T(8,128)S(1)} collective-permute-done((f32[64,64]{1,0:T(8,128)S(1)}, f32[64,64]{1,0:T(8,128)S(1)}, u32[]{:S(2)}, u32[]{:S(2)}) %collective-permute-start.20) | collective-permute-done | bytes 16416 | tf_op jit(solution)/shard_map/ppermute | solution.py:387
  176.2 3.9 %collective-permute-done.19 = f32[64,64]{1,0:T(8,128)S(1)} collective-permute-done((f32[64,64]{1,0:T(8,128)S(1)}, f32[64,64]{1,0:T(8,128)S(1)}, u32[]{:S(2)}, u32[]{:S(2)}) %collective-permute-start.19) | collective-permute-done | bytes 16416 | tf_op jit(solution)/shard_map/ppermute | solution.py:387
  182.1 4.5 %own.3.refs_6_ = f32[64,8192]{1,0:T(8,128)S(1)} custom-call(s32[3]{0:T(128)S(1)} %pad_add_fusion.1.place, s32[24]{0:T(128)S(1)} %get-tuple-element.103.tile_ref, s32[24]{0:T(128)S(1)} %compare_convert_fusion.valid_ref, s32[24]{0:T(128)S(1)} %get-tuple-element.102.row_ref, s32[24]{0:T(128)S(1)} %add_maximum_fusion.1.col_ref, ...), custom_call_target="tpu_custom_call" | custom-call | tf_op jit(solution)/shard_map/own/pallas_call | solution.py:180
  186.7 6.9 %cholesky.2 = (f32[64,64]{1,0:T(8,128)}, f32[64,64]{1,0:T(8,128)S(1)}) custom-call(f32[64,64]{1,0:T(8,128)S(1)} %add_add_fusion.2.refs_3_.gram), custom_call_target="tpu_custom_call" | custom-call | tf_op jit(solution)/shard_map/cholesky/pallas_call | solution.py:352
  193.5 21.4 %collective-permute-done.32.refs_4_ = f32[32,3072]{1,0:T(8,128)S(1)} collective-permute-done((f32[32,3072]{1,0:T(8,128)S(1)}, f32[32,3072]{1,0:T(8,128)S(1)}, u32[]{:S(2)}, u32[]{:S(2)}) %collective-permute-start.32) | collective-permute-done | bytes 393248 | tf_op jit(solution)/shard_map/ppermute | solution.py:387
  214.9 8.9 %direct.3.start = f32[64,8192]{1,0:T(8,128)S(1)} custom-call(s32[3]{0:T(128)S(1)} %pad_add_fusion.1.place, s32[24]{0:T(128)S(1)} %get-tuple-element.103.tile_ref, s32[24]{0:T(128)S(1)} %compare_convert_fusion.valid_ref, s32[24]{0:T(128)S(1)} %get-tuple-element.102.row_ref, bf16[22,512,512]{2,1,0:T(8,128)(2,1)S(1)} %copy-done.2, ...), custom_call_target="tpu_custom_call" | custom-call | tf_op jit(solution)/shard_map/direct/pallas_call | solution.py:214
  231.3 7.0 %collective-permute-done.38.arrived = f32[32,2048]{1,0:T(8,128)S(1)} collective-permute-done((f32[32,2048]{1,0:T(8,128)S(1)}, f32[32,2048]{1,0:T(8,128)S(1)}, u32[]{:S(2)}, u32[]{:S(2)}) %collective-permute-start.38) | collective-permute-done | bytes 262176 | tf_op jit(solution)/shard_map/ppermute | solution.py:387
  262.2 6.2 %collective-permute-done.49.across = f32[64,1024]{1,0:T(8,128)S(1)} collective-permute-done((f32[64,1024]{1,0:T(8,128)S(1)}, f32[64,1024]{1,0:T(8,128)S(1)}, u32[]{:S(2)}, u32[]{:S(2)}) %collective-permute-start.49) | collective-permute-done | bytes 262176 | tf_op jit(solution)/shard_map/ppermute | solution.py:387
  268.4 4.9 %collective-permute-start.50 = (f32[64,2048]{1,0:T(8,128)S(1)}, f32[64,2048]{1,0:T(8,128)S(1)}, u32[]{:S(2)}, u32[]{:S(2)}) collective-permute-start(f32[64,2048]{1,0:T(8,128)S(1)} %pad_maximum_fusion), channel_id=1, source_target_pairs={{0,1},{1,0},{2,3},{3,2},{4,5},{5,4},{6,7},{7,6},{8,9},{9,8},{10,11... | collective-permute-start | bytes 1572872 | tf_op jit(solution)/shard_map/ppermute | solution.py:387
  280.1 6.3 %cholesky.3 = (f32[64,64]{1,0:T(8,128)S(1)}, f32[64,64]{1,0:T(8,128)S(1)}) custom-call(f32[64,64]{1,0:T(8,128)S(1)} %add_add_fusion.gram), custom_call_target="tpu_custom_call" | custom-call | tf_op jit(solution)/shard_map/cholesky/pallas_call | solution.py:352
  (156 shorter events, 116.6 us)
Async XLA Ops:
  0.6 12.1 %collective-permute-start.3 = (f32[64,4096]{1,0:T(8,128)}, f32[64,4096]{1,0:T(8,128)S(1)}, u32[]{:S(2)}, u32[]{:S(2)}) collective-permute-start(f32[64,4096]{1,0:T(8,128)} %bitcast.21), channel_id=1, source_target_pairs={{0,4},{4,0},{8,12},{12,8},{16,20},{20,16},{24,28},{28,24},{1,5},{5... | collective-permute-start | bytes 3145736 | tf_op jit(solution)/shard_map/ppermute | solution.py:387
  15.9 21.8 %collective-permute-start.4 = (f32[64,3072]{1,0:T(8,128)S(1)}, f32[64,3072]{1,0:T(8,128)S(1)}, u32[]{:S(2)}, u32[]{:S(2)}) collective-permute-start(f32[64,3072]{1,0:T(8,128)S(1)} %get-tuple-element.53), channel_id=1, source_target_pairs={{0,8},{4,12},{8,0},{12,4},{16,24},{20,28},{24,16},{28,20},{1,9},{5... | collective-permute-start | bytes 2359304 | tf_op jit(solution)/shard_map/ppermute | solution.py:387
  16.4 50.9 %collective-permute-start.5 = (f32[64,3072]{1,0:T(8,128)}, f32[64,3072]{1,0:T(8,128)}, u32[]{:S(2)}, u32[]{:S(2)}) collective-permute-start(f32[64,3072]{1,0:T(8,128)} %get-tuple-element.54), channel_id=1, source_target_pairs={{0,16},{4,20},{8,24},{12,28},{16,0},{20,4},{24,8},{28,12},{1,17},{... | collective-permute-start | bytes 2359304 | tf_op jit(solution)/shard_map/ppermute | solution.py:387
  16.5 50.9 %collective-permute-start.6 = (f32[64,3072]{1,0:T(8,128)}, f32[64,3072]{1,0:T(8,128)}, u32[]{:S(2)}, u32[]{:S(2)}) collective-permute-start(f32[64,3072]{1,0:T(8,128)} %get-tuple-element.55), channel_id=1, source_target_pairs={{0,24},{4,28},{8,16},{12,20},{16,8},{20,12},{24,0},{28,4},{1,25},{... | collective-permute-start | bytes 2359304 | tf_op jit(solution)/shard_map/ppermute | solution.py:387
  35.7 49.6 %collective-permute-start.8 = (f32[64,3072]{1,0:T(8,128)}, f32[64,3072]{1,0:T(8,128)}, u32[]{:S(2)}, u32[]{:S(2)}) collective-permute-start(f32[64,3072]{1,0:T(8,128)} %get-tuple-element.57), channel_id=1, source_target_pairs={{0,16},{4,20},{8,24},{12,28},{16,0},{20,4},{24,8},{28,12},{1,17},{... | collective-permute-start | bytes 2359304 | tf_op jit(solution)/shard_map/ppermute | solution.py:387
  36.2 49.1 %collective-permute-start.9 = (f32[64,3072]{1,0:T(8,128)}, f32[64,3072]{1,0:T(8,128)}, u32[]{:S(2)}, u32[]{:S(2)}) collective-permute-start(f32[64,3072]{1,0:T(8,128)} %get-tuple-element.58), channel_id=1, source_target_pairs={{0,24},{4,28},{8,16},{12,20},{16,8},{20,12},{24,0},{28,4},{1,25},{... | collective-permute-start | bytes 2359304 | tf_op jit(solution)/shard_map/ppermute | solution.py:387
  38.6 46.7 %collective-permute-start.7 = (f32[64,3072]{1,0:T(8,128)S(1)}, f32[64,3072]{1,0:T(8,128)}, u32[]{:S(2)}, u32[]{:S(2)}) collective-permute-start(f32[64,3072]{1,0:T(8,128)S(1)} %get-tuple-element.56.refs_1_), channel_id=1, source_target_pairs={{0,8},{4,12},{8,0},{12,4},{16,24},{20,28},{24,16},{28,20},{1,9},{5... | collective-permute-start | bytes 2359304 | tf_op jit(solution)/shard_map/ppermute | solution.py:387
  92.7 18.8 %collective-permute-start.13 = (f32[32,2048]{1,0:T(8,128)S(1)}, f32[32,2048]{1,0:T(8,128)S(1)}, u32[]{:S(2)}, u32[]{:S(2)}) collective-permute-start(f32[32,2048]{1,0:T(8,128)S(1)} %get-tuple-element.66), channel_id=1, source_target_pairs={{0,1},{1,0},{2,3},{3,2},{4,5},{5,4},{6,7},{7,6},{8,9},{9,8},{10,11... | collective-permute-start | bytes 786440 | tf_op jit(solution)/shard_map/ppermute | solution.py:387
  100.3 9.8 %collective-permute-start.12 = (f32[32,1024]{1,0:T(8,128)S(1)}, f32[32,1024]{1,0:T(8,128)S(1)}, u32[]{:S(2)}, u32[]{:S(2)}) collective-permute-start(f32[32,1024]{1,0:T(8,128)S(1)} %get-tuple-element.64), channel_id=1, source_target_pairs={{0,3},{1,2},{2,1},{3,0},{4,7},{5,6},{6,5},{7,4},{8,11},{9,10},{10,... | collective-permute-start | bytes 393224 | tf_op jit(solution)/shard_map/ppermute | solution.py:387
  111.6 9.6 %collective-permute-start.14 = (f32[32,1024]{1,0:T(8,128)S(1)}, f32[32,1024]{1,0:T(8,128)S(1)}, u32[]{:S(2)}, u32[]{:S(2)}) collective-permute-start(f32[32,1024]{1,0:T(8,128)S(1)} %get-tuple-element.68), channel_id=1, source_target_pairs={{0,3},{1,2},{2,1},{3,0},{4,7},{5,6},{6,5},{7,4},{8,11},{9,10},{10,... | collective-permute-start | bytes 393224 | tf_op jit(solution)/shard_map/ppermute | solution.py:387
  127.1 11.4 %collective-permute-start.24 = (f32[32,4096]{1,0:T(8,128)S(1)}, f32[32,4096]{1,0:T(8,128)S(1)}, u32[]{:S(2)}, u32[]{:S(2)}) collective-permute-start(f32[32,4096]{1,0:T(8,128)S(1)} %join.3.own), channel_id=1, source_target_pairs={{0,4},{4,0},{8,12},{12,8},{16,20},{20,16},{24,28},{28,24},{1,5},{5... | collective-permute-start | bytes 1572872 | tf_op jit(solution)/shard_map/ppermute | solution.py:387
  129.3 10.0 %collective-permute-start.26 = (f32[32,2048]{1,0:T(8,128)S(1)}, f32[32,2048]{1,0:T(8,128)S(1)}, u32[]{:S(2)}, u32[]{:S(2)}) collective-permute-start(f32[32,2048]{1,0:T(8,128)S(1)} %pad_maximum_fusion.2), channel_id=1, source_target_pairs={{0,1},{1,0},{2,3},{3,2},{4,5},{5,4},{6,7},{7,6},{8,9},{9,8},{10,11... | collective-permute-start | bytes 786440 | tf_op jit(solution)/shard_map/ppermute | solution.py:387
  139.9 20.0 %collective-permute-start.29 = (f32[32,3072]{1,0:T(8,128)S(1)}, f32[32,3072]{1,0:T(8,128)S(1)}, u32[]{:S(2)}, u32[]{:S(2)}) collective-permute-start(f32[32,3072]{1,0:T(8,128)S(1)} %get-tuple-element.75), channel_id=1, source_target_pairs={{0,16},{4,20},{8,24},{12,28},{16,0},{20,4},{24,8},{28,12},{1,17},{... | collective-permute-start | bytes 1179656 | tf_op jit(solution)/shard_map/ppermute | solution.py:387
  140.4 19.5 %collective-permute-start.30 = (f32[32,3072]{1,0:T(8,128)S(1)}, f32[32,3072]{1,0:T(8,128)S(1)}, u32[]{:S(2)}, u32[]{:S(2)}) collective-permute-start(f32[32,3072]{1,0:T(8,128)S(1)} %get-tuple-element.76), channel_id=1, source_target_pairs={{0,24},{4,28},{8,16},{12,20},{16,8},{20,12},{24,0},{28,4},{1,25},{... | collective-permute-start | bytes 1179656 | tf_op jit(solution)/shard_map/ppermute | solution.py:387
  142.0 19.9 %collective-permute-start.28 = (f32[32,3072]{1,0:T(8,128)S(1)}, f32[32,3072]{1,0:T(8,128)S(1)}, u32[]{:S(2)}, u32[]{:S(2)}) collective-permute-start(f32[32,3072]{1,0:T(8,128)S(1)} %get-tuple-element.70.refs_0_), channel_id=1, source_target_pairs={{0,8},{4,12},{8,0},{12,4},{16,24},{20,28},{24,16},{28,20},{1,9},{5... | collective-permute-start | bytes 1179656 | tf_op jit(solution)/shard_map/ppermute | solution.py:387
  144.2 36.2 %collective-permute-start.31 = (f32[32,3072]{1,0:T(8,128)S(1)}, f32[32,3072]{1,0:T(8,128)S(1)}, u32[]{:S(2)}, u32[]{:S(2)}) collective-permute-start(f32[32,3072]{1,0:T(8,128)S(1)} %get-tuple-element.77), channel_id=1, source_target_pairs={{0,8},{4,12},{8,0},{12,4},{16,24},{20,28},{24,16},{28,20},{1,9},{5... | collective-permute-start | bytes 1179656 | tf_op jit(solution)/shard_map/ppermute | solution.py:387
  161.9 61.9 %collective-permute-start.34 = (f32[64,3072]{1,0:T(8,128)S(1)}, f32[64,3072]{1,0:T(8,128)S(1)}, u32[]{:S(2)}, u32[]{:S(2)}) collective-permute-start(f32[64,3072]{1,0:T(8,128)S(1)} %get-tuple-element.80.refs_2_), channel_id=1, source_target_pairs={{0,8},{4,12},{8,0},{12,4},{16,24},{20,28},{24,16},{28,20},{1,9},{5... | collective-permute-start | bytes 2359304 | tf_op jit(solution)/shard_map/ppermute | solution.py:387
  162.4 61.4 %collective-permute-start.36 = (f32[64,3072]{1,0:T(8,128)S(1)}, f32[64,3072]{1,0:T(8,128)S(1)}, u32[]{:S(2)}, u32[]{:S(2)}) collective-permute-start(f32[64,3072]{1,0:T(8,128)S(1)} %get-tuple-element.84), channel_id=1, source_target_pairs={{0,24},{4,28},{8,16},{12,20},{16,8},{20,12},{24,0},{28,4},{1,25},{... | collective-permute-start | bytes 2359304 | tf_op jit(solution)/shard_map/ppermute | solution.py:387
  163.7 60.1 %collective-permute-start.35 = (f32[64,3072]{1,0:T(8,128)S(1)}, f32[64,3072]{1,0:T(8,128)S(1)}, u32[]{:S(2)}, u32[]{:S(2)}) collective-permute-start(f32[64,3072]{1,0:T(8,128)S(1)} %get-tuple-element.82), channel_id=1, source_target_pairs={{0,16},{4,20},{8,24},{12,28},{16,0},{20,4},{24,8},{28,12},{1,17},{... | collective-permute-start | bytes 2359304 | tf_op jit(solution)/shard_map/ppermute | solution.py:387
  180.1 34.8 %collective-permute-start.32 = (f32[32,3072]{1,0:T(8,128)S(1)}, f32[32,3072]{1,0:T(8,128)S(1)}, u32[]{:S(2)}, u32[]{:S(2)}) collective-permute-start(f32[32,3072]{1,0:T(8,128)S(1)} %get-tuple-element.78), channel_id=1, source_target_pairs={{0,16},{4,20},{8,24},{12,28},{16,0},{20,4},{24,8},{28,12},{1,17},{... | collective-permute-start | bytes 1179656 | tf_op jit(solution)/shard_map/ppermute | solution.py:387
  180.4 34.5 %collective-permute-start.33 = (f32[32,3072]{1,0:T(8,128)S(1)}, f32[32,3072]{1,0:T(8,128)S(1)}, u32[]{:S(2)}, u32[]{:S(2)}) collective-permute-start(f32[32,3072]{1,0:T(8,128)S(1)} %get-tuple-element.79), channel_id=1, source_target_pairs={{0,24},{4,28},{8,16},{12,20},{16,8},{20,12},{24,0},{28,4},{1,25},{... | collective-permute-start | bytes 1179656 | tf_op jit(solution)/shard_map/ppermute | solution.py:387
  228.7 9.6 %collective-permute-start.38 = (f32[32,2048]{1,0:T(8,128)S(1)}, f32[32,2048]{1,0:T(8,128)S(1)}, u32[]{:S(2)}, u32[]{:S(2)}) collective-permute-start(f32[32,2048]{1,0:T(8,128)S(1)} %get-tuple-element.88), channel_id=1, source_target_pairs={{0,1},{1,0},{2,3},{3,2},{4,5},{5,4},{6,7},{7,6},{8,9},{9,8},{10,11... | collective-permute-start | bytes 786440 | tf_op jit(solution)/shard_map/ppermute | solution.py:387
  231.2 12.3 %collective-permute-start.40 = (f32[32,2048]{1,0:T(8,128)S(1)}, f32[32,2048]{1,0:T(8,128)S(1)}, u32[]{:S(2)}, u32[]{:S(2)}) collective-permute-start(f32[32,2048]{1,0:T(8,128)S(1)} %get-tuple-element.92), channel_id=1, source_target_pairs={{0,1},{1,0},{2,3},{3,2},{4,5},{5,4},{6,7},{7,6},{8,9},{9,8},{10,11... | collective-permute-start | bytes 786440 | tf_op jit(solution)/shard_map/ppermute | solution.py:387
  268.4 18.7 %collective-permute-start.50 = (f32[64,2048]{1,0:T(8,128)S(1)}, f32[64,2048]{1,0:T(8,128)S(1)}, u32[]{:S(2)}, u32[]{:S(2)}) collective-permute-start(f32[64,2048]{1,0:T(8,128)S(1)} %pad_maximum_fusion), channel_id=1, source_target_pairs={{0,1},{1,0},{2,3},{3,2},{4,5},{5,4},{6,7},{7,6},{8,9},{9,8},{10,11... | collective-permute-start | bytes 1572872 | tf_op jit(solution)/shard_map/ppermute | solution.py:387
  (36 other events, 219.0 us)

commit v3 on v2

--- a/solution.py
+++ b/solution.py
@@ -86,29 +86,38 @@
     return both[:width] + (both[width:] + rest)
 
 
-def serve_kernel(chips, group, bs, place, wanted, own, sibling, *refs):
-    pair, outs = refs[-chips], refs[1 - chips :]
+def serve_kernel(chips, group, bs, rows, place, wanted, own, sibling, *refs):
+    pair, outs = refs[-chips - 1], refs[-chips:-1]
     core = place[1]
-    rows = own.shape[1]
-    pair[:, block(core, rows)] = own[...]
-    pair[:, block(1 - core, rows)] = sibling[...]
+    pair[:, block(core, rows)] = own[:, :rows]
+    pair[:, block(1 - core, rows)] = sibling[:, :rows]
+    rider = own.shape[1] - rows
+    if rider:
+        refs[-1][...] = own[:, rows:] + sibling[:, rows:]
+    else:
+        refs[-1][...] = jnp.zeros_like(refs[-1])
     for k in range(1, chips):
         for i in range(group):
             slot = (place[0] ^ k) * group + i
             outs[k - 1][:, i * bs : (i + 1) * bs] = pair[:, block(wanted[slot], bs)]
-
-
-def serve(place, wanted, own, sibling, chips, group, bs, after=()):
-    width, rows = own.shape
+        if rider:
+            outs[k - 1][:, group * bs :] = refs[-1][...]
+
+
+def serve(place, wanted, own, sibling, rows, chips, group, bs, after=()):
+    width = own.shape[0]
+    rider = own.shape[1] - rows
     outs = pl.pallas_call(
-        functools.partial(serve_kernel, chips, group, bs),
+        functools.partial(serve_kernel, chips, group, bs, rows),
         in_specs=[SMEM, SMEM, VMEM, VMEM] + [ANY] * len(after),
-        out_specs=[VMEM] * chips,
-        out_shape=[shape(width, 2 * rows)] + [shape(width, group * bs)] * (chips - 1),
-        compiler_params=params(6),
+        out_specs=[VMEM] * (chips + 1),
+        out_shape=[shape(width, 2 * rows)]
+        + [shape(width, group * bs + rider)] * (chips - 1)
+        + [shape(width, 128)],
+        compiler_params=params(16),
         name="serve",
     )(place, wanted, own, sibling, *after)
-    return outs[0], outs[1:]
+    return outs[0], outs[1:-1], outs[-1]
 
 
 def panel_block(pieces, at):
@@ -130,7 +139,7 @@
 
 def mirror_kernel(chips, group, parts, place, tile_ref, valid_ref, row_ref, high, low, *refs):
     pairs = refs[:parts]
-    outs = refs[1 - chips :]
+    outs = refs[-HALVES * (chips - 1) :]
     bs = high.shape[1]
     base = place[1] * (pairs[0].shape[1] // (2 * bs))
 
@@ -140,7 +149,10 @@
         for k in range(1, chips):
             @pl.when(slot // group == place[0] ^ k)
             def _():
-                outs[k - 1][:, block(slot % group, bs)] = value
+                half = value.shape[0] // HALVES
+                for h in range(HALVES):
+                    out = outs[h * (chips - 1) + k - 1]
+                    out[:, block(slot % group, bs)] = value[h * half : (h + 1) * half]
 
     visit_tiles(range(1, chips), group, place, tile_ref, valid_ref, [high, low], body)
 
@@ -149,14 +161,15 @@
     half = pairs[0].shape[0]
     bs = tiles[0].shape[1]
     parts = len(pairs)
-    return pl.pallas_call(
+    outs = pl.pallas_call(
         functools.partial(mirror_kernel, chips, group, parts),
         in_specs=[SMEM] * 4 + [VMEM] * 2 + [VMEM] * parts + [ANY] * len(after),
-        out_specs=[VMEM] * (chips - 1),
-        out_shape=[shape(half * parts, group * bs)] * (chips - 1),
+        out_specs=[VMEM] * (HALVES * (chips - 1)),
+        out_shape=[shape(half * parts // HALVES, group * bs)] * (HALVES * (chips - 1)),
         compiler_params=params(6),
         name="mirror",
     )(place, *tables[:3], *tiles, *pairs, *after)
+    return [outs[h * (chips - 1) : (h + 1) * (chips - 1)] for h in range(HALVES)]
 
 
 def own_kernel(group, parts, place, tile_ref, valid_ref, row_ref, col_ref, high, low, *refs):
@@ -222,10 +235,11 @@
     )(place, *tables[:3], *tiles, *arrived, start, *after)
 
 
-def gather_kernel(chips, group, bs, place, wanted, flag, start, *refs):
+def gather_kernel(chips, group, bs, h, place, wanted, flag, start, *refs):
     returned = refs[: chips - 1]
     own, sibling, total = refs[-3:]
-    total[...] = start[...]
+    half = total.shape[0]
+    total[...] = start[h * half : (h + 1) * half]
     for k in range(1, chips):
         first = (place[0] ^ k) * group
 
@@ -242,39 +256,37 @@
     sibling[...] = total[:, block(1 - place[1], rows)]
 
 
-def gather(place, wanted, flag, start, returned, chips, group, bs, after=()):
-    width, rows = start.shape
-    return pl.pallas_call(
-        functools.partial(gather_kernel, chips, group, bs),
+def gather(place, wanted, flag, start, returned, chips, group, bs, h, after=()):
+    half, rows = returned[0].shape[0], start.shape[1]
+    return pl.pallas_call(
+        functools.partial(gather_kernel, chips, group, bs, h),
         in_specs=[SMEM] * 3 + [VMEM] * chips + [ANY] * len(after),
         out_specs=[VMEM] * 2,
-        out_shape=[shape(width, rows // 2)] * 2,
-        scratch_shapes=[pltpu.VMEM((width, rows), F32)],
-        compiler_params=params(6),
+        out_shape=[shape(half, rows // 2)] * 2,
+        scratch_shapes=[pltpu.VMEM((half, rows), F32)],
+        compiler_params=params(16),
         name="gather",
     )(place, wanted, flag, start, *returned, *after)
 
 
-def deal_kernel(place, own, other, *outs):
-    half, quarter = outs[0].shape[0], outs[0].shape[1] // 2
-    for n, out in enumerate(outs):
-        rows = slice(n // 2 * half, (n // 2 + 1) * half)
-        for at, j in enumerate(((0, 3), (1, 2))[n % 2]):
+def deal_kernel(place, own, other, kept, sent):
+    quarter = kept.shape[1] // 2
+    for out, pair in ((kept, (0, 3)), (sent, (1, 2))):
+        for at, j in enumerate(pair):
             source = block(place[2] ^ j, quarter)
-            out[:, at * quarter : (at + 1) * quarter] = own[rows, source] + other[rows, source]
-
-
-def deal(place, own, other, n_by, parts):
-    width, rows = own.shape
-    outs = pl.pallas_call(
+            out[:, at * quarter : (at + 1) * quarter] = own[:, source] + other[:, source]
+
+
+def deal(place, own, other):
+    half, rows = own.shape
+    return pl.pallas_call(
         deal_kernel,
         in_specs=[SMEM, VMEM, VMEM],
-        out_specs=[VMEM] * (parts * 2),
-        out_shape=[shape(width // parts, rows // 2)] * (parts * 2),
+        out_specs=[VMEM] * 2,
+        out_shape=[shape(half, rows // 2)] * 2,
         compiler_params=params(6),
         name="deal",
     )(place, own, other)
-    return [outs[h * 2 : (h + 1) * 2] for h in range(parts)]
 
 
 def add_kernel(kept, arrived, mine, other):
@@ -310,25 +322,55 @@
     )(mine, arrived, *after)
 
 
+def pack_kernel(segments, *refs):
+    out = refs[-1]
+    at = 0
+    for terms in segments:
+        values = [refs[n][:, low:high] for n, low, high in terms]
+        width = values[0].shape[1]
+        out[:, at : at + width] = sum(values[1:], values[0])
+        at += width
+
+
+def pack(*segments):
+    arrays, spec = [], []
+    for terms in segments:
+        spec.append([(len(arrays) + n, low, high) for n, (_, low, high) in enumerate(terms)])
+        arrays += [x for x, _, _ in terms]
+    widths = [high - low for (_, low, high), *_ in spec]
+    return pl.pallas_call(
+        functools.partial(pack_kernel, spec),
+        in_specs=[VMEM] * len(arrays),
+        out_specs=VMEM,
+        out_shape=shape(arrays[0].shape[0], sum(widths)),
+        compiler_params=params(6),
+        name="pack",
+    )(*arrays)
+
+
 def join_kernel(place, mine, across, nearby, *refs):
     out = refs[-1]
     quarter = mine.shape[1]
     out[:, block(place[2], quarter)] = mine[...]
-    out[:, block(place[2] ^ 3, quarter)] = across[...]
+    out[:, block(place[2] ^ 3, quarter)] = across[:, :quarter]
     out[:, block(place[2] ^ 1, quarter)] = nearby[:, :quarter]
-    out[:, block(place[2] ^ 2, quarter)] = nearby[:, quarter:]
-
-
-def join(place, mine, across, nearby, after=()):
+    out[:, block(place[2] ^ 2, quarter)] = nearby[:, quarter : 2 * quarter]
+    if out.shape[1] > 4 * quarter:
+        out[:, 4 * quarter :] = refs[0][...]
+
+
+def join(place, mine, across, nearby, rider=None, after=()):
     half, quarter = mine.shape
+    riders = [] if rider is None else [rider]
+    behind = 0 if rider is None else rider.shape[1]
     return pl.pallas_call(
         join_kernel,
-        in_specs=[SMEM] + [VMEM] * 3 + [ANY] * len(after),
+        in_specs=[SMEM] + [VMEM] * (3 + len(riders)) + [ANY] * len(after),
         out_specs=VMEM,
-        out_shape=shape(half, quarter * 4),
+        out_shape=shape(half, quarter * 4 + behind),
         compiler_params=params(6),
         name="join",
-    )(place, mine, across, nearby, *after)
+    )(place, mine, across, nearby, *riders, *after)
 
 
 def cholesky_kernel(gram, factor_t, inverse):
@@ -355,19 +397,21 @@
     return factor_t.T, inverse
 
 
-def final_kernel(inverse, panel, out):
-    out[...] = jnp.dot(inverse[...], panel[...], precision=HIGHEST, preferred_element_type=F32)
-
-
-def final(inverse, panel):
+def final_kernel(inverse, *refs):
+    out = refs[-1]
+    panel = jnp.concatenate([ref[...] for ref in refs[:-1]], axis=0)
+    out[...] = jnp.dot(inverse[...], panel, precision=HIGHEST, preferred_element_type=F32)
+
+
+def final(inverse, pieces):
     return pl.pallas_call(
         final_kernel,
-        in_specs=[VMEM] * 2,
+        in_specs=[VMEM] * (1 + len(pieces)),
         out_specs=VMEM,
-        out_shape=shape(*panel.shape),
+        out_shape=shape(inverse.shape[0], pieces[0].shape[1]),
         compiler_params=params(16),
         name="final",
-    )(inverse, panel)
+    )(inverse, *pieces)
 
 
 def local(tiles, tile_rows, tile_cols, start_panel):
@@ -410,8 +454,6 @@
     flag = (incoming > 0).astype(i32)
     wanted = jnp.maximum(incoming - 1, 0)
 
-    halves = range(HALVES)
-
     def gate(x, *deps):
         return lax.optimization_barrier((x, *deps))[0] if deps else x
 
@@ -434,57 +476,78 @@
         return gram
 
     def serve_half(own, sibling, after=()):
-        return serve(place, wanted, own, sibling, chips, group, bs, after)
-
-    def reduce_halves(start, returned, after=()):
-        own, other = gather(place, wanted, flag, start, returned, chips, group, bs)
-        dealt = deal(place, own, swap_core(other), n_by, HALVES)
-        crossing = [add_pair(kept, swap(sent, "by", 1)) for kept, sent in dealt]
-        quarters = []
-        for mine, other in crossing:
-            quarters.append(total(mine, swap(other, "by", 3), after))
-            after = [quarters[-1]]
-        return quarters
-
-    def spread(quarter):
-        across = swap(quarter, "by", 3)
-        nearby = swap(jnp.concatenate([quarter, across], axis=1), "by", 1)
-        return quarter, across, nearby
+        return serve(place, wanted, own, sibling, rows, chips, group, bs, after)
+
+    def reduce_half(h, start, returned, after=(), deps=()):
+        own, other = gather(place, wanted, flag, start, returned, chips, group, bs, h, after)
+        kept, sent = deal(place, own, swap_core(other))
+        arrived = swap(gate(sent, *deps), "by", 1)
+        mine, other = add_pair(kept, arrived)
+        return kept, arrived, mine, swap(other, "by", 3)
+
+    def fold(gram):
+        return jnp.concatenate([gram[: width // 2], gram[width // 2 :]], axis=1)
+
+    def unfold(gram):
+        return jnp.concatenate([gram[:, :width], gram[:, width:]], axis=0)
+
+    def tree(level):
+        while len(level) > 1:
+            level = [level[i] + level[i + 1] for i in range(0, len(level), 2)]
+        return level[0]
 
     by_all, core_pair = list(range(n_by)), [0, 1]
+    quart = rows // n_by
     panel_t = start_panel.T
-    pair, served = serve_half(panel_t, swap_core(panel_t))
+    pair, served, _ = serve_half(panel_t, swap_core(panel_t))
     received = [swap_chips(served)]
-    tiles = load(tiles, [pair])
+    tiles = load(tiles, [pair, flag, wanted, *tables])
     mirrored = mirror(place, tables, tiles, [pair], chips, group)
-    start = own(place, tables, tiles, [pair], group, [mirrored[0]])
+    start = own(place, tables, tiles, [pair], group, [mirrored[0][0]])
     start = direct(place, tables, tiles, start, received, chips, group)
-    quarters = reduce_halves(start, swap_chips(mirrored))
-    spreads = [spread(quarter) for quarter in quarters]
-    gram = all_sum(gram_of(quarters), "wide", core_pair)
-    pairs, served, last = [], [], [quarters[-1]]
-    for h in halves:
-        piece = join(place, *spreads[h], last)
-        pair, out = serve_half(piece, swap_core(piece), [gram])
-        pairs.append(pair)
-        served.append(out)
-        if h == 0:
-            gram = gram_chips(gram)
-            last = [out[0], gram]
-    received = [swap_chips(out) for out in served]
+    returned = [swap_chips(x) for x in mirrored]
+    kept, first, mine, last = reduce_half(0, start, returned[0])
+    _, _, mine_1, last_1 = reduce_half(1, start, returned[1], [first], [first])
+    quarters = [total(mine, last)]
+    quarters.append(total(mine_1, last_1, [quarters[0]]))
+    every, behind = (0, quart), (quart, quart + 2 * width)
+    across = swap(quarters[0], "by", 3)
+    nearby = swap(pack([(quarters[0], *every)], [(across, *every)]), "by", 1)
+    piece = join(place, quarters[0], across, nearby)
+    pair, served, _ = serve_half(piece, swap_core(piece))
+    pairs, received = [pair], [swap_chips(served)]
+    rider = fold(gram_of(quarters))
+    across = swap(pack([(quarters[1], *every)], [(rider, 0, 2 * width)]), "by", 3)
+    sums = [(rider, 0, 2 * width), (across, *behind)]
+    nearby = swap(pack([(quarters[1], *every)], [(across, *every)], sums), "by", 1)
+    rider = pack(sums + [(nearby, 2 * quart, 2 * quart + 2 * width)])
+    piece = join(place, quarters[1], across, nearby, rider, [piece])
+    pair, served, rider = serve_half(piece, swap_core(piece), [pairs[0]])
+    pairs.append(pair)
+    received.append(swap_chips(served))
+    gram = unfold(tree([rider] + [x[:, group * bs :] for x in received[1]]))
     mirrored = mirror(place, tables, tiles, pairs, chips, group)
-    returned = swap_chips([gate(x, *received[0]) for x in mirrored])
-    gram = all_sum(gram, "by", by_all)
-    start = own(place, tables, tiles, pairs, group, [mirrored[0], gram])
-    factor, inverse = cholesky(gate(gram, start))
-    start = direct(place, tables, tiles, start, received, chips, group, [inverse])
-    quarters = reduce_halves(start, returned)
-    quarter = jnp.dot(inverse, jnp.concatenate(quarters, axis=0), precision=HIGHEST)
-    gram = all_sum(gram_of([quarter]), "by", by_all)
-    normal = join(place, *spread(gate(quarter, gram)))
-    gram = gram_chips(all_sum(gram, "wide", core_pair))
-    factor, inverse = cholesky(gram)
-    out = final(inverse, normal)
+    returned = [swap_chips([gate(x, received[1][0]) for x in mirrored[0]])]
+    returned.append(swap_chips([gate(x, received[1][-1]) for x in mirrored[1]]))
+    start = own(place, tables, tiles, pairs, group, [mirrored[0][0]])
+    start = direct(place, tables, tiles, start, received, chips, group)
+    kept, first, mine, last = reduce_half(0, start, returned[0])
+    factor, inverse = cholesky(gate(gram, kept))
+    _, _, mine_1, last_1 = reduce_half(1, start, returned[1], [inverse, first], [first])
+    quarters = [total(mine, last)]
+    across = swap(quarters[0], "by", 3)
+    quarters.append(total(mine_1, last_1, [quarters[0]]))
+    whole = jnp.concatenate(quarters, axis=0)
+    gram_0 = gram_of([jnp.dot(inverse, whole, precision=HIGHEST)])
+    gram_1 = all_sum(gram_0, "by", by_all)
+    gram_2 = all_sum(gram_1, "wide", core_pair)
+    nearby = swap(pack([(quarters[0], *every)], [(gate(across, gram_0), *every)]), "by", 1)
+    pieces = [join(place, quarters[0], across, nearby)]
+    across = swap(gate(quarters[1], gram_0), "by", 3)
+    nearby = swap(pack([(quarters[1], *every)], [(gate(across, gram_1), *every)]), "by", 1)
+    pieces.append(join(place, quarters[1], across, nearby))
+    factor, inverse_2 = cholesky(gram_chips(gram_2))
+    out = final(jnp.dot(inverse_2, inverse, precision=HIGHEST), pieces)
     return (out.T, factor)
 
 

time: 290 us -> 277 us (0.955)
  waiting for transfers between devices: 133 us -> 110 us
  starting transfers between devices: 64.4 us -> 82.6 us
  local copies, waits for them, and re-layouts: 13 us -> 3.39 us
    ppermute x51 -> x54, waiting for transfers between devices: 133 us -> 110 us  [swap(): return lax.ppermute(x, axis, [(i, i ^ k) for i in range(size)])]
    ppermute x51 -> x54, starting transfers between devices: 64.4 us -> 82.6 us  [swap(): return lax.ppermute(x, axis, [(i, i ^ k) for i in range(size)])]
    unnamed x19 -> x3, local copies, waits for them, and re-layouts: 11.6 us -> 1.94 us
    pallas_call x9 -> x18, Pallas kernels: 10.9 us -> 12.9 us  [the longest x4 4.52 us: gather(): pl.pallas_call(functools.partial(gather_kernel, chips, group, bs, h), in_...]
  transfers between devices with their start and end apart: 51 -> 54, of which waited for: 34 -> 26; matrix products, arithmetic and copies ran while one was open for 1% -> 1% of each run, Pallas kernels for 22% -> 23%
where the time goes in v3:
time: 277 us
  waiting for transfers between devices  110 us (40%)
  starting transfers between devices  82.6 us (30%)
  Pallas kernels  76.3 us (28%)
  local copies, waits for them, and re-layouts  3.39 us (1%)
    ppermute x54, waiting for transfers between devices, swap(): return lax.ppermute(x, axis, [(i, i ^ k) for i in range(size)])  110 us
    ppermute x54, starting transfers between devices, swap(): return lax.ppermute(x, axis, [(i, i ^ k) for i in range(size)])  82.6 us
    pallas_call x2, Pallas kernels, direct(): pl.pallas_call(functools.partial(direct_kernel, chips, group, parts), in_...  18.6 us
    pallas_call x2, Pallas kernels, cholesky(): pl.pallas_call(cholesky_kernel, out_shape=[shape(n, n)] * 2, compiler_par...  13.2 us
    pallas_call x2, Pallas kernels, mirror(): pl.pallas_call(functools.partial(mirror_kernel, chips, group, parts), in_...  11.8 us
    pallas_call x2, Pallas kernels, own(): pl.pallas_call(functools.partial(own_kernel, group, parts), in_specs=[SME...  9.08 us
    pallas_call x1, Pallas kernels, load(): pl.pallas_call(load_kernel, in_specs=[ANY] * (1 + len(after)), out_specs=...  8.07 us
  transfers between devices with their start and end apart: 54, of which 26 were waited for; matrix products, arithmetic and copies ran while one was open for 1% of the time, Pallas kernels for 23%

profile of v3, /device:TPU:0, one launch (start us, length us, event | category | flops | bytes accessed | tf_op | source)
XLA Modules:
  0.0 276.6 jit_solution(7888817903986470163)
XLA Ops:
  19.6 8.1 %load.1 = (bf16[22,512,512]{2,1,0:T(8,128)(2,1)S(1)}, bf16[22,512,512]{2,1,0:T(8,128)(2,1)S(1)}) custom-call(f32[22,512,512]{2,1,0:T(8,128)} %tiles.1, f32[64,8192]{1,0:T(8,128)S(1)} %get-tuple-element.68.refs_0_, s32[24]{0:T(128)S(1)} %reshape.38.refs_1_.flag, s32[24]{0:T(128)S(1)} %max.9.wanted.refs_2_, s32[24]{0:T(128)S(1)} %get-tuple-element.139.refs_3_.tile_ref, ...), custom_call_target="tpu_custom_call" | custom-call | tf_op jit(solution)/shard_map/load/pallas_call | solution.py:65
  27.7 5.9 %mirror.2 = (f32[32,3072]{1,0:T(8,128)S(1)}, f32[32,3072]{1,0:T(8,128)S(1)}, f32[32,3072]{1,0:T(8,128)S(1)}, f32[32,3072]{1,0:T(8,128)S(1)}, f32[32,3072]{1,0:T(8,128)S(1)}, /*index=5*/f32[32,3072]{1,0:T(8,128)S(1)}) custom-call(s32[3]{0:T(128)S(1)} %pad_add_fusion.1.place, s32[24]{0:T(128)S(1)} %get-tuple-element.139.refs_3_.tile_ref, ...), custom_call_target="tpu_custom_call" | custom-call | tf_op jit(solution)/shard_map/mirror/pallas_call | solution.py:164
  37.3 4.5 %own.2.refs_3_ = f32[64,8192]{1,0:T(8,128)S(1)} custom-call(s32[3]{0:T(128)S(1)} %pad_add_fusion.1.place, s32[24]{0:T(128)S(1)} %get-tuple-element.139.refs_3_.tile_ref, s32[24]{0:T(128)S(1)} %compare_convert_fusion.refs_4_.valid_ref, s32[24]{0:T(128)S(1)} %get-tuple-element.138.refs_5_.row_ref, s32[24]{0:T(128)S(1)} %add_maximum_fusion.1.refs_6_.col_ref, ...), custom_call_target="tpu_custom_call" | custom-call | tf_op jit(solution)/shard_map/own/pallas_call | solution.py:193
  41.8 19.0 %collective-permute-done.5.refs_1_ = f32[64,3072]{1,0:T(8,128)} collective-permute-done((f32[64,3072]{1,0:T(8,128)}, f32[64,3072]{1,0:T(8,128)}, u32[]{:S(2)}, u32[]{:S(2)}) %collective-permute-start.5) | collective-permute-done | bytes 786464 | tf_op jit(solution)/shard_map/ppermute | solution.py:431
  60.8 9.7 %direct.2.start = f32[64,8192]{1,0:T(8,128)S(1)} custom-call(s32[3]{0:T(128)S(1)} %pad_add_fusion.1.place, s32[24]{0:T(128)S(1)} %get-tuple-element.139.refs_3_.tile_ref, s32[24]{0:T(128)S(1)} %compare_convert_fusion.refs_4_.valid_ref, s32[24]{0:T(128)S(1)} %get-tuple-element.138.refs_5_.row_ref, bf16[22,512,512]{2,1,0:T(8,128)(2,1)S(1)} %get-tuple-element.69.high, ...), custom_call_target="tpu_custom_call" | custom-call | tf_op jit(solution)/shard_map/direct/pallas_call | solution.py:227
  78.7 6.7 %collective-permute-done.7.refs_0_ = f32[32,3072]{1,0:T(8,128)S(1)} collective-permute-done((f32[32,3072]{1,0:T(8,128)S(1)}, f32[32,3072]{1,0:T(8,128)S(1)}, u32[]{:S(2)}, u32[]{:S(2)}) %collective-permute-start.7) | collective-permute-done | bytes 393248 | tf_op jit(solution)/shard_map/ppermute | solution.py:431
  85.4 9.6 %collective-permute-done.8.refs_1_ = f32[32,3072]{1,0:T(8,128)S(1)} collective-permute-done((f32[32,3072]{1,0:T(8,128)S(1)}, f32[32,3072]{1,0:T(8,128)S(1)}, u32[]{:S(2)}, u32[]{:S(2)}) %collective-permute-start.8) | collective-permute-done | bytes 393248 | tf_op jit(solution)/shard_map/ppermute | solution.py:431
  102.5 4.6 %collective-permute-done.16.arrived = f32[32,2048]{1,0:T(8,128)S(1)} collective-permute-done((f32[32,2048]{1,0:T(8,128)S(1)}, f32[32,2048]{1,0:T(8,128)S(1)}, u32[]{:S(2)}, u32[]{:S(2)}) %collective-permute-start.16) | collective-permute-done | bytes 262176 | tf_op jit(solution)/shard_map/ppermute | solution.py:431
  107.2 6.4 %collective-permute-start.17 = (f32[32,1024]{1,0:T(8,128)S(1)}, f32[32,1024]{1,0:T(8,128)S(1)}, u32[]{:S(2)}, u32[]{:S(2)}) collective-permute-start(f32[32,1024]{1,0:T(8,128)S(1)} %get-tuple-element.89), channel_id=1, source_target_pairs={{0,3},{1,2},{2,1},{3,0},{4,7},{5,6},{6,5},{7,4},{8,11},{9,10},{10,... | collective-permute-start | bytes 393224 | tf_op jit(solution)/shard_map/ppermute | solution.py:431
  117.1 3.8 %collective-permute-start.19 = (f32[32,1152]{1,0:T(8,128)S(1)}, f32[32,1152]{1,0:T(8,128)S(1)}, u32[]{:S(2)}, u32[]{:S(2)}) collective-permute-start(f32[32,1152]{1,0:T(8,128)S(1)} %pack.6), channel_id=1, source_target_pairs={{0,3},{1,2},{2,1},{3,0},{4,7},{5,6},{6,5},{7,4},{8,11},{9,10},{10,... | collective-permute-start | bytes 442376 | tf_op jit(solution)/shard_map/ppermute | solution.py:431
  124.2 5.2 %collective-permute-start.20 = (f32[32,2176]{1,0:T(8,128)S(1)}, f32[32,2176]{1,0:T(8,128)S(1)}, u32[]{:S(2)}, u32[]{:S(2)}) collective-permute-start(f32[32,2176]{1,0:T(8,128)S(1)} %pack.7), channel_id=1, source_target_pairs={{0,1},{1,0},{2,3},{3,2},{4,5},{5,4},{6,7},{7,6},{8,9},{9,8},{10,11... | collective-permute-start | bytes 835592 | tf_op jit(solution)/shard_map/ppermute | solution.py:431
  131.5 8.8 %collective-permute-done.22.nearby = f32[32,2048]{1,0:T(8,128)S(1)} collective-permute-done((f32[32,2048]{1,0:T(8,128)S(1)}, f32[32,2048]{1,0:T(8,128)S(1)}, u32[]{:S(2)}, u32[]{:S(2)}) %collective-permute-start.22) | collective-permute-done | bytes 262176 | tf_op jit(solution)/shard_map/ppermute | solution.py:431
  151.5 7.1 %collective-permute-done.25.refs_3_ = f32[32,3200]{1,0:T(8,128)S(1)} collective-permute-done((f32[32,3200]{1,0:T(8,128)S(1)}, f32[32,3200]{1,0:T(8,128)S(1)}, u32[]{:S(2)}, u32[]{:S(2)}) %collective-permute-start.25) | collective-permute-done | bytes 409632 | tf_op jit(solution)/shard_map/ppermute | solution.py:431
  159.7 5.9 %mirror.3 = (f32[32,3072]{1,0:T(8,128)S(1)}, f32[32,3072]{1,0:T(8,128)S(1)}, f32[32,3072]{1,0:T(8,128)S(1)}, f32[32,3072]{1,0:T(8,128)S(1)}, f32[32,3072]{1,0:T(8,128)S(1)}, /*index=5*/f32[32,3072]{1,0:T(8,128)S(1)}) custom-call(s32[3]{0:T(128)S(1)} %pad_add_fusion.1.place, s32[24]{0:T(128)S(1)} %get-tuple-element.139.refs_3_.tile_ref, ...), custom_call_target="tpu_custom_call" | custom-call | tf_op jit(solution)/shard_map/mirror/pallas_call | solution.py:164
  168.5 6.5 %collective-permute-done.30.refs_2_ = f32[32,3072]{1,0:T(8,128)S(1)} collective-permute-done((f32[32,3072]{1,0:T(8,128)S(1)}, f32[32,3072]{1,0:T(8,128)S(1)}, u32[]{:S(2)}, u32[]{:S(2)}) %collective-permute-start.30) | collective-permute-done | bytes 393248 | tf_op jit(solution)/shard_map/ppermute | solution.py:431
  177.0 4.5 %own.3.refs_6_ = f32[64,8192]{1,0:T(8,128)S(1)} custom-call(s32[3]{0:T(128)S(1)} %pad_add_fusion.1.place, s32[24]{0:T(128)S(1)} %get-tuple-element.139.refs_3_.tile_ref, s32[24]{0:T(128)S(1)} %compare_convert_fusion.refs_4_.valid_ref, s32[24]{0:T(128)S(1)} %get-tuple-element.138.refs_5_.row_ref, s32[24]{0:T(128)S(1)} %add_maximum_fusion.1.refs_6_.col_ref, ...), custom_call_target="tpu_custom_call" | custom-call | tf_op jit(solution)/shard_map/own/pallas_call | solution.py:193
  181.5 4.8 %collective-permute-done.26.refs_4_ = f32[32,3200]{1,0:T(8,128)S(1)} collective-permute-done((f32[32,3200]{1,0:T(8,128)S(1)}, f32[32,3200]{1,0:T(8,128)S(1)}, u32[]{:S(2)}, u32[]{:S(2)}) %collective-permute-start.26) | collective-permute-done | bytes 409632 | tf_op jit(solution)/shard_map/ppermute | solution.py:431
  186.3 8.9 %direct.3.start = f32[64,8192]{1,0:T(8,128)S(1)} custom-call(s32[3]{0:T(128)S(1)} %pad_add_fusion.1.place, s32[24]{0:T(128)S(1)} %get-tuple-element.139.refs_3_.tile_ref, s32[24]{0:T(128)S(1)} %compare_convert_fusion.refs_4_.valid_ref, s32[24]{0:T(128)S(1)} %get-tuple-element.138.refs_5_.row_ref, bf16[22,512,512]{2,1,0:T(8,128)(2,1)S(1)} %get-tuple-element.69.high, ...), custom_call_target="tpu_custom_call" | custom-call | tf_op jit(solution)/shard_map/direct/pallas_call | solution.py:227
  195.2 4.7 %collective-permute-done.33.refs_2_ = f32[32,3072]{1,0:T(8,128)S(1)} collective-permute-done((f32[32,3072]{1,0:T(8,128)S(1)}, f32[32,3072]{1,0:T(8,128)S(1)}, u32[]{:S(2)}, u32[]{:S(2)}) %collective-permute-start.33) | collective-permute-done | bytes 393248 | tf_op jit(solution)/shard_map/ppermute | solution.py:431
  208.9 6.9 %cholesky.2 = (f32[64,64]{1,0:T(8,128)}, f32[64,64]{1,0:T(8,128)S(1)}) custom-call(f32[64,64]{1,0:T(8,128)S(1)} %pad_maximum_fusion.gram), custom_call_target="tpu_custom_call" | custom-call | tf_op jit(solution)/shard_map/cholesky/pallas_call | solution.py:394
  215.8 7.9 %collective-permute-done.38.refs_1_ = f32[32,3072]{1,0:T(8,128)S(1)} collective-permute-done((f32[32,3072]{1,0:T(8,128)S(1)}, f32[32,3072]{1,0:T(8,128)S(1)}, u32[]{:S(2)}, u32[]{:S(2)}) %collective-permute-start.38) | collective-permute-done | bytes 393248 | tf_op jit(solution)/shard_map/ppermute | solution.py:431
  236.1 4.0 %collective-permute-start.42 = (f32[32,1024]{1,0:T(8,128)S(1)}, f32[32,1024]{1,0:T(8,128)S(1)}, u32[]{:S(2)}, u32[]{:S(2)}) collective-permute-start(f32[32,1024]{1,0:T(8,128)S(1)} %get-tuple-element.128), channel_id=1, source_target_pairs={{0,3},{1,2},{2,1},{3,0},{4,7},{5,6},{6,5},{7,4},{8,11},{9,10},{10,... | collective-permute-start | bytes 393224 | tf_op jit(solution)/shard_map/ppermute | solution.py:431
  259.1 4.4 %collective-permute-start.51 = (f32[32,2048]{1,0:T(8,128)S(1)}, f32[32,2048]{1,0:T(8,128)S(1)}, u32[]{:S(2)}, u32[]{:S(2)}) collective-permute-start(f32[32,2048]{1,0:T(8,128)S(1)} %pack.10), channel_id=1, source_target_pairs={{0,1},{1,0},{2,3},{3,2},{4,5},{5,4},{6,7},{7,6},{8,9},{9,8},{10,11... | collective-permute-start | bytes 786440 | tf_op jit(solution)/shard_map/ppermute | solution.py:431
  265.5 6.3 %cholesky.3 = (f32[64,64]{1,0:T(8,128)S(1)}, f32[64,64]{1,0:T(8,128)S(1)}) custom-call(f32[64,64]{1,0:T(8,128)S(1)} %add_add_fusion.gram), custom_call_target="tpu_custom_call" | custom-call | tf_op jit(solution)/shard_map/cholesky/pallas_call | solution.py:394
  (157 shorter events, 111.4 us)
Async XLA Ops:
  16.1 20.7 %collective-permute-start.4 = (f32[64,3072]{1,0:T(8,128)}, f32[64,3072]{1,0:T(8,128)S(1)}, u32[]{:S(2)}, u32[]{:S(2)}) collective-permute-start(f32[64,3072]{1,0:T(8,128)} %get-tuple-element.71), channel_id=1, source_target_pairs={{0,8},{4,12},{8,0},{12,4},{16,24},{20,28},{24,16},{28,20},{1,9},{5... | collective-permute-start | bytes 2359304 | tf_op jit(solution)/shard_map/ppermute | solution.py:431
  16.6 44.2 %collective-permute-start.5 = (f32[64,3072]{1,0:T(8,128)}, f32[64,3072]{1,0:T(8,128)}, u32[]{:S(2)}, u32[]{:S(2)}) collective-permute-start(f32[64,3072]{1,0:T(8,128)} %get-tuple-element.72), channel_id=1, source_target_pairs={{0,16},{4,20},{8,24},{12,28},{16,0},{20,4},{24,8},{28,12},{1,17},{... | collective-permute-start | bytes 2359304 | tf_op jit(solution)/shard_map/ppermute | solution.py:431
  16.6 44.2 %collective-permute-start.6 = (f32[64,3072]{1,0:T(8,128)}, f32[64,3072]{1,0:T(8,128)}, u32[]{:S(2)}, u32[]{:S(2)}) collective-permute-start(f32[64,3072]{1,0:T(8,128)} %get-tuple-element.73), channel_id=1, source_target_pairs={{0,24},{4,28},{8,16},{12,20},{16,8},{20,12},{24,0},{28,4},{1,25},{... | collective-permute-start | bytes 2359304 | tf_op jit(solution)/shard_map/ppermute | solution.py:431
  33.6 36.9 %collective-permute-start.11 = (f32[32,3072]{1,0:T(8,128)S(1)}, f32[32,3072]{1,0:T(8,128)S(1)}, u32[]{:S(2)}, u32[]{:S(2)}) collective-permute-start(f32[32,3072]{1,0:T(8,128)S(1)} %get-tuple-element.78), channel_id=1, source_target_pairs={{0,16},{4,20},{8,24},{12,28},{16,0},{20,4},{24,8},{28,12},{1,17},{... | collective-permute-start | bytes 1179656 | tf_op jit(solution)/shard_map/ppermute | solution.py:431
  34.5 36.0 %collective-permute-start.12 = (f32[32,3072]{1,0:T(8,128)S(1)}, f32[32,3072]{1,0:T(8,128)S(1)}, u32[]{:S(2)}, u32[]{:S(2)}) collective-permute-start(f32[32,3072]{1,0:T(8,128)S(1)} %get-tuple-element.79), channel_id=1, source_target_pairs={{0,24},{4,28},{8,16},{12,20},{16,8},{20,12},{24,0},{28,4},{1,25},{... | collective-permute-start | bytes 1179656 | tf_op jit(solution)/shard_map/ppermute | solution.py:431
  36.8 33.8 %collective-permute-start.10 = (f32[32,3072]{1,0:T(8,128)S(1)}, f32[32,3072]{1,0:T(8,128)S(1)}, u32[]{:S(2)}, u32[]{:S(2)}) collective-permute-start(f32[32,3072]{1,0:T(8,128)S(1)} %get-tuple-element.74.refs_1_), channel_id=1, source_target_pairs={{0,8},{4,12},{8,0},{12,4},{16,24},{20,28},{24,16},{28,20},{1,9},{5... | collective-permute-start | bytes 1179656 | tf_op jit(solution)/shard_map/ppermute | solution.py:431
  71.7 13.7 %collective-permute-start.7 = (f32[32,3072]{1,0:T(8,128)S(1)}, f32[32,3072]{1,0:T(8,128)S(1)}, u32[]{:S(2)}, u32[]{:S(2)}) collective-permute-start(f32[32,3072]{1,0:T(8,128)S(1)} %get-tuple-element.75), channel_id=1, source_target_pairs={{0,8},{4,12},{8,0},{12,4},{16,24},{20,28},{24,16},{28,20},{1,9},{5... | collective-permute-start | bytes 1179656 | tf_op jit(solution)/shard_map/ppermute | solution.py:431
  75.5 19.6 %collective-permute-start.8 = (f32[32,3072]{1,0:T(8,128)S(1)}, f32[32,3072]{1,0:T(8,128)S(1)}, u32[]{:S(2)}, u32[]{:S(2)}) collective-permute-start(f32[32,3072]{1,0:T(8,128)S(1)} %get-tuple-element.76), channel_id=1, source_target_pairs={{0,16},{4,20},{8,24},{12,28},{16,0},{20,4},{24,8},{28,12},{1,17},{... | collective-permute-start | bytes 1179656 | tf_op jit(solution)/shard_map/ppermute | solution.py:431
  75.5 19.6 %collective-permute-start.9 = (f32[32,3072]{1,0:T(8,128)S(1)}, f32[32,3072]{1,0:T(8,128)S(1)}, u32[]{:S(2)}, u32[]{:S(2)}) collective-permute-start(f32[32,3072]{1,0:T(8,128)S(1)} %get-tuple-element.77), channel_id=1, source_target_pairs={{0,24},{4,28},{8,16},{12,20},{16,8},{20,12},{24,0},{28,4},{1,25},{... | collective-permute-start | bytes 1179656 | tf_op jit(solution)/shard_map/ppermute | solution.py:431
  77.6 17.5 %collective-permute-start.14 = (f32[32,2048]{1,0:T(8,128)S(1)}, f32[32,2048]{1,0:T(8,128)S(1)}, u32[]{:S(2)}, u32[]{:S(2)}) collective-permute-start(f32[32,2048]{1,0:T(8,128)S(1)} %get-tuple-element.82), channel_id=1, source_target_pairs={{0,1},{1,0},{2,3},{3,2},{4,5},{5,4},{6,7},{7,6},{8,9},{9,8},{10,11... | collective-permute-start | bytes 786440 | tf_op jit(solution)/shard_map/ppermute | solution.py:431
  99.9 13.7 %collective-permute-start.18 = (f32[32,1024]{1,0:T(8,128)S(1)}, f32[32,1024]{1,0:T(8,128)S(1)}, u32[]{:S(2)}, u32[]{:S(2)}) collective-permute-start(f32[32,1024]{1,0:T(8,128)S(1)} %get-tuple-element.92), channel_id=1, source_target_pairs={{0,3},{1,2},{2,1},{3,0},{4,7},{5,6},{6,5},{7,4},{8,11},{9,10},{10,... | collective-permute-start | bytes 393224 | tf_op jit(solution)/shard_map/ppermute | solution.py:431
  124.2 16.6 %collective-permute-start.20 = (f32[32,2176]{1,0:T(8,128)S(1)}, f32[32,2176]{1,0:T(8,128)S(1)}, u32[]{:S(2)}, u32[]{:S(2)}) collective-permute-start(f32[32,2176]{1,0:T(8,128)S(1)} %pack.7), channel_id=1, source_target_pairs={{0,1},{1,0},{2,3},{3,2},{4,5},{5,4},{6,7},{7,6},{8,9},{9,8},{10,11... | collective-permute-start | bytes 835592 | tf_op jit(solution)/shard_map/ppermute | solution.py:431
  146.5 20.5 %collective-permute-start.28 = (f32[32,3072]{1,0:T(8,128)S(1)}, f32[32,3072]{1,0:T(8,128)S(1)}, u32[]{:S(2)}, u32[]{:S(2)}) collective-permute-start(f32[32,3072]{1,0:T(8,128)S(1)} %get-tuple-element.98), channel_id=1, source_target_pairs={{0,8},{4,12},{8,0},{12,4},{16,24},{20,28},{24,16},{28,20},{1,9},{5... | collective-permute-start | bytes 1179656 | tf_op jit(solution)/shard_map/ppermute | solution.py:431
  148.3 19.0 %collective-permute-start.29 = (f32[32,3072]{1,0:T(8,128)S(1)}, f32[32,3072]{1,0:T(8,128)S(1)}, u32[]{:S(2)}, u32[]{:S(2)}) collective-permute-start(f32[32,3072]{1,0:T(8,128)S(1)} %get-tuple-element.99), channel_id=1, source_target_pairs={{0,16},{4,20},{8,24},{12,28},{16,0},{20,4},{24,8},{28,12},{1,17},{... | collective-permute-start | bytes 1179656 | tf_op jit(solution)/shard_map/ppermute | solution.py:431
  148.4 26.7 %collective-permute-start.30 = (f32[32,3072]{1,0:T(8,128)S(1)}, f32[32,3072]{1,0:T(8,128)S(1)}, u32[]{:S(2)}, u32[]{:S(2)}) collective-permute-start(f32[32,3072]{1,0:T(8,128)S(1)} %get-tuple-element.100), channel_id=1, source_target_pairs={{0,24},{4,28},{8,16},{12,20},{16,8},{20,12},{24,0},{28,4},{1,25},{... | collective-permute-start | bytes 1179656 | tf_op jit(solution)/shard_map/ppermute | solution.py:431
  150.0 36.3 %collective-permute-start.26 = (f32[32,3200]{1,0:T(8,128)S(1)}, f32[32,3200]{1,0:T(8,128)S(1)}, u32[]{:S(2)}, u32[]{:S(2)}) collective-permute-start(f32[32,3200]{1,0:T(8,128)S(1)} %get-tuple-element.96), channel_id=1, source_target_pairs={{0,16},{4,20},{8,24},{12,28},{16,0},{20,4},{24,8},{28,12},{1,17},{... | collective-permute-start | bytes 1228808 | tf_op jit(solution)/shard_map/ppermute | solution.py:431
  158.6 27.7 %collective-permute-start.27 = (f32[32,3200]{1,0:T(8,128)S(1)}, f32[32,3200]{1,0:T(8,128)S(1)}, u32[]{:S(2)}, u32[]{:S(2)}) collective-permute-start(f32[32,3200]{1,0:T(8,128)S(1)} %get-tuple-element.97), channel_id=1, source_target_pairs={{0,24},{4,28},{8,16},{12,20},{16,8},{20,12},{24,0},{28,4},{1,25},{... | collective-permute-start | bytes 1228808 | tf_op jit(solution)/shard_map/ppermute | solution.py:431
  167.0 28.2 %collective-permute-start.31 = (f32[32,3072]{1,0:T(8,128)S(1)}, f32[32,3072]{1,0:T(8,128)S(1)}, u32[]{:S(2)}, u32[]{:S(2)}) collective-permute-start(f32[32,3072]{1,0:T(8,128)S(1)} %get-tuple-element.103.refs_2_), channel_id=1, source_target_pairs={{0,8},{4,12},{8,0},{12,4},{16,24},{20,28},{24,16},{28,20},{1,9},{5... | collective-permute-start | bytes 1179656 | tf_op jit(solution)/shard_map/ppermute | solution.py:431
  167.2 32.7 %collective-permute-start.33 = (f32[32,3072]{1,0:T(8,128)S(1)}, f32[32,3072]{1,0:T(8,128)S(1)}, u32[]{:S(2)}, u32[]{:S(2)}) collective-permute-start(f32[32,3072]{1,0:T(8,128)S(1)} %get-tuple-element.107), channel_id=1, source_target_pairs={{0,24},{4,28},{8,16},{12,20},{16,8},{20,12},{24,0},{28,4},{1,25},{... | collective-permute-start | bytes 1179656 | tf_op jit(solution)/shard_map/ppermute | solution.py:431
  175.0 26.7 %collective-permute-start.32 = (f32[32,3072]{1,0:T(8,128)S(1)}, f32[32,3072]{1,0:T(8,128)S(1)}, u32[]{:S(2)}, u32[]{:S(2)}) collective-permute-start(f32[32,3072]{1,0:T(8,128)S(1)} %get-tuple-element.105), channel_id=1, source_target_pairs={{0,16},{4,20},{8,24},{12,28},{16,0},{20,4},{24,8},{28,12},{1,17},{... | collective-permute-start | bytes 1179656 | tf_op jit(solution)/shard_map/ppermute | solution.py:431
  204.1 19.6 %collective-permute-start.38 = (f32[32,3072]{1,0:T(8,128)S(1)}, f32[32,3072]{1,0:T(8,128)S(1)}, u32[]{:S(2)}, u32[]{:S(2)}) collective-permute-start(f32[32,3072]{1,0:T(8,128)S(1)} %get-tuple-element.119), channel_id=1, source_target_pairs={{0,16},{4,20},{8,24},{12,28},{16,0},{20,4},{24,8},{28,12},{1,17},{... | collective-permute-start | bytes 1179656 | tf_op jit(solution)/shard_map/ppermute | solution.py:431
  204.7 19.0 %collective-permute-start.37 = (f32[32,3072]{1,0:T(8,128)S(1)}, f32[32,3072]{1,0:T(8,128)S(1)}, u32[]{:S(2)}, u32[]{:S(2)}) collective-permute-start(f32[32,3072]{1,0:T(8,128)S(1)} %get-tuple-element.117), channel_id=1, source_target_pairs={{0,8},{4,12},{8,0},{12,4},{16,24},{20,28},{24,16},{28,20},{1,9},{5... | collective-permute-start | bytes 1179656 | tf_op jit(solution)/shard_map/ppermute | solution.py:431
  207.1 16.7 %collective-permute-start.35 = (f32[32,2048]{1,0:T(8,128)S(1)}, f32[32,2048]{1,0:T(8,128)S(1)}, u32[]{:S(2)}, u32[]{:S(2)}) collective-permute-start(f32[32,2048]{1,0:T(8,128)S(1)} %get-tuple-element.113), channel_id=1, source_target_pairs={{0,1},{1,0},{2,3},{3,2},{4,5},{5,4},{6,7},{7,6},{8,9},{9,8},{10,11... | collective-permute-start | bytes 786440 | tf_op jit(solution)/shard_map/ppermute | solution.py:431
  259.1 13.6 %collective-permute-start.51 = (f32[32,2048]{1,0:T(8,128)S(1)}, f32[32,2048]{1,0:T(8,128)S(1)}, u32[]{:S(2)}, u32[]{:S(2)}) collective-permute-start(f32[32,2048]{1,0:T(8,128)S(1)} %pack.10), channel_id=1, source_target_pairs={{0,1},{1,0},{2,3},{3,2},{4,5},{5,4},{6,7},{7,6},{8,9},{9,8},{10,11... | collective-permute-start | bytes 786440 | tf_op jit(solution)/shard_map/ppermute | solution.py:431
  (31 other events, 222.6 us)

commit v4 on v3

--- a/solution.py
+++ b/solution.py
@@ -139,7 +139,7 @@
 
 def mirror_kernel(chips, group, parts, place, tile_ref, valid_ref, row_ref, high, low, *refs):
     pairs = refs[:parts]
-    outs = refs[-HALVES * (chips - 1) :]
+    outs = refs[1 - chips :]
     bs = high.shape[1]
     base = place[1] * (pairs[0].shape[1] // (2 * bs))
 
@@ -149,10 +149,7 @@
         for k in range(1, chips):
             @pl.when(slot // group == place[0] ^ k)
             def _():
-                half = value.shape[0] // HALVES
-                for h in range(HALVES):
-                    out = outs[h * (chips - 1) + k - 1]
-                    out[:, block(slot % group, bs)] = value[h * half : (h + 1) * half]
+                outs[k - 1][:, block(slot % group, bs)] = value
 
     visit_tiles(range(1, chips), group, place, tile_ref, valid_ref, [high, low], body)
 
@@ -161,15 +158,14 @@
     half = pairs[0].shape[0]
     bs = tiles[0].shape[1]
     parts = len(pairs)
-    outs = pl.pallas_call(
+    return pl.pallas_call(
         functools.partial(mirror_kernel, chips, group, parts),
         in_specs=[SMEM] * 4 + [VMEM] * 2 + [VMEM] * parts + [ANY] * len(after),
-        out_specs=[VMEM] * (HALVES * (chips - 1)),
-        out_shape=[shape(half * parts // HALVES, group * bs)] * (HALVES * (chips - 1)),
+        out_specs=[VMEM] * (chips - 1),
+        out_shape=[shape(half * parts, group * bs)] * (chips - 1),
         compiler_params=params(6),
         name="mirror",
     )(place, *tables[:3], *tiles, *pairs, *after)
-    return [outs[h * (chips - 1) : (h + 1) * (chips - 1)] for h in range(HALVES)]
 
 
 def own_kernel(group, parts, place, tile_ref, valid_ref, row_ref, col_ref, high, low, *refs):
@@ -235,11 +231,10 @@
     )(place, *tables[:3], *tiles, *arrived, start, *after)
 
 
-def gather_kernel(chips, group, bs, h, place, wanted, flag, start, *refs):
+def gather_kernel(chips, group, bs, place, wanted, flag, start, *refs):
     returned = refs[: chips - 1]
     own, sibling, total = refs[-3:]
-    half = total.shape[0]
-    total[...] = start[h * half : (h + 1) * half]
+    total[...] = start[...]
     for k in range(1, chips):
         first = (place[0] ^ k) * group
 
@@ -256,55 +251,58 @@
     sibling[...] = total[:, block(1 - place[1], rows)]
 
 
-def gather(place, wanted, flag, start, returned, chips, group, bs, h, after=()):
-    half, rows = returned[0].shape[0], start.shape[1]
-    return pl.pallas_call(
-        functools.partial(gather_kernel, chips, group, bs, h),
-        in_specs=[SMEM] * 3 + [VMEM] * chips + [ANY] * len(after),
+def gather(place, wanted, flag, start, returned, chips, group, bs):
+    width, rows = start.shape
+    return pl.pallas_call(
+        functools.partial(gather_kernel, chips, group, bs),
+        in_specs=[SMEM] * 3 + [VMEM] * chips,
         out_specs=[VMEM] * 2,
-        out_shape=[shape(half, rows // 2)] * 2,
-        scratch_shapes=[pltpu.VMEM((half, rows), F32)],
+        out_shape=[shape(width, rows // 2)] * 2,
+        scratch_shapes=[pltpu.VMEM((width, rows), F32)],
         compiler_params=params(16),
         name="gather",
-    )(place, wanted, flag, start, *returned, *after)
-
-
-def deal_kernel(place, own, other, kept, sent):
-    quarter = kept.shape[1] // 2
-    for out, pair in ((kept, (0, 3)), (sent, (1, 2))):
-        for at, j in enumerate(pair):
+    )(place, wanted, flag, start, *returned)
+
+
+def deal_kernel(place, own, other, *outs):
+    half, quarter = outs[0].shape[0], outs[0].shape[1] // 2
+    for n, out in enumerate(outs):
+        rows = slice(n // 2 * half, (n // 2 + 1) * half)
+        for at, j in enumerate(((0, 3), (1, 2))[n % 2]):
             source = block(place[2] ^ j, quarter)
-            out[:, at * quarter : (at + 1) * quarter] = own[:, source] + other[:, source]
+            out[:, at * quarter : (at + 1) * quarter] = own[rows, source] + other[rows, source]
 
 
 def deal(place, own, other):
-    half, rows = own.shape
-    return pl.pallas_call(
+    width, rows = own.shape
+    outs = pl.pallas_call(
         deal_kernel,
         in_specs=[SMEM, VMEM, VMEM],
-        out_specs=[VMEM] * 2,
-        out_shape=[shape(half, rows // 2)] * 2,
+        out_specs=[VMEM] * (HALVES * 2),
+        out_shape=[shape(width // HALVES, rows // 2)] * (HALVES * 2),
         compiler_params=params(6),
         name="deal",
     )(place, own, other)
-
-
-def add_kernel(kept, arrived, mine, other):
+    return [outs[h * 2 : (h + 1) * 2] for h in range(HALVES)]
+
+
+def add_kernel(kept, arrived, *refs):
+    mine, other = refs[-2:]
     quarter = mine.shape[1]
     mine[...] = kept[:, :quarter] + arrived[:, :quarter]
     other[...] = kept[:, quarter:] + arrived[:, quarter:]
 
 
-def add_pair(kept, arrived):
+def add_pair(kept, arrived, after=()):
     half, both = kept.shape
     return pl.pallas_call(
         add_kernel,
-        in_specs=[VMEM] * 2,
+        in_specs=[VMEM] * 2 + [ANY] * len(after),
         out_specs=[VMEM] * 2,
         out_shape=[shape(half, both // 2)] * 2,
         compiler_params=params(6),
         name="add",
-    )(kept, arrived)
+    )(kept, arrived, *after)
 
 
 def total_kernel(mine, arrived, *refs):
@@ -478,12 +476,13 @@
     def serve_half(own, sibling, after=()):
         return serve(place, wanted, own, sibling, rows, chips, group, bs, after)
 
-    def reduce_half(h, start, returned, after=(), deps=()):
-        own, other = gather(place, wanted, flag, start, returned, chips, group, bs, h, after)
-        kept, sent = deal(place, own, swap_core(other))
-        arrived = swap(gate(sent, *deps), "by", 1)
-        mine, other = add_pair(kept, arrived)
-        return kept, arrived, mine, swap(other, "by", 3)
+    def deal_halves(start, returned):
+        own, other = gather(place, wanted, flag, start, returned, chips, group, bs)
+        return deal(place, own, swap_core(other))
+
+    def reduce_half(kept, sent, hold=(), after=()):
+        mine, other = add_pair(kept, swap(sent, "by", 1), hold)
+        return total(mine, swap(other, "by", 3), after)
 
     def fold(gram):
         return jnp.concatenate([gram[: width // 2], gram[width // 2 :]], axis=1)
@@ -503,40 +502,36 @@
     received = [swap_chips(served)]
     tiles = load(tiles, [pair, flag, wanted, *tables])
     mirrored = mirror(place, tables, tiles, [pair], chips, group)
-    start = own(place, tables, tiles, [pair], group, [mirrored[0][0]])
+    start = own(place, tables, tiles, [pair], group, [mirrored[0]])
     start = direct(place, tables, tiles, start, received, chips, group)
-    returned = [swap_chips(x) for x in mirrored]
-    kept, first, mine, last = reduce_half(0, start, returned[0])
-    _, _, mine_1, last_1 = reduce_half(1, start, returned[1], [first], [first])
-    quarters = [total(mine, last)]
-    quarters.append(total(mine_1, last_1, [quarters[0]]))
     every, behind = (0, quart), (quart, quart + 2 * width)
+    dealt = deal_halves(start, swap_chips(mirrored))
+    quarters = [reduce_half(*dealt[0])]
     across = swap(quarters[0], "by", 3)
+    quarters.append(reduce_half(*dealt[1], [], [across]))
     nearby = swap(pack([(quarters[0], *every)], [(across, *every)]), "by", 1)
     piece = join(place, quarters[0], across, nearby)
     pair, served, _ = serve_half(piece, swap_core(piece))
     pairs, received = [pair], [swap_chips(served)]
-    rider = fold(gram_of(quarters))
+    rider = gate(fold(gram_of(quarters)), served[0])
     across = swap(pack([(quarters[1], *every)], [(rider, 0, 2 * width)]), "by", 3)
     sums = [(rider, 0, 2 * width), (across, *behind)]
     nearby = swap(pack([(quarters[1], *every)], [(across, *every)], sums), "by", 1)
     rider = pack(sums + [(nearby, 2 * quart, 2 * quart + 2 * width)])
-    piece = join(place, quarters[1], across, nearby, rider, [piece])
-    pair, served, rider = serve_half(piece, swap_core(piece), [pairs[0]])
+    piece = join(place, quarters[1], across, nearby, rider, received[0])
+    pair, served, rider = serve_half(piece, swap_core(piece), received[0])
     pairs.append(pair)
     received.append(swap_chips(served))
     gram = unfold(tree([rider] + [x[:, group * bs :] for x in received[1]]))
     mirrored = mirror(place, tables, tiles, pairs, chips, group)
-    returned = [swap_chips([gate(x, received[1][0]) for x in mirrored[0]])]
-    returned.append(swap_chips([gate(x, received[1][-1]) for x in mirrored[1]]))
-    start = own(place, tables, tiles, pairs, group, [mirrored[0][0]])
-    start = direct(place, tables, tiles, start, received, chips, group)
-    kept, first, mine, last = reduce_half(0, start, returned[0])
-    factor, inverse = cholesky(gate(gram, kept))
-    _, _, mine_1, last_1 = reduce_half(1, start, returned[1], [inverse, first], [first])
-    quarters = [total(mine, last)]
+    returned = swap_chips([gate(x, *received[0], *received[1]) for x in mirrored])
+    start = own(place, tables, tiles, pairs, group, [mirrored[0]])
+    start = direct(place, tables, tiles, start, received, chips, group, returned[:1])
+    dealt = deal_halves(start, returned)
+    factor, inverse = cholesky(gate(gram, dealt[0][0]))
+    quarters = [reduce_half(*dealt[0], [inverse])]
     across = swap(quarters[0], "by", 3)
-    quarters.append(total(mine_1, last_1, [quarters[0]]))
+    quarters.append(reduce_half(*dealt[1]))
     whole = jnp.concatenate(quarters, axis=0)
     gram_0 = gram_of([jnp.dot(inverse, whole, precision=HIGHEST)])
     gram_1 = all_sum(gram_0, "by", by_all)

time: 277 us -> 273 us (0.986)
  starting transfers between devices: 82.6 us -> 62.1 us
  waiting for transfers between devices: 110 us -> 129 us
  Pallas kernels: 76.3 us -> 72.3 us
    ppermute x54 -> x46, starting transfers between devices: 82.6 us -> 62.1 us  [swap(): return lax.ppermute(x, axis, [(i, i ^ k) for i in range(size)])]
    ppermute x54 -> x46, waiting for transfers between devices: 110 us -> 129 us  [swap(): return lax.ppermute(x, axis, [(i, i ^ k) for i in range(size)])]
  transfers between devices with their start and end apart: 54 -> 46, of which waited for: 26 -> 30; matrix products, arithmetic and copies ran while one was open for 1% -> 2% of each run, Pallas kernels for 23% -> 23%
where the time goes in v4:
time: 273 us
  waiting for transfers between devices  129 us (47%)
  Pallas kernels  72.3 us (26%)
  starting transfers between devices  62.1 us (23%)
  local copies, waits for them, and re-layouts  5.18 us (2%)
    ppermute x46, waiting for transfers between devices, swap(): return lax.ppermute(x, axis, [(i, i ^ k) for i in range(size)])  129 us
    ppermute x46, starting transfers between devices, swap(): return lax.ppermute(x, axis, [(i, i ^ k) for i in range(size)])  62.1 us
    pallas_call x2, Pallas kernels, direct(): pl.pallas_call(functools.partial(direct_kernel, chips, group, parts), in_...  17.8 us
    pallas_call x2, Pallas kernels, cholesky(): pl.pallas_call(cholesky_kernel, out_shape=[shape(n, n)] * 2, compiler_par...  13.2 us
    pallas_call x2, Pallas kernels, mirror(): pl.pallas_call(functools.partial(mirror_kernel, chips, group, parts), in_...  11.9 us
    pallas_call x2, Pallas kernels, own(): pl.pallas_call(functools.partial(own_kernel, group, parts), in_specs=[SME...  9.13 us
    pallas_call x1, Pallas kernels, load(): pl.pallas_call(load_kernel, in_specs=[ANY] * (1 + len(after)), out_specs=...  8.07 us
  transfers between devices with their start and end apart: 46, of which 30 were waited for; matrix products, arithmetic and copies ran while one was open for 2% of the time, Pallas kernels for 23%

profile of v4, /device:TPU:0, one launch (start us, length us, event | category | flops | bytes accessed | tf_op | source)
XLA Modules:
  0.0 272.7 jit_solution(833681782234659558)
XLA Ops:
  21.0 8.1 %load.1 = (bf16[22,512,512]{2,1,0:T(8,128)(2,1)S(1)}, bf16[22,512,512]{2,1,0:T(8,128)(2,1)S(1)}) custom-call(f32[22,512,512]{2,1,0:T(8,128)} %tiles.1, f32[64,8192]{1,0:T(8,128)S(1)} %get-tuple-element.54.refs_0_, s32[24]{0:T(128)S(1)} %reshape.38.refs_1_.flag, s32[24]{0:T(128)S(1)} %max.9.wanted.refs_2_, s32[24]{0:T(128)S(1)} %get-tuple-element.111.refs_3_.tile_ref, ...), custom_call_target="tpu_custom_call" | custom-call | tf_op jit(solution)/shard_map/load/pallas_call | solution.py:65
  29.1 6.1 %mirror.2 = (f32[64,3072]{1,0:T(8,128)S(1)}, f32[64,3072]{1,0:T(8,128)S(1)}, f32[64,3072]{1,0:T(8,128)S(1)}) custom-call(s32[3]{0:T(128)S(1)} %pad_add_fusion.1.place, s32[24]{0:T(128)S(1)} %get-tuple-element.111.refs_3_.tile_ref, s32[24]{0:T(128)S(1)} %compare_convert_fusion.refs_4_.valid_ref, s32[24]{0:T(128)S(1)} %get-tuple-element.110.refs_5_.row_ref, ...), custom_call_target="tpu_custom_call" | custom-call | tf_op jit(solution)/shard_map/mirror/pallas_call | solution.py:161
  38.7 4.6 %own.2.refs_3_ = f32[64,8192]{1,0:T(8,128)S(1)} custom-call(s32[3]{0:T(128)S(1)} %pad_add_fusion.1.place, s32[24]{0:T(128)S(1)} %get-tuple-element.111.refs_3_.tile_ref, s32[24]{0:T(128)S(1)} %compare_convert_fusion.refs_4_.valid_ref, s32[24]{0:T(128)S(1)} %get-tuple-element.110.refs_5_.row_ref, s32[24]{0:T(128)S(1)} %add_maximum_fusion.1.refs_6_.col_ref, ...), custom_call_target="tpu_custom_call" | custom-call | tf_op jit(solution)/shard_map/own/pallas_call | solution.py:189
  43.3 27.4 %collective-permute-done.5.refs_1_ = f32[64,3072]{1,0:T(8,128)S(1)} collective-permute-done((f32[64,3072]{1,0:T(8,128)}, f32[64,3072]{1,0:T(8,128)S(1)}, u32[]{:S(2)}, u32[]{:S(2)}) %collective-permute-start.5) | collective-permute-done | bytes 786464 | tf_op jit(solution)/shard_map/ppermute | solution.py:429
  70.7 8.9 %direct.2.start = f32[64,8192]{1,0:T(8,128)S(1)} custom-call(s32[3]{0:T(128)S(1)} %pad_add_fusion.1.place, s32[24]{0:T(128)S(1)} %get-tuple-element.111.refs_3_.tile_ref, s32[24]{0:T(128)S(1)} %compare_convert_fusion.refs_4_.valid_ref, s32[24]{0:T(128)S(1)} %get-tuple-element.110.refs_5_.row_ref, bf16[22,512,512]{2,1,0:T(8,128)(2,1)S(1)} %get-tuple-element.55.high, ...), custom_call_target="tpu_custom_call" | custom-call | tf_op jit(solution)/shard_map/direct/pallas_call | solution.py:223
  79.6 7.2 %collective-permute-done.8.refs_1_ = f32[64,3072]{1,0:T(8,128)S(1)} collective-permute-done((f32[64,3072]{1,0:T(8,128)S(1)}, f32[64,3072]{1,0:T(8,128)S(1)}, u32[]{:S(2)}, u32[]{:S(2)}) %collective-permute-start.8) | collective-permute-done | bytes 786464 | tf_op jit(solution)/shard_map/ppermute | solution.py:429
  93.1 6.8 %collective-permute-done.13.arrived = f32[32,2048]{1,0:T(8,128)S(1)} collective-permute-done((f32[32,2048]{1,0:T(8,128)S(1)}, f32[32,2048]{1,0:T(8,128)S(1)}, u32[]{:S(2)}, u32[]{:S(2)}) %collective-permute-start.13) | collective-permute-done | bytes 262176 | tf_op jit(solution)/shard_map/ppermute | solution.py:429
  100.0 3.6 %collective-permute-start.14 = (f32[32,1024]{1,0:T(8,128)S(1)}, f32[32,1024]{1,0:T(8,128)S(1)}, u32[]{:S(2)}, u32[]{:S(2)}) collective-permute-start(f32[32,1024]{1,0:T(8,128)S(1)} %get-tuple-element.72), channel_id=1, source_target_pairs={{0,3},{1,2},{2,1},{3,0},{4,7},{5,6},{6,5},{7,4},{8,11},{9,10},{10,... | collective-permute-start | bytes 393224 | tf_op jit(solution)/shard_map/ppermute | solution.py:429
  106.9 3.6 %collective-permute-start.15 = (f32[32,1024]{1,0:T(8,128)S(1)}, f32[32,1024]{1,0:T(8,128)S(1)}, u32[]{:S(2)}, u32[]{:S(2)}) collective-permute-start(f32[32,1024]{1,0:T(8,128)S(1)} %total.4.refs_0_.mine), channel_id=1, source_target_pairs={{0,3},{1,2},{2,1},{3,0},{4,7},{5,6},{6,5},{7,4},{8,11},{9,10},{10,... | collective-permute-start | bytes 393224 | tf_op jit(solution)/shard_map/ppermute | solution.py:429
  111.0 4.0 %collective-permute-done.15.refs_0_.refs_1_.across = f32[32,1024]{1,0:T(8,128)S(1)} collective-permute-done((f32[32,1024]{1,0:T(8,128)S(1)}, f32[32,1024]{1,0:T(8,128)S(1)}, u32[]{:S(2)}, u32[]{:S(2)}) %collective-permute-start.15) | collective-permute-done | bytes 131104 | tf_op jit(solution)/shard_map/ppermute | solution.py:429
  115.8 4.4 %collective-permute-done.11.arrived = f32[32,2048]{1,0:T(8,128)S(1)} collective-permute-done((f32[32,2048]{1,0:T(8,128)S(1)}, f32[32,2048]{1,0:T(8,128)S(1)}, u32[]{:S(2)}, u32[]{:S(2)}) %collective-permute-start.11) | collective-permute-done | bytes 262176 | tf_op jit(solution)/shard_map/ppermute | solution.py:429
  139.8 6.1 %collective-permute-done.19.refs_2_.nearby = f32[32,2176]{1,0:T(8,128)S(1)} collective-permute-done((f32[32,2176]{1,0:T(8,128)S(1)}, f32[32,2176]{1,0:T(8,128)S(1)}, u32[]{:S(2)}, u32[]{:S(2)}) %collective-permute-start.19) | collective-permute-done | bytes 278560 | tf_op jit(solution)/shard_map/ppermute | solution.py:429
  145.9 4.4 %collective-permute-done.21.refs_2_.refs_1_ = f32[32,3072]{1,0:T(8,128)S(1)} collective-permute-done((f32[32,3072]{1,0:T(8,128)S(1)}, f32[32,3072]{1,0:T(8,128)S(1)}, u32[]{:S(2)}, u32[]{:S(2)}) %collective-permute-start.21) | collective-permute-done | bytes 393248 | tf_op jit(solution)/shard_map/ppermute | solution.py:429
  158.4 5.9 %mirror.3 = (f32[64,3072]{1,0:T(8,128)S(1)}, f32[64,3072]{1,0:T(8,128)S(1)}, f32[64,3072]{1,0:T(8,128)S(1)}) custom-call(s32[3]{0:T(128)S(1)} %pad_add_fusion.1.place, s32[24]{0:T(128)S(1)} %get-tuple-element.111.refs_3_.tile_ref, s32[24]{0:T(128)S(1)} %compare_convert_fusion.refs_4_.valid_ref, s32[24]{0:T(128)S(1)} %get-tuple-element.110.refs_5_.row_ref, ...), custom_call_target="tpu_custom_call" | custom-call | tf_op jit(solution)/shard_map/mirror/pallas_call | solution.py:161
  167.3 9.2 %collective-permute-done.25.refs_4_ = f32[32,3200]{1,0:T(8,128)S(1)} collective-permute-done((f32[32,3200]{1,0:T(8,128)S(1)}, f32[32,3200]{1,0:T(8,128)S(1)}, u32[]{:S(2)}, u32[]{:S(2)}) %collective-permute-start.25) | collective-permute-done | bytes 409632 | tf_op jit(solution)/shard_map/ppermute | solution.py:429
  180.0 4.5 %own.3.refs_6_ = f32[64,8192]{1,0:T(8,128)S(1)} custom-call(s32[3]{0:T(128)S(1)} %pad_add_fusion.1.place, s32[24]{0:T(128)S(1)} %get-tuple-element.111.refs_3_.tile_ref, s32[24]{0:T(128)S(1)} %compare_convert_fusion.refs_4_.valid_ref, s32[24]{0:T(128)S(1)} %get-tuple-element.110.refs_5_.row_ref, s32[24]{0:T(128)S(1)} %add_maximum_fusion.1.refs_6_.col_ref, ...), custom_call_target="tpu_custom_call" | custom-call | tf_op jit(solution)/shard_map/own/pallas_call | solution.py:189
  184.5 12.4 %collective-permute-done.27.refs_7_.refs_0_ = f32[64,3072]{1,0:T(8,128)S(1)} collective-permute-done((f32[64,3072]{1,0:T(8,128)S(1)}, f32[64,3072]{1,0:T(8,128)S(1)}, u32[]{:S(2)}, u32[]{:S(2)}) %collective-permute-start.27) | collective-permute-done | bytes 786464 | tf_op jit(solution)/shard_map/ppermute | solution.py:429
  197.0 8.9 %direct.3.start = f32[64,8192]{1,0:T(8,128)S(1)} custom-call(s32[3]{0:T(128)S(1)} %pad_add_fusion.1.place, s32[24]{0:T(128)S(1)} %get-tuple-element.111.refs_3_.tile_ref, s32[24]{0:T(128)S(1)} %compare_convert_fusion.refs_4_.valid_ref, s32[24]{0:T(128)S(1)} %get-tuple-element.110.refs_5_.row_ref, bf16[22,512,512]{2,1,0:T(8,128)(2,1)S(1)} %get-tuple-element.55.high, ...), custom_call_target="tpu_custom_call" | custom-call | tf_op jit(solution)/shard_map/direct/pallas_call | solution.py:223
  205.9 6.0 %collective-permute-done.29.refs_2_ = f32[64,3072]{1,0:T(8,128)S(1)} collective-permute-done((f32[64,3072]{1,0:T(8,128)S(1)}, f32[64,3072]{1,0:T(8,128)S(1)}, u32[]{:S(2)}, u32[]{:S(2)}) %collective-permute-start.29) | collective-permute-done | bytes 786464 | tf_op jit(solution)/shard_map/ppermute | solution.py:429
  220.2 6.9 %cholesky.2 = (f32[64,64]{1,0:T(8,128)}, f32[64,64]{1,0:T(8,128)S(1)}) custom-call(f32[64,64]{1,0:T(8,128)S(1)} %pad_maximum_fusion.gram), custom_call_target="tpu_custom_call" | custom-call | tf_op jit(solution)/shard_map/cholesky/pallas_call | solution.py:392
  235.4 3.8 %collective-permute-done.34.arrived = f32[32,1024]{1,0:T(8,128)S(1)} collective-permute-done((f32[32,1024]{1,0:T(8,128)S(1)}, f32[32,1024]{1,0:T(8,128)S(1)}, u32[]{:S(2)}, u32[]{:S(2)}) %collective-permute-start.34) | collective-permute-done | bytes 131104 | tf_op jit(solution)/shard_map/ppermute | solution.py:429
  253.4 5.4 %collective-permute-start.43 = (f32[32,2048]{1,0:T(8,128)S(1)}, f32[32,2048]{1,0:T(8,128)S(1)}, u32[]{:S(2)}, u32[]{:S(2)}) collective-permute-start(f32[32,2048]{1,0:T(8,128)S(1)} %pack.10), channel_id=1, source_target_pairs={{0,1},{1,0},{2,3},{3,2},{4,5},{5,4},{6,7},{7,6},{8,9},{9,8},{10,11... | collective-permute-start | bytes 786440 | tf_op jit(solution)/shard_map/ppermute | solution.py:429
  259.0 6.3 %cholesky.3 = (f32[64,64]{1,0:T(8,128)S(1)}, f32[64,64]{1,0:T(8,128)S(1)}) custom-call(f32[64,64]{1,0:T(8,128)S(1)} %add_add_fusion.gram), custom_call_target="tpu_custom_call" | custom-call | tf_op jit(solution)/shard_map/cholesky/pallas_call | solution.py:392
  266.8 3.4 %collective-permute-done.45.nearby = f32[32,2048]{1,0:T(8,128)S(1)} collective-permute-done((f32[32,2048]{1,0:T(8,128)S(1)}, f32[32,2048]{1,0:T(8,128)S(1)}, u32[]{:S(2)}, u32[]{:S(2)}) %collective-permute-start.45) | collective-permute-done | bytes 262176 | tf_op jit(solution)/shard_map/ppermute | solution.py:429
  (141 shorter events, 103.5 us)
Async XLA Ops:
  0.6 12.1 %collective-permute-start.3 = (f32[64,4096]{1,0:T(8,128)}, f32[64,4096]{1,0:T(8,128)S(1)}, u32[]{:S(2)}, u32[]{:S(2)}) collective-permute-start(f32[64,4096]{1,0:T(8,128)} %bitcast.23), channel_id=1, source_target_pairs={{0,4},{4,0},{8,12},{12,8},{16,20},{20,16},{24,28},{28,24},{1,5},{5... | collective-permute-start | bytes 3145736 | tf_op jit(solution)/shard_map/ppermute | solution.py:429
  17.4 20.7 %collective-permute-start.4 = (f32[64,3072]{1,0:T(8,128)}, f32[64,3072]{1,0:T(8,128)S(1)}, u32[]{:S(2)}, u32[]{:S(2)}) collective-permute-start(f32[64,3072]{1,0:T(8,128)} %get-tuple-element.57), channel_id=1, source_target_pairs={{0,8},{4,12},{8,0},{12,4},{16,24},{20,28},{24,16},{28,20},{1,9},{5... | collective-permute-start | bytes 2359304 | tf_op jit(solution)/shard_map/ppermute | solution.py:429
  18.1 52.6 %collective-permute-start.5 = (f32[64,3072]{1,0:T(8,128)}, f32[64,3072]{1,0:T(8,128)S(1)}, u32[]{:S(2)}, u32[]{:S(2)}) collective-permute-start(f32[64,3072]{1,0:T(8,128)} %copy-done.2), channel_id=1, source_target_pairs={{0,16},{4,20},{8,24},{12,28},{16,0},{20,4},{24,8},{28,12},{1,17},{... | collective-permute-start | bytes 2359304 | tf_op jit(solution)/shard_map/ppermute | solution.py:429
  18.1 52.6 %collective-permute-start.6 = (f32[64,3072]{1,0:T(8,128)}, f32[64,3072]{1,0:T(8,128)S(1)}, u32[]{:S(2)}, u32[]{:S(2)}) collective-permute-start(f32[64,3072]{1,0:T(8,128)} %copy-done.1), channel_id=1, source_target_pairs={{0,24},{4,28},{8,16},{12,20},{16,8},{20,12},{24,0},{28,4},{1,25},{... | collective-permute-start | bytes 2359304 | tf_op jit(solution)/shard_map/ppermute | solution.py:429
  35.2 51.6 %collective-permute-start.8 = (f32[64,3072]{1,0:T(8,128)S(1)}, f32[64,3072]{1,0:T(8,128)S(1)}, u32[]{:S(2)}, u32[]{:S(2)}) collective-permute-start(f32[64,3072]{1,0:T(8,128)S(1)} %get-tuple-element.61), channel_id=1, source_target_pairs={{0,16},{4,20},{8,24},{12,28},{16,0},{20,4},{24,8},{28,12},{1,17},{... | collective-permute-start | bytes 2359304 | tf_op jit(solution)/shard_map/ppermute | solution.py:429
  36.1 50.7 %collective-permute-start.9 = (f32[64,3072]{1,0:T(8,128)S(1)}, f32[64,3072]{1,0:T(8,128)S(1)}, u32[]{:S(2)}, u32[]{:S(2)}) collective-permute-start(f32[64,3072]{1,0:T(8,128)S(1)} %get-tuple-element.62), channel_id=1, source_target_pairs={{0,24},{4,28},{8,16},{12,20},{16,8},{20,12},{24,0},{28,4},{1,25},{... | collective-permute-start | bytes 2359304 | tf_op jit(solution)/shard_map/ppermute | solution.py:429
  38.1 48.7 %collective-permute-start.7 = (f32[64,3072]{1,0:T(8,128)S(1)}, f32[64,3072]{1,0:T(8,128)S(1)}, u32[]{:S(2)}, u32[]{:S(2)}) collective-permute-start(f32[64,3072]{1,0:T(8,128)S(1)} %get-tuple-element.60.refs_1_), channel_id=1, source_target_pairs={{0,8},{4,12},{8,0},{12,4},{16,24},{20,28},{24,16},{28,20},{1,9},{5... | collective-permute-start | bytes 2359304 | tf_op jit(solution)/shard_map/ppermute | solution.py:429
  110.5 9.7 %collective-permute-start.11 = (f32[32,2048]{1,0:T(8,128)S(1)}, f32[32,2048]{1,0:T(8,128)S(1)}, u32[]{:S(2)}, u32[]{:S(2)}) collective-permute-start(f32[32,2048]{1,0:T(8,128)S(1)} %get-tuple-element.66), channel_id=1, source_target_pairs={{0,1},{1,0},{2,3},{3,2},{4,5},{5,4},{6,7},{7,6},{8,9},{9,8},{10,11... | collective-permute-start | bytes 786440 | tf_op jit(solution)/shard_map/ppermute | solution.py:429
  115.1 10.0 %collective-permute-start.16 = (f32[32,2048]{1,0:T(8,128)S(1)}, f32[32,2048]{1,0:T(8,128)S(1)}, u32[]{:S(2)}, u32[]{:S(2)}) collective-permute-start(f32[32,2048]{1,0:T(8,128)S(1)} %pack.6), channel_id=1, source_target_pairs={{0,1},{1,0},{2,3},{3,2},{4,5},{5,4},{6,7},{7,6},{8,9},{9,8},{10,11... | collective-permute-start | bytes 786440 | tf_op jit(solution)/shard_map/ppermute | solution.py:429
  131.7 18.6 %collective-permute-start.21 = (f32[32,3072]{1,0:T(8,128)S(1)}, f32[32,3072]{1,0:T(8,128)S(1)}, u32[]{:S(2)}, u32[]{:S(2)}) collective-permute-start(f32[32,3072]{1,0:T(8,128)S(1)} %get-tuple-element.75), channel_id=1, source_target_pairs={{0,16},{4,20},{8,24},{12,28},{16,0},{20,4},{24,8},{28,12},{1,17},{... | collective-permute-start | bytes 1179656 | tf_op jit(solution)/shard_map/ppermute | solution.py:429
  132.3 18.1 %collective-permute-start.22 = (f32[32,3072]{1,0:T(8,128)S(1)}, f32[32,3072]{1,0:T(8,128)S(1)}, u32[]{:S(2)}, u32[]{:S(2)}) collective-permute-start(f32[32,3072]{1,0:T(8,128)S(1)} %get-tuple-element.76), channel_id=1, source_target_pairs={{0,24},{4,28},{8,16},{12,20},{16,8},{20,12},{24,0},{28,4},{1,25},{... | collective-permute-start | bytes 1179656 | tf_op jit(solution)/shard_map/ppermute | solution.py:429
  134.7 16.9 %collective-permute-start.20 = (f32[32,3072]{1,0:T(8,128)S(1)}, f32[32,3072]{1,0:T(8,128)S(1)}, u32[]{:S(2)}, u32[]{:S(2)}) collective-permute-start(f32[32,3072]{1,0:T(8,128)S(1)} %get-tuple-element.73), channel_id=1, source_target_pairs={{0,8},{4,12},{8,0},{12,4},{16,24},{20,28},{24,16},{28,20},{1,9},{5... | collective-permute-start | bytes 1179656 | tf_op jit(solution)/shard_map/ppermute | solution.py:429
  136.8 9.1 %collective-permute-start.19 = (f32[32,2176]{1,0:T(8,128)S(1)}, f32[32,2176]{1,0:T(8,128)S(1)}, u32[]{:S(2)}, u32[]{:S(2)}) collective-permute-start(f32[32,2176]{1,0:T(8,128)S(1)} %pack.8), channel_id=1, source_target_pairs={{0,1},{1,0},{2,3},{3,2},{4,5},{5,4},{6,7},{7,6},{8,9},{9,8},{10,11... | collective-permute-start | bytes 835592 | tf_op jit(solution)/shard_map/ppermute | solution.py:429
  154.9 12.4 %collective-permute-start.24 = (f32[32,3200]{1,0:T(8,128)S(1)}, f32[32,3200]{1,0:T(8,128)S(1)}, u32[]{:S(2)}, u32[]{:S(2)}) collective-permute-start(f32[32,3200]{1,0:T(8,128)S(1)} %get-tuple-element.78), channel_id=1, source_target_pairs={{0,8},{4,12},{8,0},{12,4},{16,24},{20,28},{24,16},{28,20},{1,9},{5... | collective-permute-start | bytes 1228808 | tf_op jit(solution)/shard_map/ppermute | solution.py:429
  156.5 20.0 %collective-permute-start.25 = (f32[32,3200]{1,0:T(8,128)S(1)}, f32[32,3200]{1,0:T(8,128)S(1)}, u32[]{:S(2)}, u32[]{:S(2)}) collective-permute-start(f32[32,3200]{1,0:T(8,128)S(1)} %get-tuple-element.79), channel_id=1, source_target_pairs={{0,16},{4,20},{8,24},{12,28},{16,0},{20,4},{24,8},{28,12},{1,17},{... | collective-permute-start | bytes 1228808 | tf_op jit(solution)/shard_map/ppermute | solution.py:429
  157.0 19.5 %collective-permute-start.26 = (f32[32,3200]{1,0:T(8,128)S(1)}, f32[32,3200]{1,0:T(8,128)S(1)}, u32[]{:S(2)}, u32[]{:S(2)}) collective-permute-start(f32[32,3200]{1,0:T(8,128)S(1)} %get-tuple-element.80), channel_id=1, source_target_pairs={{0,24},{4,28},{8,16},{12,20},{16,8},{20,12},{24,0},{28,4},{1,25},{... | collective-permute-start | bytes 1228808 | tf_op jit(solution)/shard_map/ppermute | solution.py:429
  176.5 20.5 %collective-permute-start.27 = (f32[64,3072]{1,0:T(8,128)S(1)}, f32[64,3072]{1,0:T(8,128)S(1)}, u32[]{:S(2)}, u32[]{:S(2)}) collective-permute-start(f32[64,3072]{1,0:T(8,128)S(1)} %get-tuple-element.84.refs_2_), channel_id=1, source_target_pairs={{0,8},{4,12},{8,0},{12,4},{16,24},{20,28},{24,16},{28,20},{1,9},{5... | collective-permute-start | bytes 2359304 | tf_op jit(solution)/shard_map/ppermute | solution.py:429
  177.0 34.9 %collective-permute-start.29 = (f32[64,3072]{1,0:T(8,128)S(1)}, f32[64,3072]{1,0:T(8,128)S(1)}, u32[]{:S(2)}, u32[]{:S(2)}) collective-permute-start(f32[64,3072]{1,0:T(8,128)S(1)} %get-tuple-element.88), channel_id=1, source_target_pairs={{0,24},{4,28},{8,16},{12,20},{16,8},{20,12},{24,0},{28,4},{1,25},{... | collective-permute-start | bytes 2359304 | tf_op jit(solution)/shard_map/ppermute | solution.py:429
  178.5 34.8 %collective-permute-start.28 = (f32[64,3072]{1,0:T(8,128)S(1)}, f32[64,3072]{1,0:T(8,128)S(1)}, u32[]{:S(2)}, u32[]{:S(2)}) collective-permute-start(f32[64,3072]{1,0:T(8,128)S(1)} %get-tuple-element.86), channel_id=1, source_target_pairs={{0,16},{4,20},{8,24},{12,28},{16,0},{20,4},{24,8},{28,12},{1,17},{... | collective-permute-start | bytes 2359304 | tf_op jit(solution)/shard_map/ppermute | solution.py:429
  218.0 9.2 %collective-permute-start.31 = (f32[32,2048]{1,0:T(8,128)S(1)}, f32[32,2048]{1,0:T(8,128)S(1)}, u32[]{:S(2)}, u32[]{:S(2)}) collective-permute-start(f32[32,2048]{1,0:T(8,128)S(1)} %get-tuple-element.94), channel_id=1, source_target_pairs={{0,1},{1,0},{2,3},{3,2},{4,5},{5,4},{6,7},{7,6},{8,9},{9,8},{10,11... | collective-permute-start | bytes 786440 | tf_op jit(solution)/shard_map/ppermute | solution.py:429
  218.1 14.2 %collective-permute-start.33 = (f32[32,2048]{1,0:T(8,128)S(1)}, f32[32,2048]{1,0:T(8,128)S(1)}, u32[]{:S(2)}, u32[]{:S(2)}) collective-permute-start(f32[32,2048]{1,0:T(8,128)S(1)} %get-tuple-element.98), channel_id=1, source_target_pairs={{0,1},{1,0},{2,3},{3,2},{4,5},{5,4},{6,7},{7,6},{8,9},{9,8},{10,11... | collective-permute-start | bytes 786440 | tf_op jit(solution)/shard_map/ppermute | solution.py:429
  249.6 9.3 %collective-permute-start.41 = (f32[64,64]{1,0:T(8,128)S(1)}, f32[64,64]{1,0:T(8,128)S(1)}, u32[]{:S(2)}, u32[]{:S(2)}) collective-permute-start(f32[64,64]{1,0:T(8,128)S(1)} %add.77), channel_id=1, source_target_pairs={{0,24},{4,28},{8,16},{12,20},{16,8},{20,12},{24,0},{28,4},{1,25},{... | collective-permute-start | bytes 49160 | tf_op jit(solution)/shard_map/ppermute | solution.py:429
  253.4 12.8 %collective-permute-start.43 = (f32[32,2048]{1,0:T(8,128)S(1)}, f32[32,2048]{1,0:T(8,128)S(1)}, u32[]{:S(2)}, u32[]{:S(2)}) collective-permute-start(f32[32,2048]{1,0:T(8,128)S(1)} %pack.10), channel_id=1, source_target_pairs={{0,1},{1,0},{2,3},{3,2},{4,5},{5,4},{6,7},{7,6},{8,9},{9,8},{10,11... | collective-permute-start | bytes 786440 | tf_op jit(solution)/shard_map/ppermute | solution.py:429
  258.9 11.3 %collective-permute-start.45 = (f32[32,2048]{1,0:T(8,128)S(1)}, f32[32,2048]{1,0:T(8,128)S(1)}, u32[]{:S(2)}, u32[]{:S(2)}) collective-permute-start(f32[32,2048]{1,0:T(8,128)S(1)} %pack.11), channel_id=1, source_target_pairs={{0,1},{1,0},{2,3},{3,2},{4,5},{5,4},{6,7},{7,6},{8,9},{9,8},{10,11... | collective-permute-start | bytes 786440 | tf_op jit(solution)/shard_map/ppermute | solution.py:429
  (25 other events, 129.2 us)

commit v5 on v4

--- a/solution.py
+++ b/solution.py
@@ -378,12 +378,12 @@
     eye = (row[:, :n] == lane[:, :n]).astype(F32)
     work = jnp.concatenate([gram[...], eye], axis=1)
     for j in range(n):
-        scale = 1.0 / jnp.sqrt(work[j : j + 1, j : j + 1])
-        pivot_row = work[j : j + 1, :] * scale
-        column = work[:, j : j + 1] * scale
-        work = jnp.where(row == j, pivot_row, jnp.where(row > j, work - column * pivot_row, work))
-    upper = row[:, :n] <= lane[:, :n]
-    factor_t[...] = jnp.where(upper, work[:, :n], 0.0)
+        column = jnp.broadcast_to(work[:, j : j + 1], (n, 2 * n))
+        pivot_row = work[j : j + 1, :] * (1.0 / column[j : j + 1, :])
+        work = work - jnp.where(row > j, column, 0.0) * pivot_row
+    pivots = jnp.sum(jnp.where(row == lane, work, 0.0), axis=1, keepdims=True)
+    work = work * (1.0 / jnp.sqrt(pivots))
+    factor_t[...] = jnp.where(row[:, :n] <= lane[:, :n], work[:, :n], 0.0)
     inverse[...] = jnp.where(row[:, :n] >= lane[:, :n], work[:, n:], 0.0)
 
 

time: 273 us -> 273 us (level)
  transfers between devices with their start and end apart: 46 -> 46, of which waited for: 30 -> 31; matrix products, arithmetic and copies ran while one was open for 2% -> 2% of each run, Pallas kernels for 23% -> 22%
where the time goes in v5:
time: 273 us
  waiting for transfers between devices  131 us (48%)
  Pallas kernels  70.8 us (26%)
  starting transfers between devices  61.8 us (23%)
  local copies, waits for them, and re-layouts  5.17 us (2%)
    ppermute x46, waiting for transfers between devices, swap(): return lax.ppermute(x, axis, [(i, i ^ k) for i in range(size)])  131 us
    ppermute x46, starting transfers between devices, swap(): return lax.ppermute(x, axis, [(i, i ^ k) for i in range(size)])  61.8 us
    pallas_call x2, Pallas kernels, direct(): pl.pallas_call(functools.partial(direct_kernel, chips, group, parts), in_...  17.8 us
    pallas_call x2, Pallas kernels, mirror(): pl.pallas_call(functools.partial(mirror_kernel, chips, group, parts), in_...  11.9 us
    pallas_call x2, Pallas kernels, cholesky(): pl.pallas_call(cholesky_kernel, out_shape=[shape(n, n)] * 2, compiler_par...  11.6 us
    pallas_call x2, Pallas kernels, own(): pl.pallas_call(functools.partial(own_kernel, group, parts), in_specs=[SME...  9.14 us
    pallas_call x1, Pallas kernels, load(): pl.pallas_call(load_kernel, in_specs=[ANY] * (1 + len(after)), out_specs=...  8.07 us
  transfers between devices with their start and end apart: 46, of which 31 were waited for; matrix products, arithmetic and copies ran while one was open for 2% of the time, Pallas kernels for 22%

profile of v5, /device:TPU:0, one launch (start us, length us, event | category | flops | bytes accessed | tf_op | source)
XLA Modules:
  0.0 272.7 jit_solution(3175237602845310027)
XLA Ops:
  21.0 8.1 %load.1 = (bf16[22,512,512]{2,1,0:T(8,128)(2,1)S(1)}, bf16[22,512,512]{2,1,0:T(8,128)(2,1)S(1)}) custom-call(f32[22,512,512]{2,1,0:T(8,128)} %tiles.1, f32[64,8192]{1,0:T(8,128)S(1)} %get-tuple-element.54.refs_0_, s32[24]{0:T(128)S(1)} %reshape.38.refs_1_.flag, s32[24]{0:T(128)S(1)} %max.9.wanted.refs_2_, s32[24]{0:T(128)S(1)} %get-tuple-element.111.refs_3_.tile_ref, ...), custom_call_target="tpu_custom_call" | custom-call | tf_op jit(solution)/shard_map/load/pallas_call | solution.py:65
  29.1 6.1 %mirror.2 = (f32[64,3072]{1,0:T(8,128)S(1)}, f32[64,3072]{1,0:T(8,128)S(1)}, f32[64,3072]{1,0:T(8,128)S(1)}) custom-call(s32[3]{0:T(128)S(1)} %pad_add_fusion.1.place, s32[24]{0:T(128)S(1)} %get-tuple-element.111.refs_3_.tile_ref, s32[24]{0:T(128)S(1)} %compare_convert_fusion.refs_4_.valid_ref, s32[24]{0:T(128)S(1)} %get-tuple-element.110.refs_5_.row_ref, ...), custom_call_target="tpu_custom_call" | custom-call | tf_op jit(solution)/shard_map/mirror/pallas_call | solution.py:161
  38.7 4.6 %own.2.refs_3_ = f32[64,8192]{1,0:T(8,128)S(1)} custom-call(s32[3]{0:T(128)S(1)} %pad_add_fusion.1.place, s32[24]{0:T(128)S(1)} %get-tuple-element.111.refs_3_.tile_ref, s32[24]{0:T(128)S(1)} %compare_convert_fusion.refs_4_.valid_ref, s32[24]{0:T(128)S(1)} %get-tuple-element.110.refs_5_.row_ref, s32[24]{0:T(128)S(1)} %add_maximum_fusion.1.refs_6_.col_ref, ...), custom_call_target="tpu_custom_call" | custom-call | tf_op jit(solution)/shard_map/own/pallas_call | solution.py:189
  43.3 27.4 %collective-permute-done.5.refs_1_ = f32[64,3072]{1,0:T(8,128)S(1)} collective-permute-done((f32[64,3072]{1,0:T(8,128)}, f32[64,3072]{1,0:T(8,128)S(1)}, u32[]{:S(2)}, u32[]{:S(2)}) %collective-permute-start.5) | collective-permute-done | bytes 786464 | tf_op jit(solution)/shard_map/ppermute | solution.py:429
  70.7 8.9 %direct.2.start = f32[64,8192]{1,0:T(8,128)S(1)} custom-call(s32[3]{0:T(128)S(1)} %pad_add_fusion.1.place, s32[24]{0:T(128)S(1)} %get-tuple-element.111.refs_3_.tile_ref, s32[24]{0:T(128)S(1)} %compare_convert_fusion.refs_4_.valid_ref, s32[24]{0:T(128)S(1)} %get-tuple-element.110.refs_5_.row_ref, bf16[22,512,512]{2,1,0:T(8,128)(2,1)S(1)} %get-tuple-element.55.high, ...), custom_call_target="tpu_custom_call" | custom-call | tf_op jit(solution)/shard_map/direct/pallas_call | solution.py:223
  79.6 7.2 %collective-permute-done.8.refs_1_ = f32[64,3072]{1,0:T(8,128)S(1)} collective-permute-done((f32[64,3072]{1,0:T(8,128)S(1)}, f32[64,3072]{1,0:T(8,128)S(1)}, u32[]{:S(2)}, u32[]{:S(2)}) %collective-permute-start.8) | collective-permute-done | bytes 786464 | tf_op jit(solution)/shard_map/ppermute | solution.py:429
  93.1 6.8 %collective-permute-done.13.arrived = f32[32,2048]{1,0:T(8,128)S(1)} collective-permute-done((f32[32,2048]{1,0:T(8,128)S(1)}, f32[32,2048]{1,0:T(8,128)S(1)}, u32[]{:S(2)}, u32[]{:S(2)}) %collective-permute-start.13) | collective-permute-done | bytes 262176 | tf_op jit(solution)/shard_map/ppermute | solution.py:429
  100.0 3.7 %collective-permute-start.14 = (f32[32,1024]{1,0:T(8,128)S(1)}, f32[32,1024]{1,0:T(8,128)S(1)}, u32[]{:S(2)}, u32[]{:S(2)}) collective-permute-start(f32[32,1024]{1,0:T(8,128)S(1)} %get-tuple-element.72), channel_id=1, source_target_pairs={{0,3},{1,2},{2,1},{3,0},{4,7},{5,6},{6,5},{7,4},{8,11},{9,10},{10,... | collective-permute-start | bytes 393224 | tf_op jit(solution)/shard_map/ppermute | solution.py:429
  106.9 3.7 %collective-permute-start.15 = (f32[32,1024]{1,0:T(8,128)S(1)}, f32[32,1024]{1,0:T(8,128)S(1)}, u32[]{:S(2)}, u32[]{:S(2)}) collective-permute-start(f32[32,1024]{1,0:T(8,128)S(1)} %total.4.refs_0_.mine), channel_id=1, source_target_pairs={{0,3},{1,2},{2,1},{3,0},{4,7},{5,6},{6,5},{7,4},{8,11},{9,10},{10,... | collective-permute-start | bytes 393224 | tf_op jit(solution)/shard_map/ppermute | solution.py:429
  111.0 4.1 %collective-permute-done.15.refs_0_.refs_1_.across = f32[32,1024]{1,0:T(8,128)S(1)} collective-permute-done((f32[32,1024]{1,0:T(8,128)S(1)}, f32[32,1024]{1,0:T(8,128)S(1)}, u32[]{:S(2)}, u32[]{:S(2)}) %collective-permute-start.15) | collective-permute-done | bytes 131104 | tf_op jit(solution)/shard_map/ppermute | solution.py:429
  115.9 4.4 %collective-permute-done.11.arrived = f32[32,2048]{1,0:T(8,128)S(1)} collective-permute-done((f32[32,2048]{1,0:T(8,128)S(1)}, f32[32,2048]{1,0:T(8,128)S(1)}, u32[]{:S(2)}, u32[]{:S(2)}) %collective-permute-start.11) | collective-permute-done | bytes 262176 | tf_op jit(solution)/shard_map/ppermute | solution.py:429
  139.8 6.1 %collective-permute-done.19.refs_2_.nearby = f32[32,2176]{1,0:T(8,128)S(1)} collective-permute-done((f32[32,2176]{1,0:T(8,128)S(1)}, f32[32,2176]{1,0:T(8,128)S(1)}, u32[]{:S(2)}, u32[]{:S(2)}) %collective-permute-start.19) | collective-permute-done | bytes 278560 | tf_op jit(solution)/shard_map/ppermute | solution.py:429
  145.9 4.4 %collective-permute-done.21.refs_2_.refs_1_ = f32[32,3072]{1,0:T(8,128)S(1)} collective-permute-done((f32[32,3072]{1,0:T(8,128)S(1)}, f32[32,3072]{1,0:T(8,128)S(1)}, u32[]{:S(2)}, u32[]{:S(2)}) %collective-permute-start.21) | collective-permute-done | bytes 393248 | tf_op jit(solution)/shard_map/ppermute | solution.py:429
  158.4 5.9 %mirror.3 = (f32[64,3072]{1,0:T(8,128)S(1)}, f32[64,3072]{1,0:T(8,128)S(1)}, f32[64,3072]{1,0:T(8,128)S(1)}) custom-call(s32[3]{0:T(128)S(1)} %pad_add_fusion.1.place, s32[24]{0:T(128)S(1)} %get-tuple-element.111.refs_3_.tile_ref, s32[24]{0:T(128)S(1)} %compare_convert_fusion.refs_4_.valid_ref, s32[24]{0:T(128)S(1)} %get-tuple-element.110.refs_5_.row_ref, ...), custom_call_target="tpu_custom_call" | custom-call | tf_op jit(solution)/shard_map/mirror/pallas_call | solution.py:161
  167.3 9.2 %collective-permute-done.25.refs_4_ = f32[32,3200]{1,0:T(8,128)S(1)} collective-permute-done((f32[32,3200]{1,0:T(8,128)S(1)}, f32[32,3200]{1,0:T(8,128)S(1)}, u32[]{:S(2)}, u32[]{:S(2)}) %collective-permute-start.25) | collective-permute-done | bytes 409632 | tf_op jit(solution)/shard_map/ppermute | solution.py:429
  180.0 4.5 %own.3.refs_6_ = f32[64,8192]{1,0:T(8,128)S(1)} custom-call(s32[3]{0:T(128)S(1)} %pad_add_fusion.1.place, s32[24]{0:T(128)S(1)} %get-tuple-element.111.refs_3_.tile_ref, s32[24]{0:T(128)S(1)} %compare_convert_fusion.refs_4_.valid_ref, s32[24]{0:T(128)S(1)} %get-tuple-element.110.refs_5_.row_ref, s32[24]{0:T(128)S(1)} %add_maximum_fusion.1.refs_6_.col_ref, ...), custom_call_target="tpu_custom_call" | custom-call | tf_op jit(solution)/shard_map/own/pallas_call | solution.py:189
  184.5 12.4 %collective-permute-done.27.refs_7_.refs_0_ = f32[64,3072]{1,0:T(8,128)S(1)} collective-permute-done((f32[64,3072]{1,0:T(8,128)S(1)}, f32[64,3072]{1,0:T(8,128)S(1)}, u32[]{:S(2)}, u32[]{:S(2)}) %collective-permute-start.27) | collective-permute-done | bytes 786464 | tf_op jit(solution)/shard_map/ppermute | solution.py:429
  196.9 8.9 %direct.3.start = f32[64,8192]{1,0:T(8,128)S(1)} custom-call(s32[3]{0:T(128)S(1)} %pad_add_fusion.1.place, s32[24]{0:T(128)S(1)} %get-tuple-element.111.refs_3_.tile_ref, s32[24]{0:T(128)S(1)} %compare_convert_fusion.refs_4_.valid_ref, s32[24]{0:T(128)S(1)} %get-tuple-element.110.refs_5_.row_ref, bf16[22,512,512]{2,1,0:T(8,128)(2,1)S(1)} %get-tuple-element.55.high, ...), custom_call_target="tpu_custom_call" | custom-call | tf_op jit(solution)/shard_map/direct/pallas_call | solution.py:223
  205.9 6.0 %collective-permute-done.29.refs_2_ = f32[64,3072]{1,0:T(8,128)S(1)} collective-permute-done((f32[64,3072]{1,0:T(8,128)S(1)}, f32[64,3072]{1,0:T(8,128)S(1)}, u32[]{:S(2)}, u32[]{:S(2)}) %collective-permute-start.29) | collective-permute-done | bytes 786464 | tf_op jit(solution)/shard_map/ppermute | solution.py:429
  220.2 6.1 %cholesky.2 = (f32[64,64]{1,0:T(8,128)}, f32[64,64]{1,0:T(8,128)S(1)}) custom-call(f32[64,64]{1,0:T(8,128)S(1)} %pad_maximum_fusion.gram), custom_call_target="tpu_custom_call" | custom-call | tf_op jit(solution)/shard_map/cholesky/pallas_call | solution.py:392
  235.4 3.9 %collective-permute-done.34.arrived = f32[32,1024]{1,0:T(8,128)S(1)} collective-permute-done((f32[32,1024]{1,0:T(8,128)S(1)}, f32[32,1024]{1,0:T(8,128)S(1)}, u32[]{:S(2)}, u32[]{:S(2)}) %collective-permute-start.34) | collective-permute-done | bytes 131104 | tf_op jit(solution)/shard_map/ppermute | solution.py:429
  253.5 5.4 %collective-permute-start.43 = (f32[32,2048]{1,0:T(8,128)S(1)}, f32[32,2048]{1,0:T(8,128)S(1)}, u32[]{:S(2)}, u32[]{:S(2)}) collective-permute-start(f32[32,2048]{1,0:T(8,128)S(1)} %pack.10), channel_id=1, source_target_pairs={{0,1},{1,0},{2,3},{3,2},{4,5},{5,4},{6,7},{7,6},{8,9},{9,8},{10,11... | collective-permute-start | bytes 786440 | tf_op jit(solution)/shard_map/ppermute | solution.py:429
  259.0 5.5 %cholesky.3 = (f32[64,64]{1,0:T(8,128)S(1)}, f32[64,64]{1,0:T(8,128)S(1)}) custom-call(f32[64,64]{1,0:T(8,128)S(1)} %add_add_fusion.gram), custom_call_target="tpu_custom_call" | custom-call | tf_op jit(solution)/shard_map/cholesky/pallas_call | solution.py:392
  266.7 3.5 %collective-permute-done.45.nearby = f32[32,2048]{1,0:T(8,128)S(1)} collective-permute-done((f32[32,2048]{1,0:T(8,128)S(1)}, f32[32,2048]{1,0:T(8,128)S(1)}, u32[]{:S(2)}, u32[]{:S(2)}) %collective-permute-start.45) | collective-permute-done | bytes 262176 | tf_op jit(solution)/shard_map/ppermute | solution.py:429
  (141 shorter events, 104.9 us)
Async XLA Ops:
  0.6 12.1 %collective-permute-start.3 = (f32[64,4096]{1,0:T(8,128)}, f32[64,4096]{1,0:T(8,128)S(1)}, u32[]{:S(2)}, u32[]{:S(2)}) collective-permute-start(f32[64,4096]{1,0:T(8,128)} %bitcast.23), channel_id=1, source_target_pairs={{0,4},{4,0},{8,12},{12,8},{16,20},{20,16},{24,28},{28,24},{1,5},{5... | collective-permute-start | bytes 3145736 | tf_op jit(solution)/shard_map/ppermute | solution.py:429
  17.4 20.7 %collective-permute-start.4 = (f32[64,3072]{1,0:T(8,128)}, f32[64,3072]{1,0:T(8,128)S(1)}, u32[]{:S(2)}, u32[]{:S(2)}) collective-permute-start(f32[64,3072]{1,0:T(8,128)} %get-tuple-element.57), channel_id=1, source_target_pairs={{0,8},{4,12},{8,0},{12,4},{16,24},{20,28},{24,16},{28,20},{1,9},{5... | collective-permute-start | bytes 2359304 | tf_op jit(solution)/shard_map/ppermute | solution.py:429
  18.1 52.6 %collective-permute-start.5 = (f32[64,3072]{1,0:T(8,128)}, f32[64,3072]{1,0:T(8,128)S(1)}, u32[]{:S(2)}, u32[]{:S(2)}) collective-permute-start(f32[64,3072]{1,0:T(8,128)} %copy-done.2), channel_id=1, source_target_pairs={{0,16},{4,20},{8,24},{12,28},{16,0},{20,4},{24,8},{28,12},{1,17},{... | collective-permute-start | bytes 2359304 | tf_op jit(solution)/shard_map/ppermute | solution.py:429
  18.1 52.6 %collective-permute-start.6 = (f32[64,3072]{1,0:T(8,128)}, f32[64,3072]{1,0:T(8,128)S(1)}, u32[]{:S(2)}, u32[]{:S(2)}) collective-permute-start(f32[64,3072]{1,0:T(8,128)} %copy-done.1), channel_id=1, source_target_pairs={{0,24},{4,28},{8,16},{12,20},{16,8},{20,12},{24,0},{28,4},{1,25},{... | collective-permute-start | bytes 2359304 | tf_op jit(solution)/shard_map/ppermute | solution.py:429
  35.2 51.6 %collective-permute-start.8 = (f32[64,3072]{1,0:T(8,128)S(1)}, f32[64,3072]{1,0:T(8,128)S(1)}, u32[]{:S(2)}, u32[]{:S(2)}) collective-permute-start(f32[64,3072]{1,0:T(8,128)S(1)} %get-tuple-element.61), channel_id=1, source_target_pairs={{0,16},{4,20},{8,24},{12,28},{16,0},{20,4},{24,8},{28,12},{1,17},{... | collective-permute-start | bytes 2359304 | tf_op jit(solution)/shard_map/ppermute | solution.py:429
  35.7 51.1 %collective-permute-start.9 = (f32[64,3072]{1,0:T(8,128)S(1)}, f32[64,3072]{1,0:T(8,128)S(1)}, u32[]{:S(2)}, u32[]{:S(2)}) collective-permute-start(f32[64,3072]{1,0:T(8,128)S(1)} %get-tuple-element.62), channel_id=1, source_target_pairs={{0,24},{4,28},{8,16},{12,20},{16,8},{20,12},{24,0},{28,4},{1,25},{... | collective-permute-start | bytes 2359304 | tf_op jit(solution)/shard_map/ppermute | solution.py:429
  38.1 48.7 %collective-permute-start.7 = (f32[64,3072]{1,0:T(8,128)S(1)}, f32[64,3072]{1,0:T(8,128)S(1)}, u32[]{:S(2)}, u32[]{:S(2)}) collective-permute-start(f32[64,3072]{1,0:T(8,128)S(1)} %get-tuple-element.60.refs_1_), channel_id=1, source_target_pairs={{0,8},{4,12},{8,0},{12,4},{16,24},{20,28},{24,16},{28,20},{1,9},{5... | collective-permute-start | bytes 2359304 | tf_op jit(solution)/shard_map/ppermute | solution.py:429
  110.5 9.7 %collective-permute-start.11 = (f32[32,2048]{1,0:T(8,128)S(1)}, f32[32,2048]{1,0:T(8,128)S(1)}, u32[]{:S(2)}, u32[]{:S(2)}) collective-permute-start(f32[32,2048]{1,0:T(8,128)S(1)} %get-tuple-element.66), channel_id=1, source_target_pairs={{0,1},{1,0},{2,3},{3,2},{4,5},{5,4},{6,7},{7,6},{8,9},{9,8},{10,11... | collective-permute-start | bytes 786440 | tf_op jit(solution)/shard_map/ppermute | solution.py:429
  115.1 10.0 %collective-permute-start.16 = (f32[32,2048]{1,0:T(8,128)S(1)}, f32[32,2048]{1,0:T(8,128)S(1)}, u32[]{:S(2)}, u32[]{:S(2)}) collective-permute-start(f32[32,2048]{1,0:T(8,128)S(1)} %pack.6), channel_id=1, source_target_pairs={{0,1},{1,0},{2,3},{3,2},{4,5},{5,4},{6,7},{7,6},{8,9},{9,8},{10,11... | collective-permute-start | bytes 786440 | tf_op jit(solution)/shard_map/ppermute | solution.py:429
  131.8 18.6 %collective-permute-start.21 = (f32[32,3072]{1,0:T(8,128)S(1)}, f32[32,3072]{1,0:T(8,128)S(1)}, u32[]{:S(2)}, u32[]{:S(2)}) collective-permute-start(f32[32,3072]{1,0:T(8,128)S(1)} %get-tuple-element.75), channel_id=1, source_target_pairs={{0,16},{4,20},{8,24},{12,28},{16,0},{20,4},{24,8},{28,12},{1,17},{... | collective-permute-start | bytes 1179656 | tf_op jit(solution)/shard_map/ppermute | solution.py:429
  132.3 18.1 %collective-permute-start.22 = (f32[32,3072]{1,0:T(8,128)S(1)}, f32[32,3072]{1,0:T(8,128)S(1)}, u32[]{:S(2)}, u32[]{:S(2)}) collective-permute-start(f32[32,3072]{1,0:T(8,128)S(1)} %get-tuple-element.76), channel_id=1, source_target_pairs={{0,24},{4,28},{8,16},{12,20},{16,8},{20,12},{24,0},{28,4},{1,25},{... | collective-permute-start | bytes 1179656 | tf_op jit(solution)/shard_map/ppermute | solution.py:429
  134.7 16.9 %collective-permute-start.20 = (f32[32,3072]{1,0:T(8,128)S(1)}, f32[32,3072]{1,0:T(8,128)S(1)}, u32[]{:S(2)}, u32[]{:S(2)}) collective-permute-start(f32[32,3072]{1,0:T(8,128)S(1)} %get-tuple-element.73), channel_id=1, source_target_pairs={{0,8},{4,12},{8,0},{12,4},{16,24},{20,28},{24,16},{28,20},{1,9},{5... | collective-permute-start | bytes 1179656 | tf_op jit(solution)/shard_map/ppermute | solution.py:429
  136.8 9.1 %collective-permute-start.19 = (f32[32,2176]{1,0:T(8,128)S(1)}, f32[32,2176]{1,0:T(8,128)S(1)}, u32[]{:S(2)}, u32[]{:S(2)}) collective-permute-start(f32[32,2176]{1,0:T(8,128)S(1)} %pack.8), channel_id=1, source_target_pairs={{0,1},{1,0},{2,3},{3,2},{4,5},{5,4},{6,7},{7,6},{8,9},{9,8},{10,11... | collective-permute-start | bytes 835592 | tf_op jit(solution)/shard_map/ppermute | solution.py:429
  154.9 12.4 %collective-permute-start.24 = (f32[32,3200]{1,0:T(8,128)S(1)}, f32[32,3200]{1,0:T(8,128)S(1)}, u32[]{:S(2)}, u32[]{:S(2)}) collective-permute-start(f32[32,3200]{1,0:T(8,128)S(1)} %get-tuple-element.78), channel_id=1, source_target_pairs={{0,8},{4,12},{8,0},{12,4},{16,24},{20,28},{24,16},{28,20},{1,9},{5... | collective-permute-start | bytes 1228808 | tf_op jit(solution)/shard_map/ppermute | solution.py:429
  156.5 20.0 %collective-permute-start.25 = (f32[32,3200]{1,0:T(8,128)S(1)}, f32[32,3200]{1,0:T(8,128)S(1)}, u32[]{:S(2)}, u32[]{:S(2)}) collective-permute-start(f32[32,3200]{1,0:T(8,128)S(1)} %get-tuple-element.79), channel_id=1, source_target_pairs={{0,16},{4,20},{8,24},{12,28},{16,0},{20,4},{24,8},{28,12},{1,17},{... | collective-permute-start | bytes 1228808 | tf_op jit(solution)/shard_map/ppermute | solution.py:429
  157.0 19.5 %collective-permute-start.26 = (f32[32,3200]{1,0:T(8,128)S(1)}, f32[32,3200]{1,0:T(8,128)S(1)}, u32[]{:S(2)}, u32[]{:S(2)}) collective-permute-start(f32[32,3200]{1,0:T(8,128)S(1)} %get-tuple-element.80), channel_id=1, source_target_pairs={{0,24},{4,28},{8,16},{12,20},{16,8},{20,12},{24,0},{28,4},{1,25},{... | collective-permute-start | bytes 1228808 | tf_op jit(solution)/shard_map/ppermute | solution.py:429
  176.5 20.5 %collective-permute-start.27 = (f32[64,3072]{1,0:T(8,128)S(1)}, f32[64,3072]{1,0:T(8,128)S(1)}, u32[]{:S(2)}, u32[]{:S(2)}) collective-permute-start(f32[64,3072]{1,0:T(8,128)S(1)} %get-tuple-element.84.refs_2_), channel_id=1, source_target_pairs={{0,8},{4,12},{8,0},{12,4},{16,24},{20,28},{24,16},{28,20},{1,9},{5... | collective-permute-start | bytes 2359304 | tf_op jit(solution)/shard_map/ppermute | solution.py:429
  177.0 34.9 %collective-permute-start.29 = (f32[64,3072]{1,0:T(8,128)S(1)}, f32[64,3072]{1,0:T(8,128)S(1)}, u32[]{:S(2)}, u32[]{:S(2)}) collective-permute-start(f32[64,3072]{1,0:T(8,128)S(1)} %get-tuple-element.88), channel_id=1, source_target_pairs={{0,24},{4,28},{8,16},{12,20},{16,8},{20,12},{24,0},{28,4},{1,25},{... | collective-permute-start | bytes 2359304 | tf_op jit(solution)/shard_map/ppermute | solution.py:429
  178.5 34.8 %collective-permute-start.28 = (f32[64,3072]{1,0:T(8,128)S(1)}, f32[64,3072]{1,0:T(8,128)S(1)}, u32[]{:S(2)}, u32[]{:S(2)}) collective-permute-start(f32[64,3072]{1,0:T(8,128)S(1)} %get-tuple-element.86), channel_id=1, source_target_pairs={{0,16},{4,20},{8,24},{12,28},{16,0},{20,4},{24,8},{28,12},{1,17},{... | collective-permute-start | bytes 2359304 | tf_op jit(solution)/shard_map/ppermute | solution.py:429
  218.0 9.2 %collective-permute-start.31 = (f32[32,2048]{1,0:T(8,128)S(1)}, f32[32,2048]{1,0:T(8,128)S(1)}, u32[]{:S(2)}, u32[]{:S(2)}) collective-permute-start(f32[32,2048]{1,0:T(8,128)S(1)} %get-tuple-element.94), channel_id=1, source_target_pairs={{0,1},{1,0},{2,3},{3,2},{4,5},{5,4},{6,7},{7,6},{8,9},{9,8},{10,11... | collective-permute-start | bytes 786440 | tf_op jit(solution)/shard_map/ppermute | solution.py:429
  218.1 14.3 %collective-permute-start.33 = (f32[32,2048]{1,0:T(8,128)S(1)}, f32[32,2048]{1,0:T(8,128)S(1)}, u32[]{:S(2)}, u32[]{:S(2)}) collective-permute-start(f32[32,2048]{1,0:T(8,128)S(1)} %get-tuple-element.98), channel_id=1, source_target_pairs={{0,1},{1,0},{2,3},{3,2},{4,5},{5,4},{6,7},{7,6},{8,9},{9,8},{10,11... | collective-permute-start | bytes 786440 | tf_op jit(solution)/shard_map/ppermute | solution.py:429
  249.7 9.2 %collective-permute-start.41 = (f32[64,64]{1,0:T(8,128)S(1)}, f32[64,64]{1,0:T(8,128)S(1)}, u32[]{:S(2)}, u32[]{:S(2)}) collective-permute-start(f32[64,64]{1,0:T(8,128)S(1)} %add.77), channel_id=1, source_target_pairs={{0,24},{4,28},{8,16},{12,20},{16,8},{20,12},{24,0},{28,4},{1,25},{... | collective-permute-start | bytes 49160 | tf_op jit(solution)/shard_map/ppermute | solution.py:429
  253.5 12.6 %collective-permute-start.43 = (f32[32,2048]{1,0:T(8,128)S(1)}, f32[32,2048]{1,0:T(8,128)S(1)}, u32[]{:S(2)}, u32[]{:S(2)}) collective-permute-start(f32[32,2048]{1,0:T(8,128)S(1)} %pack.10), channel_id=1, source_target_pairs={{0,1},{1,0},{2,3},{3,2},{4,5},{5,4},{6,7},{7,6},{8,9},{9,8},{10,11... | collective-permute-start | bytes 786440 | tf_op jit(solution)/shard_map/ppermute | solution.py:429
  258.9 11.3 %collective-permute-start.45 = (f32[32,2048]{1,0:T(8,128)S(1)}, f32[32,2048]{1,0:T(8,128)S(1)}, u32[]{:S(2)}, u32[]{:S(2)}) collective-permute-start(f32[32,2048]{1,0:T(8,128)S(1)} %pack.11), channel_id=1, source_target_pairs={{0,1},{1,0},{2,3},{3,2},{4,5},{5,4},{6,7},{7,6},{8,9},{9,8},{10,11... | collective-permute-start | bytes 786440 | tf_op jit(solution)/shard_map/ppermute | solution.py:429
  (25 other events, 129.1 us)

commit v6 on v5

--- a/solution.py
+++ b/solution.py
@@ -536,7 +536,7 @@
     gram_0 = gram_of([jnp.dot(inverse, whole, precision=HIGHEST)])
     gram_1 = all_sum(gram_0, "by", by_all)
     gram_2 = all_sum(gram_1, "wide", core_pair)
-    nearby = swap(pack([(quarters[0], *every)], [(gate(across, gram_0), *every)]), "by", 1)
+    nearby = swap(pack([(quarters[0], *every)], [(across, *every)]), "by", 1)
     pieces = [join(place, quarters[0], across, nearby)]
     across = swap(gate(quarters[1], gram_0), "by", 3)
     nearby = swap(pack([(quarters[1], *every)], [(gate(across, gram_1), *every)]), "by", 1)

time: 273 us -> 270 us (0.989)
  waiting for transfers between devices: 131 us -> 127 us
    ppermute x46, waiting for transfers between devices: 131 us -> 127 us  [swap(): return lax.ppermute(x, axis, [(i, i ^ k) for i in range(size)])]
  transfers between devices with their start and end apart: 46 -> 46, of which waited for: 31 -> 29; matrix products, arithmetic and copies ran while one was open for 2% -> 2% of each run, Pallas kernels for 22% -> 22%
where the time goes in v6:
time: 270 us
  waiting for transfers between devices  127 us (47%)
  Pallas kernels  71.1 us (26%)
  starting transfers between devices  62.4 us (23%)
  local copies, waits for them, and re-layouts  5.17 us (2%)
    ppermute x46, waiting for transfers between devices, swap(): return lax.ppermute(x, axis, [(i, i ^ k) for i in range(size)])  127 us
    ppermute x46, starting transfers between devices, swap(): return lax.ppermute(x, axis, [(i, i ^ k) for i in range(size)])  62.4 us
    pallas_call x2, Pallas kernels, direct(): pl.pallas_call(functools.partial(direct_kernel, chips, group, parts), in_...  18.8 us
    pallas_call x2, Pallas kernels, mirror(): pl.pallas_call(functools.partial(mirror_kernel, chips, group, parts), in_...  12.5 us
    pallas_call x2, Pallas kernels, cholesky(): pl.pallas_call(cholesky_kernel, out_shape=[shape(n, n)] * 2, compiler_par...  11.6 us
    pallas_call x1, Pallas kernels, load(): pl.pallas_call(load_kernel, in_specs=[ANY] * (1 + len(after)), out_specs=...  8.07 us
    pallas_call x2, Pallas kernels, own(): pl.pallas_call(functools.partial(own_kernel, group, parts), in_specs=[SME...  7.89 us
  transfers between devices with their start and end apart: 46, of which 29 were waited for; matrix products, arithmetic and copies ran while one was open for 2% of the time, Pallas kernels for 22%

profile of v6, /device:TPU:0, one launch (start us, length us, event | category | flops | bytes accessed | tf_op | source)
XLA Modules:
  0.0 269.9 jit_solution(11424193019927041059)
XLA Ops:
  21.0 8.1 %load.1 = (bf16[22,512,512]{2,1,0:T(8,128)(2,1)S(1)}, bf16[22,512,512]{2,1,0:T(8,128)(2,1)S(1)}) custom-call(f32[22,512,512]{2,1,0:T(8,128)} %tiles.1, f32[64,8192]{1,0:T(8,128)S(1)} %get-tuple-element.53.refs_0_, s32[24]{0:T(128)S(1)} %reshape.38.refs_1_.flag, s32[24]{0:T(128)S(1)} %max.9.wanted.refs_2_, s32[24]{0:T(128)S(1)} %get-tuple-element.109.refs_3_.tile_ref, ...), custom_call_target="tpu_custom_call" | custom-call | tf_op jit(solution)/shard_map/load/pallas_call | solution.py:65
  29.1 6.4 %mirror.2 = (f32[64,3072]{1,0:T(8,128)S(1)}, f32[64,3072]{1,0:T(8,128)S(1)}, f32[64,3072]{1,0:T(8,128)S(1)}) custom-call(s32[3]{0:T(128)S(1)} %pad_add_fusion.1.place, s32[24]{0:T(128)S(1)} %get-tuple-element.109.refs_3_.tile_ref, s32[24]{0:T(128)S(1)} %compare_convert_fusion.refs_4_.valid_ref, s32[24]{0:T(128)S(1)} %get-tuple-element.108.refs_5_.row_ref, ...), custom_call_target="tpu_custom_call" | custom-call | tf_op jit(solution)/shard_map/mirror/pallas_call | solution.py:161
  39.0 4.0 %own.2.refs_3_ = f32[64,8192]{1,0:T(8,128)S(1)} custom-call(s32[3]{0:T(128)S(1)} %pad_add_fusion.1.place, s32[24]{0:T(128)S(1)} %get-tuple-element.109.refs_3_.tile_ref, s32[24]{0:T(128)S(1)} %compare_convert_fusion.refs_4_.valid_ref, s32[24]{0:T(128)S(1)} %get-tuple-element.108.refs_5_.row_ref, s32[24]{0:T(128)S(1)} %add_maximum_fusion.1.refs_6_.col_ref, ...), custom_call_target="tpu_custom_call" | custom-call | tf_op jit(solution)/shard_map/own/pallas_call | solution.py:189
  43.0 28.0 %collective-permute-done.5.refs_1_ = f32[64,3072]{1,0:T(8,128)S(1)} collective-permute-done((f32[64,3072]{1,0:T(8,128)}, f32[64,3072]{1,0:T(8,128)S(1)}, u32[]{:S(2)}, u32[]{:S(2)}) %collective-permute-start.5) | collective-permute-done | bytes 786464 | tf_op jit(solution)/shard_map/ppermute | solution.py:429
  71.0 9.4 %direct.2.start = f32[64,8192]{1,0:T(8,128)S(1)} custom-call(s32[3]{0:T(128)S(1)} %pad_add_fusion.1.place, s32[24]{0:T(128)S(1)} %get-tuple-element.109.refs_3_.tile_ref, s32[24]{0:T(128)S(1)} %compare_convert_fusion.refs_4_.valid_ref, s32[24]{0:T(128)S(1)} %get-tuple-element.108.refs_5_.row_ref, bf16[22,512,512]{2,1,0:T(8,128)(2,1)S(1)} %get-tuple-element.54.high, ...), custom_call_target="tpu_custom_call" | custom-call | tf_op jit(solution)/shard_map/direct/pallas_call | solution.py:223
  80.4 6.4 %collective-permute-done.8.refs_1_ = f32[64,3072]{1,0:T(8,128)S(1)} collective-permute-done((f32[64,3072]{1,0:T(8,128)S(1)}, f32[64,3072]{1,0:T(8,128)S(1)}, u32[]{:S(2)}, u32[]{:S(2)}) %collective-permute-start.8) | collective-permute-done | bytes 786464 | tf_op jit(solution)/shard_map/ppermute | solution.py:429
  93.1 6.8 %collective-permute-done.13.arrived = f32[32,2048]{1,0:T(8,128)S(1)} collective-permute-done((f32[32,2048]{1,0:T(8,128)S(1)}, f32[32,2048]{1,0:T(8,128)S(1)}, u32[]{:S(2)}, u32[]{:S(2)}) %collective-permute-start.13) | collective-permute-done | bytes 262176 | tf_op jit(solution)/shard_map/ppermute | solution.py:429
  100.0 3.7 %collective-permute-start.14 = (f32[32,1024]{1,0:T(8,128)S(1)}, f32[32,1024]{1,0:T(8,128)S(1)}, u32[]{:S(2)}, u32[]{:S(2)}) collective-permute-start(f32[32,1024]{1,0:T(8,128)S(1)} %get-tuple-element.71), channel_id=1, source_target_pairs={{0,3},{1,2},{2,1},{3,0},{4,7},{5,6},{6,5},{7,4},{8,11},{9,10},{10,... | collective-permute-start | bytes 393224 | tf_op jit(solution)/shard_map/ppermute | solution.py:429
  106.9 3.7 %collective-permute-start.15 = (f32[32,1024]{1,0:T(8,128)S(1)}, f32[32,1024]{1,0:T(8,128)S(1)}, u32[]{:S(2)}, u32[]{:S(2)}) collective-permute-start(f32[32,1024]{1,0:T(8,128)S(1)} %total.4.refs_0_.mine), channel_id=1, source_target_pairs={{0,3},{1,2},{2,1},{3,0},{4,7},{5,6},{6,5},{7,4},{8,11},{9,10},{10,... | collective-permute-start | bytes 393224 | tf_op jit(solution)/shard_map/ppermute | solution.py:429
  111.0 4.0 %collective-permute-done.15.refs_0_.refs_1_.across = f32[32,1024]{1,0:T(8,128)S(1)} collective-permute-done((f32[32,1024]{1,0:T(8,128)S(1)}, f32[32,1024]{1,0:T(8,128)S(1)}, u32[]{:S(2)}, u32[]{:S(2)}) %collective-permute-start.15) | collective-permute-done | bytes 131104 | tf_op jit(solution)/shard_map/ppermute | solution.py:429
  115.9 4.4 %collective-permute-done.11.arrived = f32[32,2048]{1,0:T(8,128)S(1)} collective-permute-done((f32[32,2048]{1,0:T(8,128)S(1)}, f32[32,2048]{1,0:T(8,128)S(1)}, u32[]{:S(2)}, u32[]{:S(2)}) %collective-permute-start.11) | collective-permute-done | bytes 262176 | tf_op jit(solution)/shard_map/ppermute | solution.py:429
  139.8 6.1 %collective-permute-done.19.refs_2_.nearby = f32[32,2176]{1,0:T(8,128)S(1)} collective-permute-done((f32[32,2176]{1,0:T(8,128)S(1)}, f32[32,2176]{1,0:T(8,128)S(1)}, u32[]{:S(2)}, u32[]{:S(2)}) %collective-permute-start.19) | collective-permute-done | bytes 278560 | tf_op jit(solution)/shard_map/ppermute | solution.py:429
  145.9 4.4 %collective-permute-done.21.refs_2_.refs_1_ = f32[32,3072]{1,0:T(8,128)S(1)} collective-permute-done((f32[32,3072]{1,0:T(8,128)S(1)}, f32[32,3072]{1,0:T(8,128)S(1)}, u32[]{:S(2)}, u32[]{:S(2)}) %collective-permute-start.21) | collective-permute-done | bytes 393248 | tf_op jit(solution)/shard_map/ppermute | solution.py:429
  158.4 6.2 %mirror.3 = (f32[64,3072]{1,0:T(8,128)S(1)}, f32[64,3072]{1,0:T(8,128)S(1)}, f32[64,3072]{1,0:T(8,128)S(1)}) custom-call(s32[3]{0:T(128)S(1)} %pad_add_fusion.1.place, s32[24]{0:T(128)S(1)} %get-tuple-element.109.refs_3_.tile_ref, s32[24]{0:T(128)S(1)} %compare_convert_fusion.refs_4_.valid_ref, s32[24]{0:T(128)S(1)} %get-tuple-element.108.refs_5_.row_ref, ...), custom_call_target="tpu_custom_call" | custom-call | tf_op jit(solution)/shard_map/mirror/pallas_call | solution.py:161
  167.3 9.3 %collective-permute-done.25.refs_4_ = f32[32,3200]{1,0:T(8,128)S(1)} collective-permute-done((f32[32,3200]{1,0:T(8,128)S(1)}, f32[32,3200]{1,0:T(8,128)S(1)}, u32[]{:S(2)}, u32[]{:S(2)}) %collective-permute-start.25) | collective-permute-done | bytes 409632 | tf_op jit(solution)/shard_map/ppermute | solution.py:429
  180.0 3.9 %own.3.refs_6_ = f32[64,8192]{1,0:T(8,128)S(1)} custom-call(s32[3]{0:T(128)S(1)} %pad_add_fusion.1.place, s32[24]{0:T(128)S(1)} %get-tuple-element.109.refs_3_.tile_ref, s32[24]{0:T(128)S(1)} %compare_convert_fusion.refs_4_.valid_ref, s32[24]{0:T(128)S(1)} %get-tuple-element.108.refs_5_.row_ref, s32[24]{0:T(128)S(1)} %add_maximum_fusion.1.refs_6_.col_ref, ...), custom_call_target="tpu_custom_call" | custom-call | tf_op jit(solution)/shard_map/own/pallas_call | solution.py:189
  184.0 13.1 %collective-permute-done.27.refs_7_.refs_0_ = f32[64,3072]{1,0:T(8,128)S(1)} collective-permute-done((f32[64,3072]{1,0:T(8,128)S(1)}, f32[64,3072]{1,0:T(8,128)S(1)}, u32[]{:S(2)}, u32[]{:S(2)}) %collective-permute-start.27) | collective-permute-done | bytes 786464 | tf_op jit(solution)/shard_map/ppermute | solution.py:429
  197.0 9.4 %direct.3.start = f32[64,8192]{1,0:T(8,128)S(1)} custom-call(s32[3]{0:T(128)S(1)} %pad_add_fusion.1.place, s32[24]{0:T(128)S(1)} %get-tuple-element.109.refs_3_.tile_ref, s32[24]{0:T(128)S(1)} %compare_convert_fusion.refs_4_.valid_ref, s32[24]{0:T(128)S(1)} %get-tuple-element.108.refs_5_.row_ref, bf16[22,512,512]{2,1,0:T(8,128)(2,1)S(1)} %get-tuple-element.54.high, ...), custom_call_target="tpu_custom_call" | custom-call | tf_op jit(solution)/shard_map/direct/pallas_call | solution.py:223
  206.4 5.5 %collective-permute-done.29.refs_2_ = f32[64,3072]{1,0:T(8,128)S(1)} collective-permute-done((f32[64,3072]{1,0:T(8,128)S(1)}, f32[64,3072]{1,0:T(8,128)S(1)}, u32[]{:S(2)}, u32[]{:S(2)}) %collective-permute-start.29) | collective-permute-done | bytes 786464 | tf_op jit(solution)/shard_map/ppermute | solution.py:429
  220.2 6.1 %cholesky.2 = (f32[64,64]{1,0:T(8,128)}, f32[64,64]{1,0:T(8,128)S(1)}) custom-call(f32[64,64]{1,0:T(8,128)S(1)} %pad_maximum_fusion.gram), custom_call_target="tpu_custom_call" | custom-call | tf_op jit(solution)/shard_map/cholesky/pallas_call | solution.py:392
  229.1 3.3 %collective-permute-done.33.arrived = f32[32,2048]{1,0:T(8,128)S(1)} collective-permute-done((f32[32,2048]{1,0:T(8,128)S(1)}, f32[32,2048]{1,0:T(8,128)S(1)}, u32[]{:S(2)}, u32[]{:S(2)}) %collective-permute-start.33) | collective-permute-done | bytes 262176 | tf_op jit(solution)/shard_map/ppermute | solution.py:429
  235.5 3.9 %collective-permute-done.34.arrived = f32[32,1024]{1,0:T(8,128)S(1)} collective-permute-done((f32[32,1024]{1,0:T(8,128)S(1)}, f32[32,1024]{1,0:T(8,128)S(1)}, u32[]{:S(2)}, u32[]{:S(2)}) %collective-permute-start.34) | collective-permute-done | bytes 131104 | tf_op jit(solution)/shard_map/ppermute | solution.py:429
  253.2 3.8 %collective-permute-start.43 = (f32[32,2048]{1,0:T(8,128)S(1)}, f32[32,2048]{1,0:T(8,128)S(1)}, u32[]{:S(2)}, u32[]{:S(2)}) collective-permute-start(f32[32,2048]{1,0:T(8,128)S(1)} %pack.10), channel_id=1, source_target_pairs={{0,1},{1,0},{2,3},{3,2},{4,5},{5,4},{6,7},{7,6},{8,9},{9,8},{10,11... | collective-permute-start | bytes 786440 | tf_op jit(solution)/shard_map/ppermute | solution.py:429
  258.9 5.5 %cholesky.3 = (f32[64,64]{1,0:T(8,128)S(1)}, f32[64,64]{1,0:T(8,128)S(1)}) custom-call(f32[64,64]{1,0:T(8,128)S(1)} %add_add_fusion.gram), custom_call_target="tpu_custom_call" | custom-call | tf_op jit(solution)/shard_map/cholesky/pallas_call | solution.py:392
  (141 shorter events, 103.8 us)
Async XLA Ops:
  0.6 12.1 %collective-permute-start.3 = (f32[64,4096]{1,0:T(8,128)}, f32[64,4096]{1,0:T(8,128)S(1)}, u32[]{:S(2)}, u32[]{:S(2)}) collective-permute-start(f32[64,4096]{1,0:T(8,128)} %bitcast.23), channel_id=1, source_target_pairs={{0,4},{4,0},{8,12},{12,8},{16,20},{20,16},{24,28},{28,24},{1,5},{5... | collective-permute-start | bytes 3145736 | tf_op jit(solution)/shard_map/ppermute | solution.py:429
  17.4 20.7 %collective-permute-start.4 = (f32[64,3072]{1,0:T(8,128)}, f32[64,3072]{1,0:T(8,128)S(1)}, u32[]{:S(2)}, u32[]{:S(2)}) collective-permute-start(f32[64,3072]{1,0:T(8,128)} %get-tuple-element.56), channel_id=1, source_target_pairs={{0,8},{4,12},{8,0},{12,4},{16,24},{20,28},{24,16},{28,20},{1,9},{5... | collective-permute-start | bytes 2359304 | tf_op jit(solution)/shard_map/ppermute | solution.py:429
  18.1 53.0 %collective-permute-start.5 = (f32[64,3072]{1,0:T(8,128)}, f32[64,3072]{1,0:T(8,128)S(1)}, u32[]{:S(2)}, u32[]{:S(2)}) collective-permute-start(f32[64,3072]{1,0:T(8,128)} %copy-done.2), channel_id=1, source_target_pairs={{0,16},{4,20},{8,24},{12,28},{16,0},{20,4},{24,8},{28,12},{1,17},{... | collective-permute-start | bytes 2359304 | tf_op jit(solution)/shard_map/ppermute | solution.py:429
  18.1 52.9 %collective-permute-start.6 = (f32[64,3072]{1,0:T(8,128)}, f32[64,3072]{1,0:T(8,128)S(1)}, u32[]{:S(2)}, u32[]{:S(2)}) collective-permute-start(f32[64,3072]{1,0:T(8,128)} %copy-done.1), channel_id=1, source_target_pairs={{0,24},{4,28},{8,16},{12,20},{16,8},{20,12},{24,0},{28,4},{1,25},{... | collective-permute-start | bytes 2359304 | tf_op jit(solution)/shard_map/ppermute | solution.py:429
  35.5 51.3 %collective-permute-start.8 = (f32[64,3072]{1,0:T(8,128)S(1)}, f32[64,3072]{1,0:T(8,128)S(1)}, u32[]{:S(2)}, u32[]{:S(2)}) collective-permute-start(f32[64,3072]{1,0:T(8,128)S(1)} %get-tuple-element.60), channel_id=1, source_target_pairs={{0,16},{4,20},{8,24},{12,28},{16,0},{20,4},{24,8},{28,12},{1,17},{... | collective-permute-start | bytes 2359304 | tf_op jit(solution)/shard_map/ppermute | solution.py:429
  36.1 50.7 %collective-permute-start.9 = (f32[64,3072]{1,0:T(8,128)S(1)}, f32[64,3072]{1,0:T(8,128)S(1)}, u32[]{:S(2)}, u32[]{:S(2)}) collective-permute-start(f32[64,3072]{1,0:T(8,128)S(1)} %get-tuple-element.61), channel_id=1, source_target_pairs={{0,24},{4,28},{8,16},{12,20},{16,8},{20,12},{24,0},{28,4},{1,25},{... | collective-permute-start | bytes 2359304 | tf_op jit(solution)/shard_map/ppermute | solution.py:429
  38.1 48.7 %collective-permute-start.7 = (f32[64,3072]{1,0:T(8,128)S(1)}, f32[64,3072]{1,0:T(8,128)S(1)}, u32[]{:S(2)}, u32[]{:S(2)}) collective-permute-start(f32[64,3072]{1,0:T(8,128)S(1)} %get-tuple-element.59.refs_1_), channel_id=1, source_target_pairs={{0,8},{4,12},{8,0},{12,4},{16,24},{20,28},{24,16},{28,20},{1,9},{5... | collective-permute-start | bytes 2359304 | tf_op jit(solution)/shard_map/ppermute | solution.py:429
  110.5 9.7 %collective-permute-start.11 = (f32[32,2048]{1,0:T(8,128)S(1)}, f32[32,2048]{1,0:T(8,128)S(1)}, u32[]{:S(2)}, u32[]{:S(2)}) collective-permute-start(f32[32,2048]{1,0:T(8,128)S(1)} %get-tuple-element.65), channel_id=1, source_target_pairs={{0,1},{1,0},{2,3},{3,2},{4,5},{5,4},{6,7},{7,6},{8,9},{9,8},{10,11... | collective-permute-start | bytes 786440 | tf_op jit(solution)/shard_map/ppermute | solution.py:429
  115.1 10.0 %collective-permute-start.16 = (f32[32,2048]{1,0:T(8,128)S(1)}, f32[32,2048]{1,0:T(8,128)S(1)}, u32[]{:S(2)}, u32[]{:S(2)}) collective-permute-start(f32[32,2048]{1,0:T(8,128)S(1)} %pack.6), channel_id=1, source_target_pairs={{0,1},{1,0},{2,3},{3,2},{4,5},{5,4},{6,7},{7,6},{8,9},{9,8},{10,11... | collective-permute-start | bytes 786440 | tf_op jit(solution)/shard_map/ppermute | solution.py:429
  131.8 18.6 %collective-permute-start.21 = (f32[32,3072]{1,0:T(8,128)S(1)}, f32[32,3072]{1,0:T(8,128)S(1)}, u32[]{:S(2)}, u32[]{:S(2)}) collective-permute-start(f32[32,3072]{1,0:T(8,128)S(1)} %get-tuple-element.74), channel_id=1, source_target_pairs={{0,16},{4,20},{8,24},{12,28},{16,0},{20,4},{24,8},{28,12},{1,17},{... | collective-permute-start | bytes 1179656 | tf_op jit(solution)/shard_map/ppermute | solution.py:429
  132.2 18.1 %collective-permute-start.22 = (f32[32,3072]{1,0:T(8,128)S(1)}, f32[32,3072]{1,0:T(8,128)S(1)}, u32[]{:S(2)}, u32[]{:S(2)}) collective-permute-start(f32[32,3072]{1,0:T(8,128)S(1)} %get-tuple-element.75), channel_id=1, source_target_pairs={{0,24},{4,28},{8,16},{12,20},{16,8},{20,12},{24,0},{28,4},{1,25},{... | collective-permute-start | bytes 1179656 | tf_op jit(solution)/shard_map/ppermute | solution.py:429
  134.7 16.9 %collective-permute-start.20 = (f32[32,3072]{1,0:T(8,128)S(1)}, f32[32,3072]{1,0:T(8,128)S(1)}, u32[]{:S(2)}, u32[]{:S(2)}) collective-permute-start(f32[32,3072]{1,0:T(8,128)S(1)} %get-tuple-element.72), channel_id=1, source_target_pairs={{0,8},{4,12},{8,0},{12,4},{16,24},{20,28},{24,16},{28,20},{1,9},{5... | collective-permute-start | bytes 1179656 | tf_op jit(solution)/shard_map/ppermute | solution.py:429
  154.9 12.4 %collective-permute-start.24 = (f32[32,3200]{1,0:T(8,128)S(1)}, f32[32,3200]{1,0:T(8,128)S(1)}, u32[]{:S(2)}, u32[]{:S(2)}) collective-permute-start(f32[32,3200]{1,0:T(8,128)S(1)} %get-tuple-element.77), channel_id=1, source_target_pairs={{0,8},{4,12},{8,0},{12,4},{16,24},{20,28},{24,16},{28,20},{1,9},{5... | collective-permute-start | bytes 1228808 | tf_op jit(solution)/shard_map/ppermute | solution.py:429
  156.5 20.0 %collective-permute-start.25 = (f32[32,3200]{1,0:T(8,128)S(1)}, f32[32,3200]{1,0:T(8,128)S(1)}, u32[]{:S(2)}, u32[]{:S(2)}) collective-permute-start(f32[32,3200]{1,0:T(8,128)S(1)} %get-tuple-element.78), channel_id=1, source_target_pairs={{0,16},{4,20},{8,24},{12,28},{16,0},{20,4},{24,8},{28,12},{1,17},{... | collective-permute-start | bytes 1228808 | tf_op jit(solution)/shard_map/ppermute | solution.py:429
  157.0 19.6 %collective-permute-start.26 = (f32[32,3200]{1,0:T(8,128)S(1)}, f32[32,3200]{1,0:T(8,128)S(1)}, u32[]{:S(2)}, u32[]{:S(2)}) collective-permute-start(f32[32,3200]{1,0:T(8,128)S(1)} %get-tuple-element.79), channel_id=1, source_target_pairs={{0,24},{4,28},{8,16},{12,20},{16,8},{20,12},{24,0},{28,4},{1,25},{... | collective-permute-start | bytes 1228808 | tf_op jit(solution)/shard_map/ppermute | solution.py:429
  176.5 20.5 %collective-permute-start.27 = (f32[64,3072]{1,0:T(8,128)S(1)}, f32[64,3072]{1,0:T(8,128)S(1)}, u32[]{:S(2)}, u32[]{:S(2)}) collective-permute-start(f32[64,3072]{1,0:T(8,128)S(1)} %get-tuple-element.83.refs_2_), channel_id=1, source_target_pairs={{0,8},{4,12},{8,0},{12,4},{16,24},{20,28},{24,16},{28,20},{1,9},{5... | collective-permute-start | bytes 2359304 | tf_op jit(solution)/shard_map/ppermute | solution.py:429
  177.0 34.9 %collective-permute-start.29 = (f32[64,3072]{1,0:T(8,128)S(1)}, f32[64,3072]{1,0:T(8,128)S(1)}, u32[]{:S(2)}, u32[]{:S(2)}) collective-permute-start(f32[64,3072]{1,0:T(8,128)S(1)} %get-tuple-element.87), channel_id=1, source_target_pairs={{0,24},{4,28},{8,16},{12,20},{16,8},{20,12},{24,0},{28,4},{1,25},{... | collective-permute-start | bytes 2359304 | tf_op jit(solution)/shard_map/ppermute | solution.py:429
  178.4 34.8 %collective-permute-start.28 = (f32[64,3072]{1,0:T(8,128)S(1)}, f32[64,3072]{1,0:T(8,128)S(1)}, u32[]{:S(2)}, u32[]{:S(2)}) collective-permute-start(f32[64,3072]{1,0:T(8,128)S(1)} %get-tuple-element.85), channel_id=1, source_target_pairs={{0,16},{4,20},{8,24},{12,28},{16,0},{20,4},{24,8},{28,12},{1,17},{... | collective-permute-start | bytes 2359304 | tf_op jit(solution)/shard_map/ppermute | solution.py:429
  218.0 9.2 %collective-permute-start.31 = (f32[32,2048]{1,0:T(8,128)S(1)}, f32[32,2048]{1,0:T(8,128)S(1)}, u32[]{:S(2)}, u32[]{:S(2)}) collective-permute-start(f32[32,2048]{1,0:T(8,128)S(1)} %get-tuple-element.93), channel_id=1, source_target_pairs={{0,1},{1,0},{2,3},{3,2},{4,5},{5,4},{6,7},{7,6},{8,9},{9,8},{10,11... | collective-permute-start | bytes 786440 | tf_op jit(solution)/shard_map/ppermute | solution.py:429
  218.1 14.3 %collective-permute-start.33 = (f32[32,2048]{1,0:T(8,128)S(1)}, f32[32,2048]{1,0:T(8,128)S(1)}, u32[]{:S(2)}, u32[]{:S(2)}) collective-permute-start(f32[32,2048]{1,0:T(8,128)S(1)} %get-tuple-element.97), channel_id=1, source_target_pairs={{0,1},{1,0},{2,3},{3,2},{4,5},{5,4},{6,7},{7,6},{8,9},{9,8},{10,11... | collective-permute-start | bytes 786440 | tf_op jit(solution)/shard_map/ppermute | solution.py:429
  246.0 10.9 %collective-permute-start.44 = (f32[32,1024]{1,0:T(8,128)S(1)}, f32[32,1024]{1,0:T(8,128)S(1)}, u32[]{:S(2)}, u32[]{:S(2)}) collective-permute-start(f32[32,1024]{1,0:T(8,128)S(1)} %total.7.refs_0_.mine), channel_id=1, source_target_pairs={{0,3},{1,2},{2,1},{3,0},{4,7},{5,6},{6,5},{7,4},{8,11},{9,10},{10,... | collective-permute-start | bytes 393224 | tf_op jit(solution)/shard_map/ppermute | solution.py:429
  249.7 9.2 %collective-permute-start.41 = (f32[64,64]{1,0:T(8,128)S(1)}, f32[64,64]{1,0:T(8,128)S(1)}, u32[]{:S(2)}, u32[]{:S(2)}) collective-permute-start(f32[64,64]{1,0:T(8,128)S(1)} %add.77), channel_id=1, source_target_pairs={{0,24},{4,28},{8,16},{12,20},{16,8},{20,12},{24,0},{28,4},{1,25},{... | collective-permute-start | bytes 49160 | tf_op jit(solution)/shard_map/ppermute | solution.py:429
  253.2 12.1 %collective-permute-start.43 = (f32[32,2048]{1,0:T(8,128)S(1)}, f32[32,2048]{1,0:T(8,128)S(1)}, u32[]{:S(2)}, u32[]{:S(2)}) collective-permute-start(f32[32,2048]{1,0:T(8,128)S(1)} %pack.10), channel_id=1, source_target_pairs={{0,1},{1,0},{2,3},{3,2},{4,5},{5,4},{6,7},{7,6},{8,9},{9,8},{10,11... | collective-permute-start | bytes 786440 | tf_op jit(solution)/shard_map/ppermute | solution.py:429
  257.0 10.4 %collective-permute-start.45 = (f32[32,2048]{1,0:T(8,128)S(1)}, f32[32,2048]{1,0:T(8,128)S(1)}, u32[]{:S(2)}, u32[]{:S(2)}) collective-permute-start(f32[32,2048]{1,0:T(8,128)S(1)} %pack.11), channel_id=1, source_target_pairs={{0,1},{1,0},{2,3},{3,2},{4,5},{5,4},{6,7},{7,6},{8,9},{9,8},{10,11... | collective-permute-start | bytes 786440 | tf_op jit(solution)/shard_map/ppermute | solution.py:429
  (25 other events, 130.6 us)
